TPU v7x, 256 devices: a whole 4x4x8 slice. The times are simulated.
256 devices in a mesh: tm: 8 (over x, y_lo), pts: 32 (over y_hi, z, core).
Axes of the slice: x: 4, y: 4 (y_hi: 2, y_lo: 2; y = y_hi * 2 + y_lo), z: 8, core: 2. Of those that a mesh axis runs over, the one named last changes fastest.
Arguments:
- orbitals: bfloat16 [32768, 2048], P('pts'), may hold values from -6 to 6
- panel_orbitals: bfloat16 [1024, 2048], P(('tm', 'pts')), may hold values from -0.1796875 to 0.1796875
- band_gap: float32 [2048], replicated, may hold values from 0.1 to 1
- tau_points: float32 [8], replicated, may hold values from 0.1 to 2
- quad_weight: float32 [8], replicated, may hold values from 0.1 to 1
- frequencies: float32 [8], replicated, may hold values from 0.1 to 3
- coulomb: bfloat16 [1024, 1024], P(('tm', 'pts')), may hold values from -0.1875 to 0.1875
Outputs:
- screened: bfloat16 [8, 32768, 1024], P(None, ('pts', 'tm'))
All inputs are finite; a program needn't handle non-finite values.
Results may differ from a plain program's by a relative error of at most 0.0056.
Values may be sent and summed in bfloat16 or wider, within the bound.
No kernel may reach another device: no remote copies, remote signals or barrier semaphores. Data moves between devices by JAX's collectives and lax.ppermute only.
A program may use at most 64 MiB of HBM per device.

v0:
```python
import jax
import jax.numpy as jnp
from jax import lax
from jax.sharding import PartitionSpec as P

NOCC = 512
PANEL = 1024
TAU_DEV = 1
FREQS = 8


def laid_out(pieces, dim):
    lengths = list(pieces.shape[1:])
    lengths[dim] *= pieces.shape[0]
    return jnp.moveaxis(pieces, 0, dim).reshape(lengths)


def sent_to_all(value, axis):
    copies = jnp.broadcast_to(value, (lax.axis_size(axis), *value.shape))
    return lax.all_to_all(copies, axis, split_axis=0, concat_axis=0, tiled=True)


def gather_directly(value, axis, dim):
    return laid_out(sent_to_all(value, axis), dim)


def in_blocks(value, dim, devices):
    before, after = (value.shape[:dim], value.shape[dim + 1 :])
    return jnp.moveaxis(value.reshape(*before, devices, -1, *after), dim, 0)


def cut_rows(length, count):
    lap = length // count
    if lap >= 8:
        lap -= lap % 8
    return [lap * k for k in range(1, count)]


def several_exchanges(value, axis, pieces, split_dim, concat_dim):
    blocks = in_blocks(value, split_dim, lax.axis_size(axis))
    cut = max(range(1, max(2, blocks.ndim - 1)), key=lambda d: blocks.shape[d])
    gathered = []
    for section in jnp.split(blocks, cut_rows(blocks.shape[cut], pieces), axis=cut):
        if section.size:
            gathered.append(lax.all_to_all(section, axis, split_axis=0, concat_axis=0, tiled=True))
    return laid_out(jnp.concatenate(gathered, axis=cut), concat_dim)


def contract(left, right):
    return lax.dot_general(
        left, right, (((1,), (1,)), ((), ())), preferred_element_type=jnp.float32
    )


def shards(orbitals, panel_orbitals, band_gap, tau_points, quad_weight, frequencies, coulomb):
    group = lax.axis_index("tm")
    own_taus = lax.dynamic_slice_in_dim(tau_points, group * TAU_DEV, TAU_DEV)
    decay = jnp.exp(-band_gap[None, :] * own_taus[:, None])
    occ_rows = orbitals[:, :NOCC]
    vir_rows = orbitals[:, NOCC:]
    grouped = gather_directly(panel_orbitals, "pts", 0)
    widened = lax.all_gather(grouped, "tm", axis=0, tiled=True).astype(jnp.float32)
    scaled = (widened * decay[0][None, :]).astype(jnp.bfloat16)
    green_occ = contract(occ_rows, scaled[:, :NOCC])
    green_vir = contract(vir_rows, scaled[:, NOCC:])
    layers = [(-(green_occ * green_vir)).astype(jnp.bfloat16)]
    polar = jnp.stack(layers)
    regrouped = several_exchanges(polar, "tm", 2, 1, 0)
    times_all = regrouped.shape[0]
    row_count = regrouped.shape[1]
    cosines = quad_weight[None, :] * jnp.cos(frequencies[:, None] * tau_points[None, :])
    flat = regrouped.reshape(times_all, row_count * PANEL).astype(jnp.float32)
    transformed = jnp.dot(cosines, flat, precision=lax.Precision.HIGHEST).astype(jnp.bfloat16)
    transformed = transformed.reshape(FREQS * row_count, PANEL)
    screened = jnp.dot(
        transformed,
        lax.all_gather(coulomb, ("tm", "pts"), axis=0, tiled=True),
        preferred_element_type=jnp.float32,
    )
    return screened.astype(jnp.bfloat16).reshape(FREQS, row_count, PANEL)


def solution(mesh):
    placed = (P("pts", None), P(("tm", "pts"), None), P(), P(), P(), P(), P(("tm", "pts"), None))
    return jax.shard_map(
        shards, mesh=mesh, in_specs=placed, out_specs=P(None, ("pts", "tm"), None), check_vma=False
    )
```

profile of v0, /device:TPU:1, one launch (start us, length us, event | category | flops | bytes accessed | tf_op | source)
XLA Modules:
  0.0 563.3 jit_solution(4525019650464051369)
XLA Ops:
  6.5 0.0 copy-start.2
  6.5 0.0 copy-start.1
  6.5 0.0 all-gather.4.cloned.1.call-start
  6.5 1.0 broadcast_in_dim.2
  7.5 30.6 %all_to_all.15 = bf16[32,4,2048]{2,1,0:T(4,128)(2,1)S(1)} all-to-all(bf16[32,4,2048]{2,1,0:T(4,128)(2,1)S(1)} %broadcast_in_dim.2), channel_id=1, replica_groups=mesh['tm'=8,'pts'=32] {'pts'}, dimensions={0} | all-to-all | bytes 1048576 | tf_op jit(solution)/shard_map/all_to_all | solution.py:20
  38.1 0.9 reshape.19
  39.1 0.0 all-gather.4.cloned.1.call-update
  39.1 0.0 all-gather.6.cloned.1.call-start
  39.1 0.7 all-gather.6.cloned.1.call-update
  39.8 0.0 copy-done.2
  39.9 0.7 dynamic_slice.3
  40.5 0.0 copy-done.1
  40.5 0.7 multiply_exponential_fusion
  41.2 86.1 %all-gather.4.cloned.1.call-done = bf16[1024,2048]{1,0:T(8,128)(2,1)} async-done(((bf16[128,2048]{1,0:T(8,128)(2,1)}), bf16[1024,2048]{1,0:T(8,128)(2,1)}) %all-gather.4.cloned.1.call-update) | async-done | bytes 4194320 | tf_op jit(solution)/shard_map/all_gather | solution.py:62
  127.3 0.0 copy-start
  127.3 3.4 multiply_convert_fusion
  130.8 0.0 copy-done
  130.8 3.5 fusion
  134.3 1.3 negate_convert_fusion
  135.6 1.2 fusion.11
  136.7 19.5 %all_to_all.16 = bf16[8,1,64,1024]{3,2,1,0:T(8,128)(2,1)S(1)} all-to-all(bf16[8,1,64,1024]{3,2,1,0:T(8,128)(2,1)S(1)} %get-tuple-element.5), channel_id=1, replica_groups=mesh['tm'=8,'pts'=32] {'tm'}, dimensions={0} | all-to-all | bytes 2097152 | tf_op jit(solution)/shard_map/all_to_all | solution.py:45
  156.3 3.7 all-to-all-start.2
  160.0 381.0 %all-gather.6.cloned.1.call-done = bf16[256,4,1024]{2,1,0:T(4,128)(2,1)} async-done(((bf16[1,4,1024]{2,1,0:T(4,128)(2,1)}), bf16[256,4,1024]{2,1,0:T(4,128)(2,1)}) %all-gather.6.cloned.1.call-update) | async-done | bytes 2097168 | tf_op jit(solution)/shard_map/all_gather | solution.py:77
  541.0 4.0 reshape.23
  545.0 0.0 all-to-all-done.2
  545.0 0.2 maximum_bitcast_fusion
  545.2 0.0 copy-start.3
  545.2 0.0 copy-start.4
  545.2 1.2 copy.10
  546.4 0.0 copy-done.3
  546.4 0.0 copy-done.4
  546.4 1.9 convolution_convert_fusion
  548.3 2.3 reshape.20
  550.6 5.9 %convolution_convert_fusion.1 = bf16[1024,1024]{1,0:T(8,128)(2,1)} fusion(bf16[1024,1024]{1,0:T(8,128)(2,1)} %reshape.20, bf16[1024,1024]{1,0:T(8,128)(2,1)} %reshape.23), kind=kOutput, calls=%fused_computation.7 | convolution fusion | flops 2148532224 | bytes 6291456 | tf_op jit(solution)/shard_map/dot_general | solution.py:75
Async XLA Ops:
  6.5 33.3 %copy-start.2 = (f32[8]{0:T(128)S(1)}, f32[8]{0:T(128)}, u32[]{:S(2)}) copy-start(f32[8]{0:T(128)} %param.10) | copy-start | bytes 100
  6.5 34.0 %copy-start.1 = (f32[2048]{0:T(1024)S(1)}, f32[2048]{0:T(1024)}, u32[]{:S(2)}) copy-start(f32[2048]{0:T(1024)} %param.9) | copy-start | bytes 24580
  6.5 120.8 %all-gather.4.cloned.1.call-start = ((), (), s32[]{:S(2)}) async-start(), calls=%async_computation.3 | async-start | bytes 4718592 | tf_op jit(solution)/shard_map/all_gather | solution.py:62
  39.1 501.9 %all-gather.6.cloned.1.call-start = ((), (), s32[]{:S(2)}) async-start(), calls=%async_computation.4 | async-start | bytes 2105344 | tf_op jit(solution)/shard_map/all_gather | solution.py:77
  127.3 3.5 copy-start
  156.3 388.7 %all-to-all-start.2 = ((bf16[8,1,64,1024]{3,2,1,0:T(8,128)(2,1)}), bf16[8,1,64,1024]{3,2,1,0:T(8,128)(2,1)S(1)}, u32[]{:S(2)}, u32[]{:S(2)}) async-start(bf16[8,1,64,1024]{3,2,1,0:T(8,128)(2,1)} %get-tuple-element.6), calls=%async_computation.2 | async-start | bytes 2097152 | tf_op jit(solution)/shard_map/all_to_all | solution.py:45
  545.2 1.2 copy-start.3
  545.2 1.2 copy-start.4
Sparse Core Ops, SparseCore 0:
  39.2 88.0 all-gather.3
  129.2 411.7 all-gather.5
where the time goes:
time: 567 us; the launch traced here: 563 us
  waiting for transfers between devices  468 us (83%)
  blocking collectives  50.2 us (9%)
  between operations  13.5 us (2%)
  matrix products  12.5 us (2%)
  local copies, waits for them, and re-layouts  11.1 us (2%)
    all_gather x1, waiting for transfers between devices, shards(): lax.all_gather(coulomb, ('tm', 'pts'), axis=0, tiled=True)  381 us
    all_gather x1, waiting for transfers between devices, shards(): lax.all_gather(grouped, 'tm', axis=0, tiled=True).astype(jnp.float32)  86.1 us
    all_to_all x1, blocking collectives, sent_to_all(): return lax.all_to_all(copies, axis, split_axis=0, concat_axis=0, tiled=True)  30.6 us
    all_to_all x1, blocking collectives, several_exchanges(): lax.all_to_all(section, axis, split_axis=0, concat_axis=0, tiled=True)  19.5 us
  transfers between devices with their start and end apart: 3, of which 2 were waited for; matrix products, arithmetic and copies ran while one was open for 3% of the time, Pallas kernels for 0%

commit v1 on v0

v1 whole, which is shorter than its diff:
```python
import jax
import jax.numpy as jnp
from jax import lax
from jax.experimental import pallas as pl
from jax.experimental.pallas import tpu as pltpu
from jax.sharding import Mesh
from jax.sharding import PartitionSpec as P

NOCC = 512
BANDS = 2048
PANEL = 1024
FREQS = 8
TAUS = 8
COLS = 256

TM = ("x", "ylo")
PTS = ("yhi", "z", "core")
SIZES = (4, 2, 2, 8, 2)
Y = ("ylo", "yhi")


def along(value, axis, partner):
    size = lax.axis_size(axis)
    return lax.ppermute(value, axis, [(k, partner(k, size)) for k in range(size)])


def shifted(step):
    return lambda k, size: (k + step) % size


def shifted_y(step):
    def partner(k, size):
        y = (2 * (k % 2) + k // 2 + step) % size
        return 2 * (y % 2) + y // 2

    return partner


def flipped(bit):
    return lambda k, size: k ^ bit


def contract(left, right):
    return lax.dot_general(
        left, right, (((1,), (1,)), ((), ())), preferred_element_type=jnp.float32
    )


def screen_kernel(cosines_ref, scaled_ref, *refs):
    pieces, out_ref, transformed_ref = refs[:-2], refs[-2], refs[-1]
    height = pieces[0].shape[0]
    rows = scaled_ref.shape[0] // TAUS
    group = COLS // height
    for chunk in range(PANEL // COLS):
        held = pieces[chunk * group : (chunk + 1) * group]
        occ = jnp.concatenate([p[:, :NOCC] for p in held], axis=0)
        vir = jnp.concatenate([p[:, NOCC:BANDS] for p in held], axis=0)
        polar = -(contract(scaled_ref[:, :NOCC], occ) * contract(scaled_ref[:, NOCC:], vir))
        for k in range(FREQS):
            total = cosines_ref[k, 0] * polar[:rows]
            for t in range(1, TAUS):
                total += cosines_ref[k, t] * polar[t * rows : (t + 1) * rows]
            transformed_ref[k * rows : (k + 1) * rows, chunk * COLS : (chunk + 1) * COLS] = (
                total.astype(jnp.bfloat16)
            )
    for chunk in range(PANEL // COLS):
        start = BANDS + chunk * COLS
        coulomb = jnp.concatenate([p[:, start : start + COLS] for p in pieces], axis=0)
        out_ref[:, chunk * COLS : (chunk + 1) * COLS] = jnp.dot(
            transformed_ref[...], coulomb, preferred_element_type=jnp.float32
        ).astype(jnp.bfloat16)


def screen(cosines, scaled, pieces):
    rows = scaled.shape[0]
    vmem = pl.BlockSpec(memory_space=pltpu.VMEM)
    return pl.pallas_call(
        screen_kernel,
        out_shape=jax.ShapeDtypeStruct((rows, PANEL), jnp.bfloat16),
        in_specs=[pl.BlockSpec(memory_space=pltpu.SMEM), vmem] + [vmem] * len(pieces),
        out_specs=vmem,
        scratch_shapes=[pltpu.VMEM((rows, PANEL), jnp.bfloat16)],
        compiler_params=pltpu.CompilerParams(vmem_limit_bytes=40 * 2**20),
        cost_estimate=pl.CostEstimate(
            flops=2 * rows * PANEL * (BANDS + PANEL), bytes_accessed=2**24, transcendentals=0
        ),
    )(cosines, scaled, *pieces)


def shards(orbitals, panel_orbitals, band_gap, tau_points, quad_weight, frequencies, coulomb):
    held = jnp.concatenate([panel_orbitals, coulomb], axis=1)
    for bit in (4, 2, 1):
        held = jnp.concatenate([held, along(held, "z", flipped(bit))], axis=0)
    half = held.shape[0] // 2
    first, second = held[:half], held[half:]
    first = jnp.concatenate([first] + [along(first, Y, shifted_y(s)) for s in (1, 3, 2)], axis=0)
    second = jnp.concatenate([second] + [along(second, "x", shifted(s)) for s in (1, 3, 2)], axis=0)
    pieces = [first, second]
    for s in (1, 3, 2):
        pieces.append(along(first, "x", shifted(s)))
        pieces.append(along(second, Y, shifted_y(s)))
    pieces += [along(p, "core", flipped(1)) for p in pieces]

    rows = orbitals.shape[0] // lax.axis_size(TM)
    own = lax.dynamic_slice_in_dim(orbitals, lax.axis_index(TM) * rows, rows).astype(jnp.float32)
    decay = jnp.exp(-band_gap[None, :] * tau_points[:, None])
    scaled = (own[None] * decay[:, None, :]).astype(jnp.bfloat16).reshape(TAUS * rows, BANDS)
    cosines = quad_weight[None, :] * jnp.cos(frequencies[:, None] * tau_points[None, :])
    return screen(cosines, scaled, pieces).reshape(FREQS, rows, PANEL)


def solution(mesh):
    split = Mesh(mesh.devices.reshape(SIZES), TM + PTS)
    everywhere = P(TM + PTS, None)
    placed = (P(PTS, None), everywhere, P(), P(), P(), P(), everywhere)
    return jax.shard_map(
        shards, mesh=split, in_specs=placed, out_specs=P(None, PTS + TM, None), check_vma=False
    )
```

time: 567 us -> 96.3 us (0.17)
  waiting for transfers between devices: 468 us -> 47.2 us
  blocking collectives: 50.2 us -> 0 us
  starting transfers between devices: 3.78 us -> 33.8 us
  between operations: 13.5 us -> 0.15 us
  matrix products: 12.5 us -> 0 us
  local copies, waits for them, and re-layouts: 11.1 us -> 1.54 us
  Pallas kernels: 0 us -> 9.52 us
    all_gather x2 -> x0, waiting for transfers between devices: 467 us -> none  [the longest x1 381 us: shards(): lax.all_gather(coulomb, ('tm', 'pts'), axis=0, tiled=True)]
    all_to_all x2 -> x0, blocking collectives: 50.2 us -> none  [the longest x1 30.6 us: sent_to_all(): return lax.all_to_all(copies, axis, split_axis=0, concat_axis=0, tiled=True)]
    ppermute x0 -> x23, waiting for transfers between devices: none -> 47.2 us  [along(): lax.ppermute(value, axis, [(k, partner(k, size)) for k in range(size)])]
    ppermute x0 -> x23, starting transfers between devices: none -> 33.8 us  [along(): lax.ppermute(value, axis, [(k, partner(k, size)) for k in range(size)])]
    dot_general x4 -> x0, matrix products: 12.5 us -> none  [the longest x1 5.87 us: shards(): jnp.dot(transformed, lax.all_gather(coulomb, ('tm', 'pts'), axis=0, tiled...]
    pallas_call x0 -> x1, Pallas kernels: none -> 9.52 us  [screen(): pl.pallas_call(screen_kernel, out_shape=jax.ShapeDtypeStruct((rows, PANEL...]
  transfers between devices with their start and end apart: 3 -> 23, of which waited for: 2 -> 11; matrix products, arithmetic and copies ran while one was open for 3% -> 4% of each run, Pallas kernels for 0% -> 0%
where the time goes in v1:
time: 96.3 us; the launch traced here: 96 us
  waiting for transfers between devices  47.2 us (49%)
  starting transfers between devices  33.8 us (35%)
  Pallas kernels  9.52 us (10%)
  other arithmetic  3.86 us (4%)
  local copies, waits for them, and re-layouts  1.54 us (2%)
    ppermute x23, waiting for transfers between devices, along(): lax.ppermute(value, axis, [(k, partner(k, size)) for k in range(size)])  47.2 us
    ppermute x23, starting transfers between devices, along(): lax.ppermute(value, axis, [(k, partner(k, size)) for k in range(size)])  33.8 us
    pallas_call x1, Pallas kernels, screen(): pl.pallas_call(screen_kernel, out_shape=jax.ShapeDtypeStruct((rows, PANEL...  9.52 us
  transfers between devices with their start and end apart: 23, of which 11 were waited for; matrix products, arithmetic and copies ran while one was open for 4% of the time, Pallas kernels for 0%

profile of v1, /device:TPU:1, one launch (start us, length us, event | category | flops | bytes accessed | tf_op | source)
XLA Modules:
  0.0 96.0 jit_solution(24964901806659732)
XLA Ops:
  0.0 0.7 constant_dynamic-update-slice_fusion.1
  0.7 0.7 constant_dynamic-update-slice_fusion
  1.4 7.7 %collective-permute-start = (bf16[4,3072]{1,0:T(4,128)(2,1)S(1)}, bf16[4,3072]{1,0:T(4,128)(2,1)S(1)}, u32[]{:S(2)}, u32[]{:S(2)}) collective-permute-start(bf16[4,3072]{1,0:T(4,128)(2,1)S(1)} %constant_dynamic-update-slice_fusion), channel_id=1, source_target_pairs={{0,8},{2,10},{4,12},{6,14},{8,0},{10,2},{12,4},{14,6},{1,9},{3,11}... | collective-permute-start | bytes 73736 | tf_op jit(solution)/shard_map/ppermute | solution.py:24
  9.2 1.2 %collective-permute-done = bf16[4,3072]{1,0:T(4,128)(2,1)S(1)} collective-permute-done((bf16[4,3072]{1,0:T(4,128)(2,1)S(1)}, bf16[4,3072]{1,0:T(4,128)(2,1)S(1)}, u32[]{:S(2)}, u32[]{:S(2)}) %collective-permute-start) | collective-permute-done | bytes 24608 | tf_op jit(solution)/shard_map/ppermute | solution.py:24
  10.4 1.5 %collective-permute-start.1 = (bf16[8,3072]{1,0:T(8,128)(2,1)S(1)}, bf16[8,3072]{1,0:T(8,128)(2,1)S(1)}, u32[]{:S(2)}, u32[]{:S(2)}) collective-permute-start(bf16[8,3072]{1,0:T(8,128)(2,1)S(1)} %pad_maximum_fusion.1), channel_id=1, source_target_pairs={{0,4},{2,6},{4,0},{6,2},{8,12},{10,14},{12,8},{14,10},{1,5},{3,7},... | collective-permute-start | bytes 147464 | tf_op jit(solution)/shard_map/ppermute | solution.py:24
  12.0 2.4 %collective-permute-done.1 = bf16[8,3072]{1,0:T(8,128)(2,1)S(1)} collective-permute-done((bf16[8,3072]{1,0:T(8,128)(2,1)S(1)}, bf16[8,3072]{1,0:T(8,128)(2,1)S(1)}, u32[]{:S(2)}, u32[]{:S(2)}) %collective-permute-start.1) | collective-permute-done | bytes 49184 | tf_op jit(solution)/shard_map/ppermute | solution.py:24
  14.4 0.0 copy-start
  14.4 0.0 copy-start.1
  14.4 0.0 copy-start.2
  14.4 0.9 collective-permute-start.5
  15.3 2.9 %collective-permute-start.4 = (bf16[16,3072]{1,0:T(8,128)(2,1)S(1)}, bf16[16,3072]{1,0:T(8,128)(2,1)S(1)}, u32[]{:S(2)}, u32[]{:S(2)}) collective-permute-start(bf16[16,3072]{1,0:T(8,128)(2,1)S(1)} %pad_maximum_fusion), channel_id=1, source_target_pairs={{0,16},{16,0},{32,48},{48,32},{1,17},{17,1},{33,49},{49,33},{2,18}... | collective-permute-start | bytes 294920 | tf_op jit(solution)/shard_map/ppermute | solution.py:24
  18.2 0.8 collective-permute-start.3
  19.0 0.7 collective-permute-start.2
  19.7 1.1 %dynamic-slice_convert_fusion = f32[128,2048]{1,0:T(8,128)S(1)} fusion(bf16[1024,2048]{1,0:T(8,128)(2,1)} %param.7, s32[]{:T(128)S(6)} %select_n.3), kind=kLoop, calls=%fused_computation.1 | loop fusion | flops 262144 | bytes 1572868 | tf_op jit(solution)/shard_map/convert_element_type | solution.py:105
  20.9 0.7 neg.4
  21.6 0.0 collective-permute-done.4
  21.6 0.5 collective-permute-done.3
  22.0 2.7 %collective-permute-done.2 = bf16[16,3072]{1,0:T(8,128)(2,1)S(1)} collective-permute-done((bf16[16,3072]{1,0:T(8,128)(2,1)S(1)}, bf16[16,3072]{1,0:T(8,128)(2,1)S(1)}, u32[]{:S(2)}, u32[]{:S(2)}) %collective-permute-start.2) | collective-permute-done | bytes 98336 | tf_op jit(solution)/shard_map/ppermute | solution.py:24
  24.8 0.1 concatenate.20.refs_0_
  24.8 3.7 %collective-permute-start.15 = (bf16[64,3072]{1,0:T(8,128)(2,1)S(1)}, bf16[64,3072]{1,0:T(8,128)(2,1)S(1)}, u32[]{:S(2)}, u32[]{:S(2)}) collective-permute-start(bf16[64,3072]{1,0:T(8,128)(2,1)S(1)} %concatenate.20.refs_0_), channel_id=1, source_target_pairs={{0,1},{1,0},{2,3},{3,2},{4,5},{5,4},{6,7},{7,6},{8,9},{9,8},{10,11... | collective-permute-start | bytes 1179656 | tf_op jit(solution)/shard_map/ppermute | solution.py:24
  28.5 2.8 %collective-permute-start.13 = (bf16[64,3072]{1,0:T(8,128)(2,1)S(1)}, bf16[64,3072]{1,0:T(8,128)(2,1)S(1)}, u32[]{:S(2)}, u32[]{:S(2)}) collective-permute-start(bf16[64,3072]{1,0:T(8,128)(2,1)S(1)} %concatenate.20.refs_0_), channel_id=1, source_target_pairs={{0,128},{64,192},{128,0},{192,64},{1,129},{65,193},{129,1},{193,65... | collective-permute-start | bytes 1179656 | tf_op jit(solution)/shard_map/ppermute | solution.py:24
  31.3 0.9 collective-permute-start.11
  32.2 0.6 collective-permute-start.9
  32.8 0.0 collective-permute-done.5
  32.8 0.3 collective-permute-start.6
  33.1 18.5 %collective-permute-done.6 = bf16[16,3072]{1,0:T(8,128)(2,1)S(1)} collective-permute-done((bf16[16,3072]{1,0:T(8,128)(2,1)S(1)}, bf16[16,3072]{1,0:T(8,128)(2,1)S(1)}, u32[]{:S(2)}, u32[]{:S(2)}) %collective-permute-start.6) | collective-permute-done | bytes 98336 | tf_op jit(solution)/shard_map/ppermute | solution.py:24
  51.6 0.0 collective-permute-start.7
  51.6 3.9 %collective-permute-done.7 = bf16[16,3072]{1,0:T(8,128)(2,1)S(1)} collective-permute-done((bf16[16,3072]{1,0:T(8,128)(2,1)S(1)}, bf16[16,3072]{1,0:T(8,128)(2,1)S(1)}, u32[]{:S(2)}, u32[]{:S(2)}) %collective-permute-start.7) | collective-permute-done | bytes 98336 | tf_op jit(solution)/shard_map/ppermute | solution.py:24
  55.5 2.7 %collective-permute-start.8 = (bf16[16,3072]{1,0:T(8,128)(2,1)S(1)}, bf16[16,3072]{1,0:T(8,128)(2,1)S(1)}, u32[]{:S(2)}, u32[]{:S(2)}) collective-permute-start(bf16[16,3072]{1,0:T(8,128)(2,1)S(1)} %collective-permute-done.5), channel_id=1, source_target_pairs={{0,128},{64,192},{128,0},{192,64},{1,129},{65,193},{129,1},{193,65... | collective-permute-start | bytes 294920 | tf_op jit(solution)/shard_map/ppermute | solution.py:24
  58.3 2.2 %collective-permute-done.8 = bf16[16,3072]{1,0:T(8,128)(2,1)S(1)} collective-permute-done((bf16[16,3072]{1,0:T(8,128)(2,1)S(1)}, bf16[16,3072]{1,0:T(8,128)(2,1)S(1)}, u32[]{:S(2)}, u32[]{:S(2)}) %collective-permute-start.8) | collective-permute-done | bytes 98336 | tf_op jit(solution)/shard_map/ppermute | solution.py:24
  60.5 2.6 %collective-permute-start.16 = (bf16[64,3072]{1,0:T(8,128)(2,1)S(1)}, bf16[64,3072]{1,0:T(8,128)(2,1)S(1)}, u32[]{:S(2)}, u32[]{:S(2)}) collective-permute-start(bf16[64,3072]{1,0:T(8,128)(2,1)S(1)} %constant_dynamic-update-slice_fusion.2.refs_1_), channel_id=1, source_target_pairs={{0,1},{1,0},{2,3},{3,2},{4,5},{5,4},{6,7},{7,6},{8,9},{9,8},{10,11... | collective-permute-start | bytes 1179656 | tf_op jit(solution)/shard_map/ppermute | solution.py:24
  63.1 0.2 collective-permute-start.14
  63.3 1.7 %collective-permute-start.12 = (bf16[64,3072]{1,0:T(8,128)(2,1)S(1)}, bf16[64,3072]{1,0:T(8,128)(2,1)S(1)}, u32[]{:S(2)}, u32[]{:S(2)}) collective-permute-start(bf16[64,3072]{1,0:T(8,128)(2,1)S(1)} %constant_dynamic-update-slice_fusion.2.refs_1_), channel_id=1, source_target_pairs={{0,48},{16,32},{32,0},{48,16},{1,49},{17,33},{33,1},{49,17},{2,50}... | collective-permute-start | bytes 1179656 | tf_op jit(solution)/shard_map/ppermute | solution.py:24
  65.0 0.7 collective-permute-start.21
  65.7 0.7 multiply_exponential_fusion
  66.5 0.3 collective-permute-start.19
  66.7 8.5 %collective-permute-done.14.refs_7_ = bf16[64,3072]{1,0:T(8,128)(2,1)S(1)} collective-permute-done((bf16[64,3072]{1,0:T(8,128)(2,1)S(1)}, bf16[64,3072]{1,0:T(8,128)(2,1)S(1)}, u32[]{:S(2)}, u32[]{:S(2)}) %collective-permute-start.14) | collective-permute-done | bytes 393248 | tf_op jit(solution)/shard_map/ppermute | solution.py:24
  75.3 1.3 %collective-permute-start.17 = (bf16[64,3072]{1,0:T(8,128)(2,1)S(1)}, bf16[64,3072]{1,0:T(8,128)(2,1)S(1)}, u32[]{:S(2)}, u32[]{:S(2)}) collective-permute-start(bf16[64,3072]{1,0:T(8,128)(2,1)S(1)} %collective-permute-done.9.refs_2_), channel_id=1, source_target_pairs={{0,1},{1,0},{2,3},{3,2},{4,5},{5,4},{6,7},{7,6},{8,9},{9,8},{10,11... | collective-permute-start | bytes 1179656 | tf_op jit(solution)/shard_map/ppermute | solution.py:24
  76.6 4.5 %collective-permute-done.12.refs_5_ = bf16[64,3072]{1,0:T(8,128)(2,1)S(1)} collective-permute-done((bf16[64,3072]{1,0:T(8,128)(2,1)S(1)}, bf16[64,3072]{1,0:T(8,128)(2,1)S(1)}, u32[]{:S(2)}, u32[]{:S(2)}) %collective-permute-start.12) | collective-permute-done | bytes 393248 | tf_op jit(solution)/shard_map/ppermute | solution.py:24
  81.2 0.9 collective-permute-start.22
  82.0 2.0 %collective-permute-done.10.refs_3_ = bf16[64,3072]{1,0:T(8,128)(2,1)S(1)} collective-permute-done((bf16[64,3072]{1,0:T(8,128)(2,1)S(1)}, bf16[64,3072]{1,0:T(8,128)(2,1)S(1)}, u32[]{:S(2)}, u32[]{:S(2)}) %collective-permute-start.10) | collective-permute-done | bytes 393248 | tf_op jit(solution)/shard_map/ppermute | solution.py:24
  84.1 0.5 collective-permute-start.20
  84.6 0.0 collective-permute-start.18
  84.6 1.1 %multiply_convert_fusion = bf16[8,128,2048]{2,1,0:T(8,128)(2,1)S(1)} fusion(f32[8,2048]{1,0:T(8,128)S(1)} %multiply_exponential_fusion, f32[128,2048]{1,0:T(8,128)S(1)} %dynamic-slice_convert_fusion), kind=kLoop, calls=%fused_computation | loop fusion | flops 4194304 | bytes 5308416 | tf_op jit(solution)/shard_map/convert_element_type | solution.py:107
  85.7 0.1 cosine_multiply_fusion.cosines_ref
  85.9 0.0 collective-permute-done.20.refs_13_
  85.9 0.6 collective-permute-done.18.refs_11_
  86.5 9.5 %shard_map.73 = bf16[1024,1024]{1,0:T(8,128)(2,1)} custom-call(f32[8,8]{1,0:T(8,128)S(1)} %cosine_multiply_fusion.cosines_ref, bf16[1024,2048]{1,0:T(8,128)(2,1)S(1)} %bitcast.2, bf16[64,3072]{1,0:T(8,128)(2,1)S(1)} %concatenate.20.refs_0_, bf16[64,3072]{1,0:T(8,128)(2,1)S(1)} %constant_dynamic-update-slice_fusion.2.refs_1_, ...), custom_call_target="tpu_custom_call" | custom-call | flops 6442450944 | bytes 16777216 | tf_op jit(solution)/shard_map/pallas_call | solution.py:77
  (19 shorter events, 0.1 us)
Async XLA Ops:
  1.4 9.0 %collective-permute-start = (bf16[4,3072]{1,0:T(4,128)(2,1)S(1)}, bf16[4,3072]{1,0:T(4,128)(2,1)S(1)}, u32[]{:S(2)}, u32[]{:S(2)}) collective-permute-start(bf16[4,3072]{1,0:T(4,128)(2,1)S(1)} %constant_dynamic-update-slice_fusion), channel_id=1, source_target_pairs={{0,8},{2,10},{4,12},{6,14},{8,0},{10,2},{12,4},{14,6},{1,9},{3,11}... | collective-permute-start | bytes 73736 | tf_op jit(solution)/shard_map/ppermute | solution.py:24
  10.4 3.9 %collective-permute-start.1 = (bf16[8,3072]{1,0:T(8,128)(2,1)S(1)}, bf16[8,3072]{1,0:T(8,128)(2,1)S(1)}, u32[]{:S(2)}, u32[]{:S(2)}) collective-permute-start(bf16[8,3072]{1,0:T(8,128)(2,1)S(1)} %pad_maximum_fusion.1), channel_id=1, source_target_pairs={{0,4},{2,6},{4,0},{6,2},{8,12},{10,14},{12,8},{14,10},{1,5},{3,7},... | collective-permute-start | bytes 147464 | tf_op jit(solution)/shard_map/ppermute | solution.py:24
  14.4 71.3 %copy-start = (f32[8]{0:T(128)S(1)}, f32[8]{0:T(128)}, u32[]{:S(2)}) copy-start(f32[8]{0:T(128)} %param.10) | copy-start | bytes 100
  14.4 71.3 %copy-start.1 = (f32[8]{0:T(128)S(1)}, f32[8]{0:T(128)}, u32[]{:S(2)}) copy-start(f32[8]{0:T(128)} %param.12) | copy-start | bytes 100
  14.4 71.3 %copy-start.2 = (f32[8]{0:T(128)S(1)}, f32[8]{0:T(128)}, u32[]{:S(2)}) copy-start(f32[8]{0:T(128)} %param.11) | copy-start | bytes 100
  14.4 18.3 %collective-permute-start.5 = (bf16[16,3072]{1,0:T(8,128)(2,1)S(1)}, bf16[16,3072]{1,0:T(8,128)(2,1)S(1)}, u32[]{:S(2)}, u32[]{:S(2)}) collective-permute-start(bf16[16,3072]{1,0:T(8,128)(2,1)S(1)} %pad_maximum_fusion), channel_id=1, source_target_pairs={{0,2},{2,0},{4,6},{6,4},{8,10},{10,8},{12,14},{14,12},{1,3},{3,1},... | collective-permute-start | bytes 294920 | tf_op jit(solution)/shard_map/ppermute | solution.py:24
  15.3 6.2 %collective-permute-start.4 = (bf16[16,3072]{1,0:T(8,128)(2,1)S(1)}, bf16[16,3072]{1,0:T(8,128)(2,1)S(1)}, u32[]{:S(2)}, u32[]{:S(2)}) collective-permute-start(bf16[16,3072]{1,0:T(8,128)(2,1)S(1)} %pad_maximum_fusion), channel_id=1, source_target_pairs={{0,16},{16,0},{32,48},{48,32},{1,17},{17,1},{33,49},{49,33},{2,18}... | collective-permute-start | bytes 294920 | tf_op jit(solution)/shard_map/ppermute | solution.py:24
  18.2 3.8 %collective-permute-start.3 = (bf16[16,3072]{1,0:T(8,128)(2,1)S(1)}, bf16[16,3072]{1,0:T(8,128)(2,1)S(1)}, u32[]{:S(2)}, u32[]{:S(2)}) collective-permute-start(bf16[16,3072]{1,0:T(8,128)(2,1)S(1)} %pad_maximum_fusion), channel_id=1, source_target_pairs={{0,48},{16,32},{32,0},{48,16},{1,49},{17,33},{33,1},{49,17},{2,50}... | collective-permute-start | bytes 294920 | tf_op jit(solution)/shard_map/ppermute | solution.py:24
  19.0 5.7 %collective-permute-start.2 = (bf16[16,3072]{1,0:T(8,128)(2,1)S(1)}, bf16[16,3072]{1,0:T(8,128)(2,1)S(1)}, u32[]{:S(2)}, u32[]{:S(2)}) collective-permute-start(bf16[16,3072]{1,0:T(8,128)(2,1)S(1)} %pad_maximum_fusion), channel_id=1, source_target_pairs={{0,32},{16,48},{32,16},{48,0},{1,33},{17,49},{33,17},{49,1},{2,34}... | collective-permute-start | bytes 294920 | tf_op jit(solution)/shard_map/ppermute | solution.py:24
  24.8 38.2 %collective-permute-start.15 = (bf16[64,3072]{1,0:T(8,128)(2,1)S(1)}, bf16[64,3072]{1,0:T(8,128)(2,1)S(1)}, u32[]{:S(2)}, u32[]{:S(2)}) collective-permute-start(bf16[64,3072]{1,0:T(8,128)(2,1)S(1)} %concatenate.20.refs_0_), channel_id=1, source_target_pairs={{0,1},{1,0},{2,3},{3,2},{4,5},{5,4},{6,7},{7,6},{8,9},{9,8},{10,11... | collective-permute-start | bytes 1179656 | tf_op jit(solution)/shard_map/ppermute | solution.py:24
  28.5 34.8 %collective-permute-start.13 = (bf16[64,3072]{1,0:T(8,128)(2,1)S(1)}, bf16[64,3072]{1,0:T(8,128)(2,1)S(1)}, u32[]{:S(2)}, u32[]{:S(2)}) collective-permute-start(bf16[64,3072]{1,0:T(8,128)(2,1)S(1)} %concatenate.20.refs_0_), channel_id=1, source_target_pairs={{0,128},{64,192},{128,0},{192,64},{1,129},{65,193},{129,1},{193,65... | collective-permute-start | bytes 1179656 | tf_op jit(solution)/shard_map/ppermute | solution.py:24
  31.3 33.7 %collective-permute-start.11 = (bf16[64,3072]{1,0:T(8,128)(2,1)S(1)}, bf16[64,3072]{1,0:T(8,128)(2,1)S(1)}, u32[]{:S(2)}, u32[]{:S(2)}) collective-permute-start(bf16[64,3072]{1,0:T(8,128)(2,1)S(1)} %concatenate.20.refs_0_), channel_id=1, source_target_pairs={{0,192},{64,0},{128,64},{192,128},{1,193},{65,1},{129,65},{193,129... | collective-permute-start | bytes 1179656 | tf_op jit(solution)/shard_map/ppermute | solution.py:24
  32.2 32.8 %collective-permute-start.9 = (bf16[64,3072]{1,0:T(8,128)(2,1)S(1)}, bf16[64,3072]{1,0:T(8,128)(2,1)S(1)}, u32[]{:S(2)}, u32[]{:S(2)}) collective-permute-start(bf16[64,3072]{1,0:T(8,128)(2,1)S(1)} %concatenate.20.refs_0_), channel_id=1, source_target_pairs={{0,64},{64,128},{128,192},{192,0},{1,65},{65,129},{129,193},{193,1... | collective-permute-start | bytes 1179656 | tf_op jit(solution)/shard_map/ppermute | solution.py:24
  32.8 18.9 %collective-permute-start.6 = (bf16[16,3072]{1,0:T(8,128)(2,1)S(1)}, bf16[16,3072]{1,0:T(8,128)(2,1)S(1)}, u32[]{:S(2)}, u32[]{:S(2)}) collective-permute-start(bf16[16,3072]{1,0:T(8,128)(2,1)S(1)} %collective-permute-done.5), channel_id=1, source_target_pairs={{0,64},{64,128},{128,192},{192,0},{1,65},{65,129},{129,193},{193,1... | collective-permute-start | bytes 294920 | tf_op jit(solution)/shard_map/ppermute | solution.py:24
  51.6 3.9 %collective-permute-start.7 = (bf16[16,3072]{1,0:T(8,128)(2,1)S(1)}, bf16[16,3072]{1,0:T(8,128)(2,1)S(1)}, u32[]{:S(2)}, u32[]{:S(2)}) collective-permute-start(bf16[16,3072]{1,0:T(8,128)(2,1)S(1)} %collective-permute-done.5), channel_id=1, source_target_pairs={{0,192},{64,0},{128,64},{192,128},{1,193},{65,1},{129,65},{193,129... | collective-permute-start | bytes 294920 | tf_op jit(solution)/shard_map/ppermute | solution.py:24
  55.5 5.0 %collective-permute-start.8 = (bf16[16,3072]{1,0:T(8,128)(2,1)S(1)}, bf16[16,3072]{1,0:T(8,128)(2,1)S(1)}, u32[]{:S(2)}, u32[]{:S(2)}) collective-permute-start(bf16[16,3072]{1,0:T(8,128)(2,1)S(1)} %collective-permute-done.5), channel_id=1, source_target_pairs={{0,128},{64,192},{128,0},{192,64},{1,129},{65,193},{129,1},{193,65... | collective-permute-start | bytes 294920 | tf_op jit(solution)/shard_map/ppermute | solution.py:24
  60.5 6.0 %collective-permute-start.16 = (bf16[64,3072]{1,0:T(8,128)(2,1)S(1)}, bf16[64,3072]{1,0:T(8,128)(2,1)S(1)}, u32[]{:S(2)}, u32[]{:S(2)}) collective-permute-start(bf16[64,3072]{1,0:T(8,128)(2,1)S(1)} %constant_dynamic-update-slice_fusion.2.refs_1_), channel_id=1, source_target_pairs={{0,1},{1,0},{2,3},{3,2},{4,5},{5,4},{6,7},{7,6},{8,9},{9,8},{10,11... | collective-permute-start | bytes 1179656 | tf_op jit(solution)/shard_map/ppermute | solution.py:24
  63.1 12.2 %collective-permute-start.14 = (bf16[64,3072]{1,0:T(8,128)(2,1)S(1)}, bf16[64,3072]{1,0:T(8,128)(2,1)S(1)}, u32[]{:S(2)}, u32[]{:S(2)}) collective-permute-start(bf16[64,3072]{1,0:T(8,128)(2,1)S(1)} %constant_dynamic-update-slice_fusion.2.refs_1_), channel_id=1, source_target_pairs={{0,16},{16,0},{32,48},{48,32},{1,17},{17,1},{33,49},{49,33},{2,18}... | collective-permute-start | bytes 1179656 | tf_op jit(solution)/shard_map/ppermute | solution.py:24
  63.3 17.9 %collective-permute-start.12 = (bf16[64,3072]{1,0:T(8,128)(2,1)S(1)}, bf16[64,3072]{1,0:T(8,128)(2,1)S(1)}, u32[]{:S(2)}, u32[]{:S(2)}) collective-permute-start(bf16[64,3072]{1,0:T(8,128)(2,1)S(1)} %constant_dynamic-update-slice_fusion.2.refs_1_), channel_id=1, source_target_pairs={{0,48},{16,32},{32,0},{48,16},{1,49},{17,33},{33,1},{49,17},{2,50}... | collective-permute-start | bytes 1179656 | tf_op jit(solution)/shard_map/ppermute | solution.py:24
  65.0 19.1 %collective-permute-start.10 = (bf16[64,3072]{1,0:T(8,128)(2,1)S(1)}, bf16[64,3072]{1,0:T(8,128)(2,1)S(1)}, u32[]{:S(2)}, u32[]{:S(2)}) collective-permute-start(bf16[64,3072]{1,0:T(8,128)(2,1)S(1)} %constant_dynamic-update-slice_fusion.2.refs_1_), channel_id=1, source_target_pairs={{0,32},{16,48},{32,16},{48,0},{1,33},{17,49},{33,17},{49,1},{2,34}... | collective-permute-start | bytes 1179656 | tf_op jit(solution)/shard_map/ppermute | solution.py:24
  65.0 19.6 %collective-permute-start.21 = (bf16[64,3072]{1,0:T(8,128)(2,1)S(1)}, bf16[64,3072]{1,0:T(8,128)(2,1)S(1)}, u32[]{:S(2)}, u32[]{:S(2)}) collective-permute-start(bf16[64,3072]{1,0:T(8,128)(2,1)S(1)} %collective-permute-done.13.refs_6_), channel_id=1, source_target_pairs={{0,1},{1,0},{2,3},{3,2},{4,5},{5,4},{6,7},{7,6},{8,9},{9,8},{10,11... | collective-permute-start | bytes 1179656 | tf_op jit(solution)/shard_map/ppermute | solution.py:24
  66.5 19.4 %collective-permute-start.19 = (bf16[64,3072]{1,0:T(8,128)(2,1)S(1)}, bf16[64,3072]{1,0:T(8,128)(2,1)S(1)}, u32[]{:S(2)}, u32[]{:S(2)}) collective-permute-start(bf16[64,3072]{1,0:T(8,128)(2,1)S(1)} %collective-permute-done.11.refs_4_), channel_id=1, source_target_pairs={{0,1},{1,0},{2,3},{3,2},{4,5},{5,4},{6,7},{7,6},{8,9},{9,8},{10,11... | collective-permute-start | bytes 1179656 | tf_op jit(solution)/shard_map/ppermute | solution.py:24
  75.3 10.5 %collective-permute-start.17 = (bf16[64,3072]{1,0:T(8,128)(2,1)S(1)}, bf16[64,3072]{1,0:T(8,128)(2,1)S(1)}, u32[]{:S(2)}, u32[]{:S(2)}) collective-permute-start(bf16[64,3072]{1,0:T(8,128)(2,1)S(1)} %collective-permute-done.9.refs_2_), channel_id=1, source_target_pairs={{0,1},{1,0},{2,3},{3,2},{4,5},{5,4},{6,7},{7,6},{8,9},{9,8},{10,11... | collective-permute-start | bytes 1179656 | tf_op jit(solution)/shard_map/ppermute | solution.py:24
  81.2 4.7 %collective-permute-start.22 = (bf16[64,3072]{1,0:T(8,128)(2,1)S(1)}, bf16[64,3072]{1,0:T(8,128)(2,1)S(1)}, u32[]{:S(2)}, u32[]{:S(2)}) collective-permute-start(bf16[64,3072]{1,0:T(8,128)(2,1)S(1)} %collective-permute-done.14.refs_7_), channel_id=1, source_target_pairs={{0,1},{1,0},{2,3},{3,2},{4,5},{5,4},{6,7},{7,6},{8,9},{9,8},{10,11... | collective-permute-start | bytes 1179656 | tf_op jit(solution)/shard_map/ppermute | solution.py:24
  84.1 1.8 %collective-permute-start.20 = (bf16[64,3072]{1,0:T(8,128)(2,1)S(1)}, bf16[64,3072]{1,0:T(8,128)(2,1)S(1)}, u32[]{:S(2)}, u32[]{:S(2)}) collective-permute-start(bf16[64,3072]{1,0:T(8,128)(2,1)S(1)} %collective-permute-done.12.refs_5_), channel_id=1, source_target_pairs={{0,1},{1,0},{2,3},{3,2},{4,5},{5,4},{6,7},{7,6},{8,9},{9,8},{10,11... | collective-permute-start | bytes 1179656 | tf_op jit(solution)/shard_map/ppermute | solution.py:24
  84.6 1.9 %collective-permute-start.18 = (bf16[64,3072]{1,0:T(8,128)(2,1)S(1)}, bf16[64,3072]{1,0:T(8,128)(2,1)S(1)}, u32[]{:S(2)}, u32[]{:S(2)}) collective-permute-start(bf16[64,3072]{1,0:T(8,128)(2,1)S(1)} %collective-permute-done.10.refs_3_), channel_id=1, source_target_pairs={{0,1},{1,0},{2,3},{3,2},{4,5},{5,4},{6,7},{7,6},{8,9},{9,8},{10,11... | collective-permute-start | bytes 1179656 | tf_op jit(solution)/shard_map/ppermute | solution.py:24

commit v2 on v1

v2 whole, which is shorter than its diff:
```python
import itertools

import jax
import jax.numpy as jnp
import numpy as np
from jax import lax
from jax.experimental import pallas as pl
from jax.experimental.pallas import tpu as pltpu
from jax.sharding import Mesh
from jax.sharding import PartitionSpec as P

NOCC = 512
BANDS = 2048
PANEL = 1024
FREQS = 8
TAUS = 8
COLS = 256

TM = ("x", "ylo")
PTS = ("yhi", "z", "core")
SIZES = (4, 2, 2, 8, 2)
RING = 4


def moved(value, target):
    pairs = []
    for source, (x, ylo, yhi, z, core) in enumerate(itertools.product(*map(range, SIZES))):
        x, y, z, core = target(x, 2 * yhi + ylo, z, core)
        place = (x % RING, y % 2, y % RING // 2, z % SIZES[3], core)
        pairs.append((source, int(np.ravel_multi_index(place, SIZES))))
    return lax.ppermute(value, TM + PTS, pairs)


def z_flip(bit):
    return lambda x, y, z, core: (x, y, z ^ bit, core)


def y_then_x(step):
    return lambda x, y, z, core: (x + step * core, y + step * (1 - core), z, core)


def x_then_y(step):
    return lambda x, y, z, core: (x + step * (1 - core), y + step * core, z, core)


def other_core(x, y, z, core):
    return x, y, z, 1 - core


def contract(left, right):
    return lax.dot_general(
        left, right, (((1,), (1,)), ((), ())), preferred_element_type=jnp.float32
    )


def transform_kernel(cosines_ref, scaled_ref, *refs):
    pieces, out_ref = refs[:-1], refs[-1]
    rows = scaled_ref.shape[0] // TAUS
    occ = jnp.concatenate([p[:, :NOCC] for p in pieces], axis=0)
    vir = jnp.concatenate([p[:, NOCC:BANDS] for p in pieces], axis=0)
    polar = -(contract(scaled_ref[:, :NOCC], occ) * contract(scaled_ref[:, NOCC:], vir))
    for k in range(FREQS):
        total = cosines_ref[k, 0] * polar[:rows]
        for t in range(1, TAUS):
            total += cosines_ref[k, t] * polar[t * rows : (t + 1) * rows]
        out_ref[k * rows : (k + 1) * rows, :] = total.astype(jnp.bfloat16)


def screen_kernel(*refs):
    blocks, pieces, out_ref = refs[:4], refs[4:-1], refs[-1]
    transformed = jnp.concatenate([b[...] for b in blocks], axis=1)
    for start in range(0, PANEL, COLS):
        columns = slice(BANDS + start, BANDS + start + COLS)
        coulomb = jnp.concatenate([p[:, columns] for p in pieces], axis=0)
        out_ref[:, start : start + COLS] = jnp.dot(
            transformed, coulomb, preferred_element_type=jnp.float32
        ).astype(jnp.bfloat16)


VMEM = pl.BlockSpec(memory_space=pltpu.VMEM)


def transform(cosines, scaled, pieces):
    rows, width = scaled.shape[0], sum(p.shape[0] for p in pieces)
    return pl.pallas_call(
        transform_kernel,
        out_shape=jax.ShapeDtypeStruct((rows, width), jnp.bfloat16),
        in_specs=[pl.BlockSpec(memory_space=pltpu.SMEM), VMEM] + [VMEM] * len(pieces),
        out_specs=VMEM,
        compiler_params=pltpu.CompilerParams(vmem_limit_bytes=24 * 2**20),
        cost_estimate=pl.CostEstimate(
            flops=2 * rows * width * BANDS, bytes_accessed=2**20, transcendentals=0
        ),
    )(cosines, scaled, *pieces)


def screen(blocks, pieces):
    rows = blocks[0].shape[0]
    return pl.pallas_call(
        screen_kernel,
        out_shape=jax.ShapeDtypeStruct((rows, PANEL), jnp.bfloat16),
        in_specs=[VMEM] * (len(blocks) + len(pieces)),
        out_specs=VMEM,
        compiler_params=pltpu.CompilerParams(vmem_limit_bytes=24 * 2**20),
        cost_estimate=pl.CostEstimate(
            flops=2 * rows * PANEL * PANEL, bytes_accessed=2**22, transcendentals=0
        ),
    )(*blocks, *pieces)


def join_kernel(*refs):
    del refs


def joined(values, after):
    return pl.pallas_call(
        join_kernel,
        out_shape=[jax.ShapeDtypeStruct(v.shape, v.dtype) for v in values],
        in_specs=[pl.BlockSpec(memory_space=pl.ANY)] * (len(values) + 1),
        out_specs=[pl.BlockSpec(memory_space=pl.ANY)] * len(values),
        input_output_aliases={k: k for k in range(len(values))},
        compiler_params=pltpu.CompilerParams(vmem_limit_bytes=2**20),
    )(*values, after)


def shards(orbitals, panel_orbitals, band_gap, tau_points, quad_weight, frequencies, coulomb):
    held = jnp.concatenate([panel_orbitals, coulomb], axis=1)
    for bit in (4, 2, 1):
        held = jnp.concatenate([held, moved(held, z_flip(bit))], axis=0)
    rows = orbitals.shape[0] // lax.axis_size(TM)
    own = lax.dynamic_slice_in_dim(orbitals, lax.axis_index(TM) * rows, rows).astype(jnp.float32)
    decay = jnp.exp(-band_gap[None, :] * tau_points[:, None])
    scaled = (own[None] * decay[:, None, :]).astype(jnp.bfloat16).reshape(TAUS * rows, BANDS)
    cosines = quad_weight[None, :] * jnp.cos(frequencies[:, None] * tau_points[None, :])

    held, cosines, scaled = lax.optimization_barrier((held, cosines, scaled))
    held = jnp.concatenate([held] + [moved(held, y_then_x(s)) for s in (1, 3, 2)], axis=0)
    others = [moved(held, x_then_y(s)) for s in (1, 3, 2)]
    both = [held, moved(held, other_core)]
    blocks, pieces = [transform(cosines, scaled, both)], both
    for chunk in joined(others, blocks[0]):
        both = [chunk, moved(chunk, other_core)]
        blocks.append(transform(cosines, scaled, both))
        pieces += both
    return screen(blocks, pieces).reshape(FREQS, rows, PANEL)


def solution(mesh):
    split = Mesh(mesh.devices.reshape(SIZES), TM + PTS)
    everywhere = P(TM + PTS, None)
    placed = (P(PTS, None), everywhere, P(), P(), P(), P(), everywhere)
    return jax.shard_map(
        shards, mesh=split, in_specs=placed, out_specs=P(None, PTS + TM, None), check_vma=False
    )
```

time: 96.3 us -> 69.4 us (0.72)
  waiting for transfers between devices: 47.2 us -> 27 us
  starting transfers between devices: 33.8 us -> 23.2 us
  Pallas kernels: 9.52 us -> 13.4 us
    ppermute x23 -> x13, waiting for transfers between devices: 47.2 us -> 27 us  [moved(): return lax.ppermute(value, TM + PTS, pairs)]
    ppermute x23 -> x13, starting transfers between devices: 33.8 us -> 23.2 us  [moved(): return lax.ppermute(value, TM + PTS, pairs)]
    pallas_call x0 -> x5, Pallas kernels: none -> 9.69 us  [the longest x4 9.68 us: transform(): pl.pallas_call(transform_kernel, out_shape=jax.ShapeDtypeStruct((rows, wi...]
    pallas_call x1, Pallas kernels: 9.52 us -> 3.67 us  [screen(): pl.pallas_call(screen_kernel, out_shape=jax.ShapeDtypeStruct((rows, PANEL...]
  transfers between devices with their start and end apart: 23 -> 13, of which waited for: 11 -> 7; matrix products, arithmetic and copies ran while one was open for 4% -> 6% of each run, Pallas kernels for 0% -> 11%
where the time goes in v2:
time: 69.4 us; the launch traced here: 69.1 us
  waiting for transfers between devices  27 us (39%)
  starting transfers between devices  23.2 us (33%)
  Pallas kernels  13.4 us (19%)
  other arithmetic  3.91 us (6%)
  local copies, waits for them, and re-layouts  1.54 us (2%)
    ppermute x13, waiting for transfers between devices, moved(): return lax.ppermute(value, TM + PTS, pairs)  27 us
    ppermute x13, starting transfers between devices, moved(): return lax.ppermute(value, TM + PTS, pairs)  23.2 us
    pallas_call x4, Pallas kernels, transform(): pl.pallas_call(transform_kernel, out_shape=jax.ShapeDtypeStruct((rows, wi...  9.68 us
    pallas_call x1, Pallas kernels, screen(): pl.pallas_call(screen_kernel, out_shape=jax.ShapeDtypeStruct((rows, PANEL...  3.67 us
  transfers between devices with their start and end apart: 13, of which 7 were waited for; matrix products, arithmetic and copies ran while one was open for 6% of the time, Pallas kernels for 11%

profile of v2, /device:TPU:1, one launch (start us, length us, event | category | flops | bytes accessed | tf_op | source)
XLA Modules:
  0.0 69.1 jit_solution(7788403067460662196)
XLA Ops:
  0.0 0.0 copy-start
  0.0 0.0 copy-start.1
  0.0 0.0 copy-start.2
  0.0 0.8 %constant_dynamic-update-slice_fusion.1 = bf16[4,3072]{1,0:T(4,128)(2,1)S(1)} fusion(bf16[4,2048]{1,0:T(4,128)(2,1)} %param.8), kind=kLoop, calls=%fused_computation.7 | loop fusion | bytes 32768
  0.8 0.7 %constant_dynamic-update-slice_fusion = bf16[4,3072]{1,0:T(4,128)(2,1)S(1)} fusion(bf16[4,3072]{1,0:T(4,128)(2,1)S(1)} %constant_dynamic-update-slice_fusion.1, bf16[4,1024]{1,0:T(4,128)(2,1)} %param.13), kind=kLoop, calls=%fused_computation.6 | loop fusion | bytes 16384 | tf_op jit(solution)/shard_map/concatenate | solution.py:127
  1.5 7.7 %collective-permute-start = (bf16[4,3072]{1,0:T(4,128)(2,1)S(1)}, bf16[4,3072]{1,0:T(4,128)(2,1)S(1)}, u32[]{:S(2)}, u32[]{:S(2)}) collective-permute-start(bf16[4,3072]{1,0:T(4,128)(2,1)S(1)} %constant_dynamic-update-slice_fusion), channel_id=1, source_target_pairs={{0,8},{1,9},{2,10},{3,11},{4,12},{5,13},{6,14},{7,15},{8,0},{9,1},... | collective-permute-start | bytes 73736 | tf_op jit(solution)/shard_map/ppermute | solution.py:31
  9.2 0.7 %neg.4 = f32[2048]{0:T(1024)S(1)} negate(f32[2048]{0:T(1024)} %param.9) | non-fusion elementwise | flops 2048 | bytes 16384 | tf_op jit(solution)/shard_map/neg | solution.py:132
  9.9 0.7 %multiply_exponential_fusion = f32[8,2048]{1,0:T(8,128)S(1)} fusion(f32[8]{0:T(128)} %param.10, f32[2048]{0:T(1024)S(1)} %neg.4), kind=kLoop, calls=%fused_computation.4 | loop fusion | flops 16384 | bytes 73760 | tf_op jit(solution)/shard_map/exp | solution.py:132
  10.7 1.1 %dynamic-slice_convert_fusion = f32[128,2048]{1,0:T(8,128)S(1)} fusion(bf16[1024,2048]{1,0:T(8,128)(2,1)} %param.7, s32[]{:T(128)S(6)} %select_n.3), kind=kLoop, calls=%fused_computation.1 | loop fusion | flops 262144 | bytes 1572868 | tf_op jit(solution)/shard_map/convert_element_type | solution.py:131
  11.8 0.0 collective-permute-done
  11.9 1.3 %collective-permute-start.1 = (bf16[8,3072]{1,0:T(8,128)(2,1)S(1)}, bf16[8,3072]{1,0:T(8,128)(2,1)S(1)}, u32[]{:S(2)}, u32[]{:S(2)}) collective-permute-start(bf16[8,3072]{1,0:T(8,128)(2,1)S(1)} %pad_maximum_fusion.2), channel_id=1, source_target_pairs={{0,4},{1,5},{2,6},{3,7},{4,0},{5,1},{6,2},{7,3},{8,12},{9,13},{10,... | collective-permute-start | bytes 147464 | tf_op jit(solution)/shard_map/ppermute | solution.py:31
  13.1 1.1 %multiply_convert_fusion = bf16[8,128,2048]{2,1,0:T(8,128)(2,1)S(1)} fusion(f32[8,2048]{1,0:T(8,128)S(1)} %multiply_exponential_fusion, f32[128,2048]{1,0:T(8,128)S(1)} %dynamic-slice_convert_fusion), kind=kLoop, calls=%fused_computation | loop fusion | flops 4194304 | bytes 5308416 | tf_op jit(solution)/shard_map/convert_element_type | solution.py:133
  14.2 1.5 %collective-permute-done.1 = bf16[8,3072]{1,0:T(8,128)(2,1)S(1)} collective-permute-done((bf16[8,3072]{1,0:T(8,128)(2,1)S(1)}, bf16[8,3072]{1,0:T(8,128)(2,1)S(1)}, u32[]{:S(2)}, u32[]{:S(2)}) %collective-permute-start.1) | collective-permute-done | bytes 49184 | tf_op jit(solution)/shard_map/ppermute | solution.py:31
  15.8 0.9 %collective-permute-start.2 = (bf16[16,3072]{1,0:T(8,128)(2,1)S(1)}, bf16[16,3072]{1,0:T(8,128)(2,1)S(1)}, u32[]{:S(2)}, u32[]{:S(2)}) collective-permute-start(bf16[16,3072]{1,0:T(8,128)(2,1)S(1)} %pad_maximum_fusion.1), channel_id=1, source_target_pairs={{0,2},{1,3},{2,0},{3,1},{4,6},{5,7},{6,4},{7,5},{8,10},{9,11},{10,... | collective-permute-start | bytes 294920 | tf_op jit(solution)/shard_map/ppermute | solution.py:31
  16.7 0.0 copy-done
  16.7 0.0 copy-done.1
  16.7 0.0 copy-done.2
  16.7 0.1 cosine_multiply_fusion.cosines_ref
  16.8 2.5 %collective-permute-done.2 = bf16[16,3072]{1,0:T(8,128)(2,1)S(1)} collective-permute-done((bf16[16,3072]{1,0:T(8,128)(2,1)S(1)}, bf16[16,3072]{1,0:T(8,128)(2,1)S(1)}, u32[]{:S(2)}, u32[]{:S(2)}) %collective-permute-start.2) | collective-permute-done | bytes 98336 | tf_op jit(solution)/shard_map/ppermute | solution.py:31
  19.4 2.8 %collective-permute-start.5 = (bf16[32,3072]{1,0:T(8,128)(2,1)S(1)}, bf16[32,3072]{1,0:T(8,128)(2,1)S(1)}, u32[]{:S(2)}, u32[]{:S(2)}) collective-permute-start(bf16[32,3072]{1,0:T(8,128)(2,1)S(1)} %pad_maximum_fusion), channel_id=1, source_target_pairs={{0,16},{1,129},{2,18},{3,131},{4,20},{5,133},{6,22},{7,135},{8,24}... | collective-permute-start | bytes 589832 | tf_op jit(solution)/shard_map/ppermute | solution.py:31
  22.3 0.9 %collective-permute-start.4 = (bf16[32,3072]{1,0:T(8,128)(2,1)S(1)}, bf16[32,3072]{1,0:T(8,128)(2,1)S(1)}, u32[]{:S(2)}, u32[]{:S(2)}) collective-permute-start(bf16[32,3072]{1,0:T(8,128)(2,1)S(1)} %pad_maximum_fusion), channel_id=1, source_target_pairs={{0,48},{1,193},{2,50},{3,195},{4,52},{5,197},{6,54},{7,199},{8,56}... | collective-permute-start | bytes 589832 | tf_op jit(solution)/shard_map/ppermute | solution.py:31
  23.1 0.6 collective-permute-start.3
  23.8 5.4 %collective-permute-done.3 = bf16[32,3072]{1,0:T(8,128)(2,1)S(1)} collective-permute-done((bf16[32,3072]{1,0:T(8,128)(2,1)S(1)}, bf16[32,3072]{1,0:T(8,128)(2,1)S(1)}, u32[]{:S(2)}, u32[]{:S(2)}) %collective-permute-start.3) | collective-permute-done | bytes 196640 | tf_op jit(solution)/shard_map/ppermute | solution.py:31
  29.2 0.0 collective-permute-done.4
  29.2 0.0 collective-permute-done.5
  29.2 4.8 %collective-permute-start.6 = (bf16[128,3072]{1,0:T(8,128)(2,1)S(1)}, bf16[128,3072]{1,0:T(8,128)(2,1)S(1)}, u32[]{:S(2)}, u32[]{:S(2)}) collective-permute-start(bf16[128,3072]{1,0:T(8,128)(2,1)S(1)} %constant_dynamic-update-slice_fusion.2.refs_0_.refs_4_), channel_id=1, source_target_pairs={{0,1},{1,0},{2,3},{3,2},{4,5},{5,4},{6,7},{7,6},{8,9},{9,8},{10,11... | collective-permute-start | bytes 2359304 | tf_op jit(solution)/shard_map/ppermute | solution.py:31
  34.1 1.1 %collective-permute-start.9 = (bf16[128,3072]{1,0:T(8,128)(2,1)S(1)}, bf16[128,3072]{1,0:T(8,128)(2,1)S(1)}, u32[]{:S(2)}, u32[]{:S(2)}) collective-permute-start(bf16[128,3072]{1,0:T(8,128)(2,1)S(1)} %constant_dynamic-update-slice_fusion.2.refs_0_.refs_4_), channel_id=1, source_target_pairs={{0,128},{1,17},{2,130},{3,19},{4,132},{5,21},{6,134},{7,23},{8,136... | collective-permute-start | bytes 2359304 | tf_op jit(solution)/shard_map/ppermute | solution.py:31
  35.2 0.9 %collective-permute-start.8 = (bf16[128,3072]{1,0:T(8,128)(2,1)S(1)}, bf16[128,3072]{1,0:T(8,128)(2,1)S(1)}, u32[]{:S(2)}, u32[]{:S(2)}) collective-permute-start(bf16[128,3072]{1,0:T(8,128)(2,1)S(1)} %constant_dynamic-update-slice_fusion.2.refs_0_.refs_4_), channel_id=1, source_target_pairs={{0,192},{1,49},{2,194},{3,51},{4,196},{5,53},{6,198},{7,55},{8,200... | collective-permute-start | bytes 2359304 | tf_op jit(solution)/shard_map/ppermute | solution.py:31
  36.0 0.6 collective-permute-start.7
  36.6 0.0 collective-permute-done.6.refs_1_.refs_5_
  36.6 2.4 %shard_map.73.refs_3_.refs_0_ = bf16[1024,256]{1,0:T(8,128)(2,1)S(1)} custom-call(f32[8,8]{1,0:T(8,128)S(1)} %cosine_multiply_fusion.cosines_ref, bf16[1024,2048]{1,0:T(8,128)(2,1)S(1)} %bitcast.2, bf16[128,3072]{1,0:T(8,128)(2,1)S(1)} %constant_dynamic-update-slice_fusion.2.refs_0_.refs_4_, bf16[128,3072]{1,0:T(8,128)(2,1)S(1)} %collective-permute-done.6.refs_1_.refs_5_), custom_call_target="tpu_custom_call" | custom-call | flops 1073741824 | bytes 1048576 | tf_op jit(solution)/shard_map/pallas_call | solution.py:85
  39.1 7.7 %collective-permute-done.9.refs_2_ = bf16[128,3072]{1,0:T(8,128)(2,1)S(1)} collective-permute-done((bf16[128,3072]{1,0:T(8,128)(2,1)S(1)}, bf16[128,3072]{1,0:T(8,128)(2,1)S(1)}, u32[]{:S(2)}, u32[]{:S(2)}) %collective-permute-start.9) | collective-permute-done | bytes 786464 | tf_op jit(solution)/shard_map/ppermute | solution.py:31
  46.8 6.9 %collective-permute-done.8.refs_1_ = bf16[128,3072]{1,0:T(8,128)(2,1)S(1)} collective-permute-done((bf16[128,3072]{1,0:T(8,128)(2,1)S(1)}, bf16[128,3072]{1,0:T(8,128)(2,1)S(1)}, u32[]{:S(2)}, u32[]{:S(2)}) %collective-permute-start.8) | collective-permute-done | bytes 786464 | tf_op jit(solution)/shard_map/ppermute | solution.py:31
  53.7 1.5 %collective-permute-done.7.refs_0_ = bf16[128,3072]{1,0:T(8,128)(2,1)S(1)} collective-permute-done((bf16[128,3072]{1,0:T(8,128)(2,1)S(1)}, bf16[128,3072]{1,0:T(8,128)(2,1)S(1)}, u32[]{:S(2)}, u32[]{:S(2)}) %collective-permute-start.7) | collective-permute-done | bytes 786464 | tf_op jit(solution)/shard_map/ppermute | solution.py:31
  55.2 1.1 %collective-permute-start.10 = (bf16[128,3072]{1,0:T(8,128)(2,1)S(1)}, bf16[128,3072]{1,0:T(8,128)(2,1)S(1)}, u32[]{:S(2)}, u32[]{:S(2)}) collective-permute-start(bf16[128,3072]{1,0:T(8,128)(2,1)S(1)} %get-tuple-element.14.refs_0_.refs_6_), channel_id=1, source_target_pairs={{0,1},{1,0},{2,3},{3,2},{4,5},{5,4},{6,7},{7,6},{8,9},{9,8},{10,11... | collective-permute-start | bytes 2359304 | tf_op jit(solution)/shard_map/ppermute | solution.py:31
  56.2 0.1 collective-permute-start.11
  56.3 0.4 collective-permute-start.12
  56.8 1.4 %collective-permute-done.10.refs_1_.refs_7_ = bf16[128,3072]{1,0:T(8,128)(2,1)S(1)} collective-permute-done((bf16[128,3072]{1,0:T(8,128)(2,1)S(1)}, bf16[128,3072]{1,0:T(8,128)(2,1)S(1)}, u32[]{:S(2)}, u32[]{:S(2)}) %collective-permute-start.10) | collective-permute-done | bytes 786464 | tf_op jit(solution)/shard_map/ppermute | solution.py:31
  58.2 2.4 %shard_map.75.refs_1_ = bf16[1024,256]{1,0:T(8,128)(2,1)S(1)} custom-call(f32[8,8]{1,0:T(8,128)S(1)} %cosine_multiply_fusion.cosines_ref, bf16[1024,2048]{1,0:T(8,128)(2,1)S(1)} %bitcast.3, bf16[128,3072]{1,0:T(8,128)(2,1)S(1)} %get-tuple-element.14.refs_0_.refs_6_, bf16[128,3072]{1,0:T(8,128)(2,1)S(1)} %collective-permute-done.10.refs_1_.refs_7_), custom_call_target="tpu_custom_call" | custom-call | flops 1073741824 | bytes 1048576 | tf_op jit(solution)/shard_map/pallas_call | solution.py:85
  60.6 0.0 collective-permute-done.11.refs_1_.refs_9_
  60.6 2.4 %shard_map.76.refs_2_ = bf16[1024,256]{1,0:T(8,128)(2,1)S(1)} custom-call(f32[8,8]{1,0:T(8,128)S(1)} %cosine_multiply_fusion.cosines_ref, bf16[1024,2048]{1,0:T(8,128)(2,1)S(1)} %bitcast.4, bf16[128,3072]{1,0:T(8,128)(2,1)S(1)} %get-tuple-element.15.refs_0_.refs_8_, bf16[128,3072]{1,0:T(8,128)(2,1)S(1)} %collective-permute-done.11.refs_1_.refs_9_), custom_call_target="tpu_custom_call" | custom-call | flops 1073741824 | bytes 1048576 | tf_op jit(solution)/shard_map/pallas_call | solution.py:85
  63.0 0.0 collective-permute-done.12.refs_1_.refs_11_
  63.0 2.4 %shard_map.77.refs_3_ = bf16[1024,256]{1,0:T(8,128)(2,1)S(1)} custom-call(f32[8,8]{1,0:T(8,128)S(1)} %cosine_multiply_fusion.cosines_ref, bf16[1024,2048]{1,0:T(8,128)(2,1)S(1)} %bitcast.5, bf16[128,3072]{1,0:T(8,128)(2,1)S(1)} %get-tuple-element.16.refs_0_.refs_10_, bf16[128,3072]{1,0:T(8,128)(2,1)S(1)} %collective-permute-done.12.refs_1_.refs_11_), custom_call_target="tpu_custom_call" | custom-call | flops 1073741824 | bytes 1048576 | tf_op jit(solution)/shard_map/pallas_call | solution.py:85
  65.5 3.7 %shard_map.78 = bf16[1024,1024]{1,0:T(8,128)(2,1)} custom-call(bf16[1024,256]{1,0:T(8,128)(2,1)S(1)} %shard_map.73.refs_3_.refs_0_, bf16[1024,256]{1,0:T(8,128)(2,1)S(1)} %shard_map.75.refs_1_, bf16[1024,256]{1,0:T(8,128)(2,1)S(1)} %shard_map.76.refs_2_, bf16[1024,256]{1,0:T(8,128)(2,1)S(1)} %shard_map.77.refs_3_, ...), custom_call_target="tpu_custom_call" | custom-call | flops 2147483648 | bytes 4194304 | tf_op jit(solution)/shard_map/pallas_call | solution.py:99
  (8 shorter events, 0.2 us)
Async XLA Ops:
  0.0 16.7 %copy-start = (f32[8]{0:T(128)S(1)}, f32[8]{0:T(128)}, u32[]{:S(2)}) copy-start(f32[8]{0:T(128)} %param.10) | copy-start | bytes 100
  0.0 16.7 %copy-start.1 = (f32[8]{0:T(128)S(1)}, f32[8]{0:T(128)}, u32[]{:S(2)}) copy-start(f32[8]{0:T(128)} %param.12) | copy-start | bytes 100
  0.0 16.7 %copy-start.2 = (f32[8]{0:T(128)S(1)}, f32[8]{0:T(128)}, u32[]{:S(2)}) copy-start(f32[8]{0:T(128)} %param.11) | copy-start | bytes 100
  1.5 10.3 %collective-permute-start = (bf16[4,3072]{1,0:T(4,128)(2,1)S(1)}, bf16[4,3072]{1,0:T(4,128)(2,1)S(1)}, u32[]{:S(2)}, u32[]{:S(2)}) collective-permute-start(bf16[4,3072]{1,0:T(4,128)(2,1)S(1)} %constant_dynamic-update-slice_fusion), channel_id=1, source_target_pairs={{0,8},{1,9},{2,10},{3,11},{4,12},{5,13},{6,14},{7,15},{8,0},{9,1},... | collective-permute-start | bytes 73736 | tf_op jit(solution)/shard_map/ppermute | solution.py:31
  11.9 3.9 %collective-permute-start.1 = (bf16[8,3072]{1,0:T(8,128)(2,1)S(1)}, bf16[8,3072]{1,0:T(8,128)(2,1)S(1)}, u32[]{:S(2)}, u32[]{:S(2)}) collective-permute-start(bf16[8,3072]{1,0:T(8,128)(2,1)S(1)} %pad_maximum_fusion.2), channel_id=1, source_target_pairs={{0,4},{1,5},{2,6},{3,7},{4,0},{5,1},{6,2},{7,3},{8,12},{9,13},{10,... | collective-permute-start | bytes 147464 | tf_op jit(solution)/shard_map/ppermute | solution.py:31
  15.8 3.6 %collective-permute-start.2 = (bf16[16,3072]{1,0:T(8,128)(2,1)S(1)}, bf16[16,3072]{1,0:T(8,128)(2,1)S(1)}, u32[]{:S(2)}, u32[]{:S(2)}) collective-permute-start(bf16[16,3072]{1,0:T(8,128)(2,1)S(1)} %pad_maximum_fusion.1), channel_id=1, source_target_pairs={{0,2},{1,3},{2,0},{3,1},{4,6},{5,7},{6,4},{7,5},{8,10},{9,11},{10,... | collective-permute-start | bytes 294920 | tf_op jit(solution)/shard_map/ppermute | solution.py:31
  19.4 9.8 %collective-permute-start.5 = (bf16[32,3072]{1,0:T(8,128)(2,1)S(1)}, bf16[32,3072]{1,0:T(8,128)(2,1)S(1)}, u32[]{:S(2)}, u32[]{:S(2)}) collective-permute-start(bf16[32,3072]{1,0:T(8,128)(2,1)S(1)} %pad_maximum_fusion), channel_id=1, source_target_pairs={{0,16},{1,129},{2,18},{3,131},{4,20},{5,133},{6,22},{7,135},{8,24}... | collective-permute-start | bytes 589832 | tf_op jit(solution)/shard_map/ppermute | solution.py:31
  22.3 6.9 %collective-permute-start.4 = (bf16[32,3072]{1,0:T(8,128)(2,1)S(1)}, bf16[32,3072]{1,0:T(8,128)(2,1)S(1)}, u32[]{:S(2)}, u32[]{:S(2)}) collective-permute-start(bf16[32,3072]{1,0:T(8,128)(2,1)S(1)} %pad_maximum_fusion), channel_id=1, source_target_pairs={{0,48},{1,193},{2,50},{3,195},{4,52},{5,197},{6,54},{7,199},{8,56}... | collective-permute-start | bytes 589832 | tf_op jit(solution)/shard_map/ppermute | solution.py:31
  23.1 6.0 %collective-permute-start.3 = (bf16[32,3072]{1,0:T(8,128)(2,1)S(1)}, bf16[32,3072]{1,0:T(8,128)(2,1)S(1)}, u32[]{:S(2)}, u32[]{:S(2)}) collective-permute-start(bf16[32,3072]{1,0:T(8,128)(2,1)S(1)} %pad_maximum_fusion), channel_id=1, source_target_pairs={{0,32},{1,65},{2,34},{3,67},{4,36},{5,69},{6,38},{7,71},{8,40},{9,... | collective-permute-start | bytes 589832 | tf_op jit(solution)/shard_map/ppermute | solution.py:31
  29.2 7.4 %collective-permute-start.6 = (bf16[128,3072]{1,0:T(8,128)(2,1)S(1)}, bf16[128,3072]{1,0:T(8,128)(2,1)S(1)}, u32[]{:S(2)}, u32[]{:S(2)}) collective-permute-start(bf16[128,3072]{1,0:T(8,128)(2,1)S(1)} %constant_dynamic-update-slice_fusion.2.refs_0_.refs_4_), channel_id=1, source_target_pairs={{0,1},{1,0},{2,3},{3,2},{4,5},{5,4},{6,7},{7,6},{8,9},{9,8},{10,11... | collective-permute-start | bytes 2359304 | tf_op jit(solution)/shard_map/ppermute | solution.py:31
  34.1 12.7 %collective-permute-start.9 = (bf16[128,3072]{1,0:T(8,128)(2,1)S(1)}, bf16[128,3072]{1,0:T(8,128)(2,1)S(1)}, u32[]{:S(2)}, u32[]{:S(2)}) collective-permute-start(bf16[128,3072]{1,0:T(8,128)(2,1)S(1)} %constant_dynamic-update-slice_fusion.2.refs_0_.refs_4_), channel_id=1, source_target_pairs={{0,128},{1,17},{2,130},{3,19},{4,132},{5,21},{6,134},{7,23},{8,136... | collective-permute-start | bytes 2359304 | tf_op jit(solution)/shard_map/ppermute | solution.py:31
  35.2 18.5 %collective-permute-start.8 = (bf16[128,3072]{1,0:T(8,128)(2,1)S(1)}, bf16[128,3072]{1,0:T(8,128)(2,1)S(1)}, u32[]{:S(2)}, u32[]{:S(2)}) collective-permute-start(bf16[128,3072]{1,0:T(8,128)(2,1)S(1)} %constant_dynamic-update-slice_fusion.2.refs_0_.refs_4_), channel_id=1, source_target_pairs={{0,192},{1,49},{2,194},{3,51},{4,196},{5,53},{6,198},{7,55},{8,200... | collective-permute-start | bytes 2359304 | tf_op jit(solution)/shard_map/ppermute | solution.py:31
  36.0 19.1 %collective-permute-start.7 = (bf16[128,3072]{1,0:T(8,128)(2,1)S(1)}, bf16[128,3072]{1,0:T(8,128)(2,1)S(1)}, u32[]{:S(2)}, u32[]{:S(2)}) collective-permute-start(bf16[128,3072]{1,0:T(8,128)(2,1)S(1)} %constant_dynamic-update-slice_fusion.2.refs_0_.refs_4_), channel_id=1, source_target_pairs={{0,64},{1,33},{2,66},{3,35},{4,68},{5,37},{6,70},{7,39},{8,72},{9,... | collective-permute-start | bytes 2359304 | tf_op jit(solution)/shard_map/ppermute | solution.py:31
  55.2 3.0 %collective-permute-start.10 = (bf16[128,3072]{1,0:T(8,128)(2,1)S(1)}, bf16[128,3072]{1,0:T(8,128)(2,1)S(1)}, u32[]{:S(2)}, u32[]{:S(2)}) collective-permute-start(bf16[128,3072]{1,0:T(8,128)(2,1)S(1)} %get-tuple-element.14.refs_0_.refs_6_), channel_id=1, source_target_pairs={{0,1},{1,0},{2,3},{3,2},{4,5},{5,4},{6,7},{7,6},{8,9},{9,8},{10,11... | collective-permute-start | bytes 2359304 | tf_op jit(solution)/shard_map/ppermute | solution.py:31
  56.2 4.3 %collective-permute-start.11 = (bf16[128,3072]{1,0:T(8,128)(2,1)S(1)}, bf16[128,3072]{1,0:T(8,128)(2,1)S(1)}, u32[]{:S(2)}, u32[]{:S(2)}) collective-permute-start(bf16[128,3072]{1,0:T(8,128)(2,1)S(1)} %get-tuple-element.15.refs_0_.refs_8_), channel_id=1, source_target_pairs={{0,1},{1,0},{2,3},{3,2},{4,5},{5,4},{6,7},{7,6},{8,9},{9,8},{10,11... | collective-permute-start | bytes 2359304 | tf_op jit(solution)/shard_map/ppermute | solution.py:31
  56.3 6.7 %collective-permute-start.12 = (bf16[128,3072]{1,0:T(8,128)(2,1)S(1)}, bf16[128,3072]{1,0:T(8,128)(2,1)S(1)}, u32[]{:S(2)}, u32[]{:S(2)}) collective-permute-start(bf16[128,3072]{1,0:T(8,128)(2,1)S(1)} %get-tuple-element.16.refs_0_.refs_10_), channel_id=1, source_target_pairs={{0,1},{1,0},{2,3},{3,2},{4,5},{5,4},{6,7},{7,6},{8,9},{9,8},{10,11... | collective-permute-start | bytes 2359304 | tf_op jit(solution)/shard_map/ppermute | solution.py:31

commit v3 on v2

v3 whole, which is shorter than its diff:
```python
import functools
import itertools

import jax
import jax.numpy as jnp
import numpy as np
from jax import lax
from jax.experimental import pallas as pl
from jax.experimental.pallas import tpu as pltpu
from jax.sharding import Mesh
from jax.sharding import PartitionSpec as P

NOCC = 512
BANDS = 2048
PANEL = 1024
FREQS = 8
TAUS = 8
COLS = 256

TM = ("x", "ylo")
PTS = ("yhi", "z", "core")
SIZES = (4, 2, 2, 8, 2)
RING = 4


def moved(value, target):
    pairs = []
    for source, (x, ylo, yhi, z, core) in enumerate(itertools.product(*map(range, SIZES))):
        x, y, z, core = target(x, 2 * yhi + ylo, z, core)
        place = (x % RING, y % 2, y % RING // 2, z % SIZES[3], core)
        pairs.append((source, int(np.ravel_multi_index(place, SIZES))))
    return lax.ppermute(value, TM + PTS, pairs)


def z_flip(bit):
    return lambda x, y, z, core: (x, y, z ^ bit, core)


def y_then_x(step):
    return lambda x, y, z, core: (x + step * core, y + step * (1 - core), z, core)


def x_then_y(step):
    return lambda x, y, z, core: (x + step * (1 - core), y + step * core, z, core)


def other_core(x, y, z, core):
    return x, y, z, 1 - core


def contract(left, right):
    return lax.dot_general(
        left, right, (((1,), (1,)), ((), ())), preferred_element_type=jnp.float32
    )


def polar_of(scaled_ref, pieces):
    occ = jnp.concatenate([p[:, :NOCC] for p in pieces], axis=0)
    vir = jnp.concatenate([p[:, NOCC:BANDS] for p in pieces], axis=0)
    return contract(scaled_ref[:, :NOCC], occ) * contract(scaled_ref[:, NOCC:], vir)


def at_frequency(weights_ref, polar, k):
    rows = polar.shape[0] // TAUS
    terms = [
        weights_ref[k * TAUS + t, :][None, :] * polar[t * rows : (t + 1) * rows] for t in range(TAUS)
    ]
    total = functools.reduce(jnp.add, terms)
    return total.astype(jnp.bfloat16)


def transform_kernel(weights_ref, scaled_ref, *refs):
    pieces, out_ref = refs[:-1], refs[-1]
    rows = scaled_ref.shape[0] // TAUS
    polar = polar_of(scaled_ref, pieces)
    for k in range(FREQS):
        out_ref[k * rows : (k + 1) * rows, :] = at_frequency(weights_ref, polar, k)


def first_kernel(weights_ref, decay_ref, rows_ref, *refs):
    pieces, (out_ref, scaled_ref) = refs[:-2], refs[-2:]
    rows = rows_ref.shape[0]
    for t in range(TAUS):
        scaled_ref[t * rows : (t + 1) * rows, :] = (
            rows_ref[...].astype(jnp.float32) * decay_ref[t, :][None, :]
        ).astype(jnp.bfloat16)
    transform_kernel(weights_ref, scaled_ref, *pieces, out_ref)


def screen_kernel(blocks_held, last_held, weights_ref, scaled_ref, *refs):
    blocks, refs = refs[:blocks_held], refs[blocks_held:]
    pieces, (out_ref, done_ref, sems) = refs[:-3], refs[-3:]
    rows = scaled_ref.shape[0] // TAUS
    polar = polar_of(scaled_ref, pieces[-last_held:])
    coulomb = jnp.concatenate([p[:, BANDS:] for p in pieces], axis=0)
    copies = []
    for step in range(FREQS // 2):
        here = slice(2 * step * rows, 2 * (step + 1) * rows)
        last = [at_frequency(weights_ref, polar, k) for k in (2 * step, 2 * step + 1)]
        transformed = jnp.concatenate(
            [b[here, :] for b in blocks] + [jnp.concatenate(last, axis=0)], axis=1
        )
        done_ref[here, :] = jnp.dot(
            transformed, coulomb, preferred_element_type=jnp.float32
        ).astype(jnp.bfloat16)
        copies.append(
            pltpu.make_async_copy(done_ref.at[here, :], out_ref.at[here, :], sems.at[step])
        )
        copies[-1].start()
    for copy in copies:
        copy.wait()


VMEM = pl.BlockSpec(memory_space=pltpu.VMEM)


def transform(weights, scaled, pieces):
    rows, width = scaled.shape[0], sum(p.shape[0] for p in pieces)
    return pl.pallas_call(
        transform_kernel,
        out_shape=jax.ShapeDtypeStruct((rows, width), jnp.bfloat16),
        in_specs=[VMEM] * (2 + len(pieces)),
        out_specs=VMEM,
        compiler_params=pltpu.CompilerParams(vmem_limit_bytes=12 * 2**20),
        cost_estimate=pl.CostEstimate(
            flops=2 * rows * width * BANDS, bytes_accessed=2**20, transcendentals=0
        ),
    )(weights, scaled, *pieces)


def transform_first(weights, decay, own, pieces):
    rows, width = TAUS * own.shape[0], sum(p.shape[0] for p in pieces)
    return pl.pallas_call(
        first_kernel,
        out_shape=[
            jax.ShapeDtypeStruct((rows, width), jnp.bfloat16),
            jax.ShapeDtypeStruct((rows, BANDS), jnp.bfloat16),
        ],
        in_specs=[VMEM] * (3 + len(pieces)),
        out_specs=[VMEM, VMEM],
        compiler_params=pltpu.CompilerParams(vmem_limit_bytes=12 * 2**20),
        cost_estimate=pl.CostEstimate(
            flops=2 * rows * width * BANDS, bytes_accessed=2**20, transcendentals=0
        ),
    )(weights, decay, own, *pieces)


def screen(weights, scaled, blocks, pieces, last):
    rows = scaled.shape[0]
    pieces = pieces + last
    return pl.pallas_call(
        functools.partial(screen_kernel, len(blocks), len(last)),
        out_shape=jax.ShapeDtypeStruct((rows, PANEL), jnp.bfloat16),
        in_specs=[VMEM] * (2 + len(blocks) + len(pieces)),
        out_specs=pl.BlockSpec(memory_space=pl.ANY),
        scratch_shapes=[
            pltpu.VMEM((rows, PANEL), jnp.bfloat16),
            pltpu.SemaphoreType.DMA((FREQS // 2,)),
        ],
        compiler_params=pltpu.CompilerParams(vmem_limit_bytes=12 * 2**20),
        cost_estimate=pl.CostEstimate(
            flops=2 * rows * PANEL * (PANEL + BANDS // 4), bytes_accessed=2**22, transcendentals=0
        ),
    )(weights, scaled, *blocks, *pieces)


def join_kernel(*refs):
    del refs


def joined(values, after):
    return pl.pallas_call(
        join_kernel,
        out_shape=[jax.ShapeDtypeStruct(v.shape, v.dtype) for v in values],
        in_specs=[pl.BlockSpec(memory_space=pl.ANY)] * (len(values) + 1),
        out_specs=[pl.BlockSpec(memory_space=pl.ANY)] * len(values),
        input_output_aliases={k: k for k in range(len(values))},
        compiler_params=pltpu.CompilerParams(vmem_limit_bytes=2**20),
    )(*values, after)


def shards(orbitals, panel_orbitals, band_gap, tau_points, quad_weight, frequencies, coulomb):
    held = jnp.pad(panel_orbitals, ((0, 0), (0, PANEL))) + jnp.pad(coulomb, ((0, 0), (BANDS, 0)))
    for bit in (4, 2, 1):
        held = jnp.concatenate([held, moved(held, z_flip(bit))], axis=0)
    rows = orbitals.shape[0] // lax.axis_size(TM)
    own = lax.dynamic_slice_in_dim(orbitals, lax.axis_index(TM) * rows, rows)
    decay = jnp.exp(-band_gap[None, :] * tau_points[:, None])
    weights = -quad_weight[None, :] * jnp.cos(frequencies[:, None] * tau_points[None, :])
    weights = jnp.broadcast_to(weights.reshape(FREQS * TAUS, 1), (FREQS * TAUS, COLS))

    held, weights, decay, own = lax.optimization_barrier((held, weights, decay, own))
    held = jnp.concatenate([held] + [moved(held, y_then_x(s)) for s in (1, -1, 2)], axis=0)
    others = [moved(held, x_then_y(s)) for s in (1, -1, 2)]
    pieces = [held, moved(held, other_core)]
    block, scaled = transform_first(weights, decay, own, pieces)
    blocks = [block]
    below, above, far = joined(others, blocks[0])
    for chunk in (below, above):
        both = [chunk, moved(chunk, other_core)]
        blocks.append(transform(weights, scaled, both))
        pieces += both
    last = [far, moved(far, other_core)]
    return screen(weights, scaled, blocks, pieces, last).reshape(FREQS, rows, PANEL)


def solution(mesh):
    split = Mesh(mesh.devices.reshape(SIZES), TM + PTS)
    everywhere = P(TM + PTS, None)
    placed = (P(PTS, None), everywhere, P(), P(), P(), P(), everywhere)
    return jax.shard_map(
        shards, mesh=split, in_specs=placed, out_specs=P(None, PTS + TM, None), check_vma=False
    )
```

time: 69.4 us -> 66.3 us (0.955)
  Pallas kernels: 13.4 us -> 11.2 us
  waiting for transfers between devices: 27 us -> 26.1 us
    pallas_call x4 -> x2, Pallas kernels: 9.68 us -> 3.6 us  [transform(): pl.pallas_call(transform_kernel, out_shape=jax.ShapeDtypeStruct((rows, wi...]
    pallas_call x1 -> x2, Pallas kernels: 3.67 us -> 7.55 us  [the longest x1 5.44 us: screen(): pl.pallas_call(functools.partial(screen_kernel, len(blocks), len(last)),...]
    convert_element_type x2 -> x0, other arithmetic: 2.24 us -> none  [the longest x1 1.14 us: shards(): lax.dynamic_slice_in_dim(orbitals, lax.axis_index(TM) * rows, rows)]
    dynamic_slice x0 -> x1, local copies, waits for them, and re-layouts: none -> 1.08 us  [shards(): own = lax.dynamic_slice_in_dim(orbitals, lax.axis_index(TM) * rows, rows)]
    ppermute x13, waiting for transfers between devices: 27 us -> 26.1 us  [moved(): return lax.ppermute(value, TM + PTS, pairs)]
    unnamed x10 -> x3, local copies, waits for them, and re-layouts: 0.82 us -> 0.04 us
    add x0 -> x1, other arithmetic: none -> 0.75 us  [shards(): jnp.pad(panel_orbitals, ((0, 0), (0, PANEL)))]
    concatenate x2 -> x1, local copies, waits for them, and re-layouts: 0.72 us -> 0.02 us  [shards(): jnp.concatenate([held] + [moved(held, y_then_x(s)) for s in (1, -1, 2)],...]
  transfers between devices with their start and end apart: 13 -> 13, of which waited for: 7 -> 7; matrix products, arithmetic and copies ran while one was open for 6% -> 6% of each run, Pallas kernels for 11% -> 9%
where the time goes in v3:
time: 66.3 us; the launch traced here: 66 us
  waiting for transfers between devices  26.1 us (39%)
  starting transfers between devices  23.4 us (35%)
  Pallas kernels  11.2 us (17%)
  other arithmetic  3.74 us (6%)
  local copies, waits for them, and re-layouts  1.29 us (2%)
    ppermute x13, waiting for transfers between devices, moved(): return lax.ppermute(value, TM + PTS, pairs)  26.1 us
    ppermute x13, starting transfers between devices, moved(): return lax.ppermute(value, TM + PTS, pairs)  23.4 us
    pallas_call x1, Pallas kernels, screen(): pl.pallas_call(functools.partial(screen_kernel, len(blocks), len(last)),...  5.44 us
    pallas_call x2, Pallas kernels, transform(): pl.pallas_call(transform_kernel, out_shape=jax.ShapeDtypeStruct((rows, wi...  3.6 us
    pallas_call x1, Pallas kernels, transform_first(): pl.pallas_call(first_kernel, out_shape=[jax.ShapeDtypeStruct((rows, width...  2.11 us
  transfers between devices with their start and end apart: 13, of which 7 were waited for; matrix products, arithmetic and copies ran while one was open for 6% of the time, Pallas kernels for 9%

profile of v3, /device:TPU:1, one launch (start us, length us, event | category | flops | bytes accessed | tf_op | source)
XLA Modules:
  0.0 66.0 jit_solution(9231630874373717581)
XLA Ops:
  0.0 0.7 %pad_add_fusion = bf16[4,3072]{1,0:T(4,128)(2,1)S(1)} fusion(bf16[4,1024]{1,0:T(4,128)(2,1)} %param.13, bf16[4,2048]{1,0:T(4,128)(2,1)} %param.8), kind=kLoop, calls=%fused_computation.4 | loop fusion | flops 49152 | bytes 49152 | tf_op jit(solution)/shard_map/add | solution.py:183
  0.8 7.8 %collective-permute-start = (bf16[4,3072]{1,0:T(4,128)(2,1)S(1)}, bf16[4,3072]{1,0:T(4,128)(2,1)S(1)}, u32[]{:S(2)}, u32[]{:S(2)}) collective-permute-start(bf16[4,3072]{1,0:T(4,128)(2,1)S(1)} %pad_add_fusion), channel_id=1, source_target_pairs={{0,8},{1,9},{2,10},{3,11},{4,12},{5,13},{6,14},{7,15},{8,0},{9,1},... | collective-permute-start | bytes 73736 | tf_op jit(solution)/shard_map/ppermute | solution.py:32
  8.6 0.7 %neg.9 = f32[2048]{0:T(1024)S(1)} negate(f32[2048]{0:T(1024)} %param.9) | non-fusion elementwise | flops 2048 | bytes 16384 | tf_op jit(solution)/shard_map/neg | solution.py:188
  9.3 0.7 %multiply_exponential_fusion.decay_ref = f32[8,2048]{1,0:T(8,128)S(1)} fusion(f32[8]{0:T(128)} %param.10, f32[2048]{0:T(1024)S(1)} %neg.9), kind=kLoop, calls=%fused_computation.2 | loop fusion | flops 16384 | bytes 73760 | tf_op jit(solution)/shard_map/exp | solution.py:188
  10.0 0.0 collective-permute-done
  10.1 1.3 %collective-permute-start.1 = (bf16[8,3072]{1,0:T(8,128)(2,1)S(1)}, bf16[8,3072]{1,0:T(8,128)(2,1)S(1)}, u32[]{:S(2)}, u32[]{:S(2)}) collective-permute-start(bf16[8,3072]{1,0:T(8,128)(2,1)S(1)} %pad_maximum_fusion.2), channel_id=1, source_target_pairs={{0,4},{1,5},{2,6},{3,7},{4,0},{5,1},{6,2},{7,3},{8,12},{9,13},{10,... | collective-permute-start | bytes 147464 | tf_op jit(solution)/shard_map/ppermute | solution.py:32
  11.4 1.1 %constant_dynamic-slice_fusion.rows_ref = bf16[128,2048]{1,0:T(8,128)(2,1)S(1)} fusion(bf16[1024,2048]{1,0:T(8,128)(2,1)} %param.7, s32[]{:T(128)S(6)} %select_n.3), kind=kLoop, calls=%fused_computation.10 | loop fusion | bytes 1048580 | tf_op jit(solution)/shard_map/dynamic_slice | solution.py:187
  12.5 0.7 %neg.8 = f32[8]{0:T(128)S(1)} negate(f32[8]{0:T(128)} %param.11) | non-fusion elementwise | flops 8 | bytes 64 | tf_op jit(solution)/shard_map/neg | solution.py:189
  13.1 0.9 %collective-permute-done.1 = bf16[8,3072]{1,0:T(8,128)(2,1)S(1)} collective-permute-done((bf16[8,3072]{1,0:T(8,128)(2,1)S(1)}, bf16[8,3072]{1,0:T(8,128)(2,1)S(1)}, u32[]{:S(2)}, u32[]{:S(2)}) %collective-permute-start.1) | collective-permute-done | bytes 49184 | tf_op jit(solution)/shard_map/ppermute | solution.py:32
  14.1 0.9 %collective-permute-start.2 = (bf16[16,3072]{1,0:T(8,128)(2,1)S(1)}, bf16[16,3072]{1,0:T(8,128)(2,1)S(1)}, u32[]{:S(2)}, u32[]{:S(2)}) collective-permute-start(bf16[16,3072]{1,0:T(8,128)(2,1)S(1)} %pad_maximum_fusion.1), channel_id=1, source_target_pairs={{0,2},{1,3},{2,0},{3,1},{4,6},{5,7},{6,4},{7,5},{8,10},{9,11},{10,... | collective-permute-start | bytes 294920 | tf_op jit(solution)/shard_map/ppermute | solution.py:32
  14.9 0.8 %cosine_multiply_fusion = f32[8,8]{1,0:T(8,128)S(1)} fusion(f32[8]{0:T(128)} %param.10, f32[8]{0:T(128)} %param.12, f32[8]{0:T(128)S(1)} %neg.8), kind=kLoop, calls=%fused_computation.9 | loop fusion | flops 128 | bytes 352 | tf_op jit(solution)/shard_map/mul | solution.py:189
  15.7 0.1 mul.57
  15.8 2.0 %collective-permute-done.2 = bf16[16,3072]{1,0:T(8,128)(2,1)S(1)} collective-permute-done((bf16[16,3072]{1,0:T(8,128)(2,1)S(1)}, bf16[16,3072]{1,0:T(8,128)(2,1)S(1)}, u32[]{:S(2)}, u32[]{:S(2)}) %collective-permute-start.2) | collective-permute-done | bytes 98336 | tf_op jit(solution)/shard_map/ppermute | solution.py:32
  17.8 0.1 broadcast_in_dim.2.weights_ref
  17.9 2.6 %collective-permute-start.5 = (bf16[32,3072]{1,0:T(8,128)(2,1)S(1)}, bf16[32,3072]{1,0:T(8,128)(2,1)S(1)}, u32[]{:S(2)}, u32[]{:S(2)}) collective-permute-start(bf16[32,3072]{1,0:T(8,128)(2,1)S(1)} %pad_maximum_fusion), channel_id=1, source_target_pairs={{0,16},{1,129},{2,18},{3,131},{4,20},{5,133},{6,22},{7,135},{8,24}... | collective-permute-start | bytes 589832 | tf_op jit(solution)/shard_map/ppermute | solution.py:32
  20.5 0.9 %collective-permute-start.4 = (bf16[32,3072]{1,0:T(8,128)(2,1)S(1)}, bf16[32,3072]{1,0:T(8,128)(2,1)S(1)}, u32[]{:S(2)}, u32[]{:S(2)}) collective-permute-start(bf16[32,3072]{1,0:T(8,128)(2,1)S(1)} %pad_maximum_fusion), channel_id=1, source_target_pairs={{0,48},{1,193},{2,50},{3,195},{4,52},{5,197},{6,54},{7,199},{8,56}... | collective-permute-start | bytes 589832 | tf_op jit(solution)/shard_map/ppermute | solution.py:32
  21.4 0.6 collective-permute-start.3
  22.0 5.4 %collective-permute-done.3 = bf16[32,3072]{1,0:T(8,128)(2,1)S(1)} collective-permute-done((bf16[32,3072]{1,0:T(8,128)(2,1)S(1)}, bf16[32,3072]{1,0:T(8,128)(2,1)S(1)}, u32[]{:S(2)}, u32[]{:S(2)}) %collective-permute-start.3) | collective-permute-done | bytes 196640 | tf_op jit(solution)/shard_map/ppermute | solution.py:32
  27.4 0.0 collective-permute-done.4
  27.4 0.0 collective-permute-done.5
  27.5 5.2 %collective-permute-start.6 = (bf16[128,3072]{1,0:T(8,128)(2,1)S(1)}, bf16[128,3072]{1,0:T(8,128)(2,1)S(1)}, u32[]{:S(2)}, u32[]{:S(2)}) collective-permute-start(bf16[128,3072]{1,0:T(8,128)(2,1)S(1)} %constant_dynamic-update-slice_fusion.refs_0_.refs_3_), channel_id=1, source_target_pairs={{0,1},{1,0},{2,3},{3,2},{4,5},{5,4},{6,7},{7,6},{8,9},{9,8},{10,11... | collective-permute-start | bytes 2359304 | tf_op jit(solution)/shard_map/ppermute | solution.py:32
  32.7 1.1 %collective-permute-start.9 = (bf16[128,3072]{1,0:T(8,128)(2,1)S(1)}, bf16[128,3072]{1,0:T(8,128)(2,1)S(1)}, u32[]{:S(2)}, u32[]{:S(2)}) collective-permute-start(bf16[128,3072]{1,0:T(8,128)(2,1)S(1)} %constant_dynamic-update-slice_fusion.refs_0_.refs_3_), channel_id=1, source_target_pairs={{0,128},{1,17},{2,130},{3,19},{4,132},{5,21},{6,134},{7,23},{8,136... | collective-permute-start | bytes 2359304 | tf_op jit(solution)/shard_map/ppermute | solution.py:32
  33.7 0.9 %collective-permute-start.8 = (bf16[128,3072]{1,0:T(8,128)(2,1)S(1)}, bf16[128,3072]{1,0:T(8,128)(2,1)S(1)}, u32[]{:S(2)}, u32[]{:S(2)}) collective-permute-start(bf16[128,3072]{1,0:T(8,128)(2,1)S(1)} %constant_dynamic-update-slice_fusion.refs_0_.refs_3_), channel_id=1, source_target_pairs={{0,192},{1,49},{2,194},{3,51},{4,196},{5,53},{6,198},{7,55},{8,200... | collective-permute-start | bytes 2359304 | tf_op jit(solution)/shard_map/ppermute | solution.py:32
  34.6 0.6 collective-permute-start.7
  35.2 0.0 collective-permute-done.6.refs_1_.refs_4_
  35.2 2.1 %shard_map.73 = (bf16[1024,256]{1,0:T(8,128)(2,1)S(1)}, bf16[1024,2048]{1,0:T(8,128)(2,1)S(1)}) custom-call(f32[64,256]{1,0:T(8,128)S(1)} %broadcast_in_dim.2.weights_ref, f32[8,2048]{1,0:T(8,128)S(1)} %multiply_exponential_fusion.decay_ref, bf16[128,2048]{1,0:T(8,128)(2,1)S(1)} %constant_dynamic-slice_fusion.rows_ref, ...), custom_call_target="tpu_custom_call" | custom-call | flops 1073741824 | bytes 1048576 | tf_op jit(solution)/shard_map/pallas_call | solution.py:133
  37.3 8.0 %collective-permute-done.9.refs_2_ = bf16[128,3072]{1,0:T(8,128)(2,1)S(1)} collective-permute-done((bf16[128,3072]{1,0:T(8,128)(2,1)S(1)}, bf16[128,3072]{1,0:T(8,128)(2,1)S(1)}, u32[]{:S(2)}, u32[]{:S(2)}) %collective-permute-start.9) | collective-permute-done | bytes 786464 | tf_op jit(solution)/shard_map/ppermute | solution.py:32
  45.4 6.9 %collective-permute-done.8.refs_1_ = bf16[128,3072]{1,0:T(8,128)(2,1)S(1)} collective-permute-done((bf16[128,3072]{1,0:T(8,128)(2,1)S(1)}, bf16[128,3072]{1,0:T(8,128)(2,1)S(1)}, u32[]{:S(2)}, u32[]{:S(2)}) %collective-permute-start.8) | collective-permute-done | bytes 786464 | tf_op jit(solution)/shard_map/ppermute | solution.py:32
  52.2 1.5 %collective-permute-done.7.refs_0_ = bf16[128,3072]{1,0:T(8,128)(2,1)S(1)} collective-permute-done((bf16[128,3072]{1,0:T(8,128)(2,1)S(1)}, bf16[128,3072]{1,0:T(8,128)(2,1)S(1)}, u32[]{:S(2)}, u32[]{:S(2)}) %collective-permute-start.7) | collective-permute-done | bytes 786464 | tf_op jit(solution)/shard_map/ppermute | solution.py:32
  53.7 1.1 %collective-permute-start.10 = (bf16[128,3072]{1,0:T(8,128)(2,1)S(1)}, bf16[128,3072]{1,0:T(8,128)(2,1)S(1)}, u32[]{:S(2)}, u32[]{:S(2)}) collective-permute-start(bf16[128,3072]{1,0:T(8,128)(2,1)S(1)} %get-tuple-element.20.refs_0_.refs_5_), channel_id=1, source_target_pairs={{0,1},{1,0},{2,3},{3,2},{4,5},{5,4},{6,7},{7,6},{8,9},{9,8},{10,11... | collective-permute-start | bytes 2359304 | tf_op jit(solution)/shard_map/ppermute | solution.py:32
  54.8 0.1 collective-permute-start.11
  54.9 0.4 collective-permute-start.12
  55.3 1.4 %collective-permute-done.10.refs_1_.refs_6_ = bf16[128,3072]{1,0:T(8,128)(2,1)S(1)} collective-permute-done((bf16[128,3072]{1,0:T(8,128)(2,1)S(1)}, bf16[128,3072]{1,0:T(8,128)(2,1)S(1)}, u32[]{:S(2)}, u32[]{:S(2)}) %collective-permute-start.10) | collective-permute-done | bytes 786464 | tf_op jit(solution)/shard_map/ppermute | solution.py:32
  56.7 1.8 %shard_map.75.refs_1_ = bf16[1024,256]{1,0:T(8,128)(2,1)S(1)} custom-call(f32[64,256]{1,0:T(8,128)S(1)} %broadcast_in_dim.2.weights_ref, bf16[1024,2048]{1,0:T(8,128)(2,1)S(1)} %get-tuple-element.18.scaled_ref, bf16[128,3072]{1,0:T(8,128)(2,1)S(1)} %get-tuple-element.20.refs_0_.refs_5_, bf16[128,3072]{1,0:T(8,128)(2,1)S(1)} %collective-permute-done.10.refs_1_.refs_6_), custom_call_target="tpu_custom_call" | custom-call | flops 1073741824 | bytes 1048576 | tf_op jit(solution)/shard_map/pallas_call | solution.py:119
  58.5 0.0 collective-permute-done.11.refs_1_.refs_8_
  58.6 1.8 %shard_map.76.refs_2_ = bf16[1024,256]{1,0:T(8,128)(2,1)S(1)} custom-call(f32[64,256]{1,0:T(8,128)S(1)} %broadcast_in_dim.2.weights_ref, bf16[1024,2048]{1,0:T(8,128)(2,1)S(1)} %get-tuple-element.18.scaled_ref, bf16[128,3072]{1,0:T(8,128)(2,1)S(1)} %get-tuple-element.21.refs_0_.refs_7_, bf16[128,3072]{1,0:T(8,128)(2,1)S(1)} %collective-permute-done.11.refs_1_.refs_8_), custom_call_target="tpu_custom_call" | custom-call | flops 1073741824 | bytes 1048576 | tf_op jit(solution)/shard_map/pallas_call | solution.py:119
  60.4 0.0 collective-permute-done.12.refs_10_
  60.4 5.4 %shard_map.77 = bf16[1024,1024]{1,0:T(8,128)(2,1)} custom-call(f32[64,256]{1,0:T(8,128)S(1)} %broadcast_in_dim.2.weights_ref, bf16[1024,2048]{1,0:T(8,128)(2,1)S(1)} %get-tuple-element.18.scaled_ref, bf16[1024,256]{1,0:T(8,128)(2,1)S(1)} %get-tuple-element.19.refs_3_.refs_0_, bf16[1024,256]{1,0:T(8,128)(2,1)S(1)} %shard_map.75.refs_1_, ...), custom_call_target="tpu_custom_call" | custom-call | flops 3221225472 | bytes 4194304 | tf_op jit(solution)/shard_map/pallas_call | solution.py:151
  (8 shorter events, 0.2 us)
Async XLA Ops:
  0.8 9.3 %collective-permute-start = (bf16[4,3072]{1,0:T(4,128)(2,1)S(1)}, bf16[4,3072]{1,0:T(4,128)(2,1)S(1)}, u32[]{:S(2)}, u32[]{:S(2)}) collective-permute-start(bf16[4,3072]{1,0:T(4,128)(2,1)S(1)} %pad_add_fusion), channel_id=1, source_target_pairs={{0,8},{1,9},{2,10},{3,11},{4,12},{5,13},{6,14},{7,15},{8,0},{9,1},... | collective-permute-start | bytes 73736 | tf_op jit(solution)/shard_map/ppermute | solution.py:32
  10.1 3.9 %collective-permute-start.1 = (bf16[8,3072]{1,0:T(8,128)(2,1)S(1)}, bf16[8,3072]{1,0:T(8,128)(2,1)S(1)}, u32[]{:S(2)}, u32[]{:S(2)}) collective-permute-start(bf16[8,3072]{1,0:T(8,128)(2,1)S(1)} %pad_maximum_fusion.2), channel_id=1, source_target_pairs={{0,4},{1,5},{2,6},{3,7},{4,0},{5,1},{6,2},{7,3},{8,12},{9,13},{10,... | collective-permute-start | bytes 147464 | tf_op jit(solution)/shard_map/ppermute | solution.py:32
  14.1 3.7 %collective-permute-start.2 = (bf16[16,3072]{1,0:T(8,128)(2,1)S(1)}, bf16[16,3072]{1,0:T(8,128)(2,1)S(1)}, u32[]{:S(2)}, u32[]{:S(2)}) collective-permute-start(bf16[16,3072]{1,0:T(8,128)(2,1)S(1)} %pad_maximum_fusion.1), channel_id=1, source_target_pairs={{0,2},{1,3},{2,0},{3,1},{4,6},{5,7},{6,4},{7,5},{8,10},{9,11},{10,... | collective-permute-start | bytes 294920 | tf_op jit(solution)/shard_map/ppermute | solution.py:32
  17.9 9.5 %collective-permute-start.5 = (bf16[32,3072]{1,0:T(8,128)(2,1)S(1)}, bf16[32,3072]{1,0:T(8,128)(2,1)S(1)}, u32[]{:S(2)}, u32[]{:S(2)}) collective-permute-start(bf16[32,3072]{1,0:T(8,128)(2,1)S(1)} %pad_maximum_fusion), channel_id=1, source_target_pairs={{0,16},{1,129},{2,18},{3,131},{4,20},{5,133},{6,22},{7,135},{8,24}... | collective-permute-start | bytes 589832 | tf_op jit(solution)/shard_map/ppermute | solution.py:32
  20.5 6.9 %collective-permute-start.4 = (bf16[32,3072]{1,0:T(8,128)(2,1)S(1)}, bf16[32,3072]{1,0:T(8,128)(2,1)S(1)}, u32[]{:S(2)}, u32[]{:S(2)}) collective-permute-start(bf16[32,3072]{1,0:T(8,128)(2,1)S(1)} %pad_maximum_fusion), channel_id=1, source_target_pairs={{0,48},{1,193},{2,50},{3,195},{4,52},{5,197},{6,54},{7,199},{8,56}... | collective-permute-start | bytes 589832 | tf_op jit(solution)/shard_map/ppermute | solution.py:32
  21.4 6.0 %collective-permute-start.3 = (bf16[32,3072]{1,0:T(8,128)(2,1)S(1)}, bf16[32,3072]{1,0:T(8,128)(2,1)S(1)}, u32[]{:S(2)}, u32[]{:S(2)}) collective-permute-start(bf16[32,3072]{1,0:T(8,128)(2,1)S(1)} %pad_maximum_fusion), channel_id=1, source_target_pairs={{0,32},{1,65},{2,34},{3,67},{4,36},{5,69},{6,38},{7,71},{8,40},{9,... | collective-permute-start | bytes 589832 | tf_op jit(solution)/shard_map/ppermute | solution.py:32
  27.5 7.7 %collective-permute-start.6 = (bf16[128,3072]{1,0:T(8,128)(2,1)S(1)}, bf16[128,3072]{1,0:T(8,128)(2,1)S(1)}, u32[]{:S(2)}, u32[]{:S(2)}) collective-permute-start(bf16[128,3072]{1,0:T(8,128)(2,1)S(1)} %constant_dynamic-update-slice_fusion.refs_0_.refs_3_), channel_id=1, source_target_pairs={{0,1},{1,0},{2,3},{3,2},{4,5},{5,4},{6,7},{7,6},{8,9},{9,8},{10,11... | collective-permute-start | bytes 2359304 | tf_op jit(solution)/shard_map/ppermute | solution.py:32
  32.7 12.7 %collective-permute-start.9 = (bf16[128,3072]{1,0:T(8,128)(2,1)S(1)}, bf16[128,3072]{1,0:T(8,128)(2,1)S(1)}, u32[]{:S(2)}, u32[]{:S(2)}) collective-permute-start(bf16[128,3072]{1,0:T(8,128)(2,1)S(1)} %constant_dynamic-update-slice_fusion.refs_0_.refs_3_), channel_id=1, source_target_pairs={{0,128},{1,17},{2,130},{3,19},{4,132},{5,21},{6,134},{7,23},{8,136... | collective-permute-start | bytes 2359304 | tf_op jit(solution)/shard_map/ppermute | solution.py:32
  33.7 18.5 %collective-permute-start.8 = (bf16[128,3072]{1,0:T(8,128)(2,1)S(1)}, bf16[128,3072]{1,0:T(8,128)(2,1)S(1)}, u32[]{:S(2)}, u32[]{:S(2)}) collective-permute-start(bf16[128,3072]{1,0:T(8,128)(2,1)S(1)} %constant_dynamic-update-slice_fusion.refs_0_.refs_3_), channel_id=1, source_target_pairs={{0,192},{1,49},{2,194},{3,51},{4,196},{5,53},{6,198},{7,55},{8,200... | collective-permute-start | bytes 2359304 | tf_op jit(solution)/shard_map/ppermute | solution.py:32
  34.6 19.1 %collective-permute-start.7 = (bf16[128,3072]{1,0:T(8,128)(2,1)S(1)}, bf16[128,3072]{1,0:T(8,128)(2,1)S(1)}, u32[]{:S(2)}, u32[]{:S(2)}) collective-permute-start(bf16[128,3072]{1,0:T(8,128)(2,1)S(1)} %constant_dynamic-update-slice_fusion.refs_0_.refs_3_), channel_id=1, source_target_pairs={{0,64},{1,33},{2,66},{3,35},{4,68},{5,37},{6,70},{7,39},{8,72},{9,... | collective-permute-start | bytes 2359304 | tf_op jit(solution)/shard_map/ppermute | solution.py:32
  53.7 3.0 %collective-permute-start.10 = (bf16[128,3072]{1,0:T(8,128)(2,1)S(1)}, bf16[128,3072]{1,0:T(8,128)(2,1)S(1)}, u32[]{:S(2)}, u32[]{:S(2)}) collective-permute-start(bf16[128,3072]{1,0:T(8,128)(2,1)S(1)} %get-tuple-element.20.refs_0_.refs_5_), channel_id=1, source_target_pairs={{0,1},{1,0},{2,3},{3,2},{4,5},{5,4},{6,7},{7,6},{8,9},{9,8},{10,11... | collective-permute-start | bytes 2359304 | tf_op jit(solution)/shard_map/ppermute | solution.py:32
  54.8 3.7 %collective-permute-start.11 = (bf16[128,3072]{1,0:T(8,128)(2,1)S(1)}, bf16[128,3072]{1,0:T(8,128)(2,1)S(1)}, u32[]{:S(2)}, u32[]{:S(2)}) collective-permute-start(bf16[128,3072]{1,0:T(8,128)(2,1)S(1)} %get-tuple-element.21.refs_0_.refs_7_), channel_id=1, source_target_pairs={{0,1},{1,0},{2,3},{3,2},{4,5},{5,4},{6,7},{7,6},{8,9},{9,8},{10,11... | collective-permute-start | bytes 2359304 | tf_op jit(solution)/shard_map/ppermute | solution.py:32
  54.9 5.5 %collective-permute-start.12 = (bf16[128,3072]{1,0:T(8,128)(2,1)S(1)}, bf16[128,3072]{1,0:T(8,128)(2,1)S(1)}, u32[]{:S(2)}, u32[]{:S(2)}) collective-permute-start(bf16[128,3072]{1,0:T(8,128)(2,1)S(1)} %get-tuple-element.22.refs_9_), channel_id=1, source_target_pairs={{0,1},{1,0},{2,3},{3,2},{4,5},{5,4},{6,7},{7,6},{8,9},{9,8},{10,11... | collective-permute-start | bytes 2359304 | tf_op jit(solution)/shard_map/ppermute | solution.py:32

commit v4 on v3

--- a/solution.py
+++ b/solution.py
@@ -20,14 +20,13 @@
 TM = ("x", "ylo")
 PTS = ("yhi", "z", "core")
 SIZES = (4, 2, 2, 8, 2)
-RING = 4
 
 
 def moved(value, target):
     pairs = []
     for source, (x, ylo, yhi, z, core) in enumerate(itertools.product(*map(range, SIZES))):
         x, y, z, core = target(x, 2 * yhi + ylo, z, core)
-        place = (x % RING, y % 2, y % RING // 2, z % SIZES[3], core)
+        place = (x, y % 2, y // 2, z, core)
         pairs.append((source, int(np.ravel_multi_index(place, SIZES))))
     return lax.ppermute(value, TM + PTS, pairs)
 
@@ -36,12 +35,12 @@
     return lambda x, y, z, core: (x, y, z ^ bit, core)
 
 
-def y_then_x(step):
-    return lambda x, y, z, core: (x + step * core, y + step * (1 - core), z, core)
-
-
-def x_then_y(step):
-    return lambda x, y, z, core: (x + step * (1 - core), y + step * core, z, core)
+def y_then_x(bits):
+    return lambda x, y, z, core: (x ^ bits * core, y ^ bits * (1 - core), z, core)
+
+
+def x_then_y(bits):
+    return lambda x, y, z, core: (x ^ bits * (1 - core), y ^ bits * core, z, core)
 
 
 def other_core(x, y, z, core):
@@ -164,21 +163,6 @@
     )(weights, scaled, *blocks, *pieces)
 
 
-def join_kernel(*refs):
-    del refs
-
-
-def joined(values, after):
-    return pl.pallas_call(
-        join_kernel,
-        out_shape=[jax.ShapeDtypeStruct(v.shape, v.dtype) for v in values],
-        in_specs=[pl.BlockSpec(memory_space=pl.ANY)] * (len(values) + 1),
-        out_specs=[pl.BlockSpec(memory_space=pl.ANY)] * len(values),
-        input_output_aliases={k: k for k in range(len(values))},
-        compiler_params=pltpu.CompilerParams(vmem_limit_bytes=2**20),
-    )(*values, after)
-
-
 def shards(orbitals, panel_orbitals, band_gap, tau_points, quad_weight, frequencies, coulomb):
     held = jnp.pad(panel_orbitals, ((0, 0), (0, PANEL))) + jnp.pad(coulomb, ((0, 0), (BANDS, 0)))
     for bit in (4, 2, 1):
@@ -190,17 +174,20 @@
     weights = jnp.broadcast_to(weights.reshape(FREQS * TAUS, 1), (FREQS * TAUS, COLS))
 
     held, weights, decay, own = lax.optimization_barrier((held, weights, decay, own))
-    held = jnp.concatenate([held] + [moved(held, y_then_x(s)) for s in (1, -1, 2)], axis=0)
-    others = [moved(held, x_then_y(s)) for s in (1, -1, 2)]
+    held = jnp.concatenate([held] + [moved(held, y_then_x(bits)) for bits in (1, 3, 2)], axis=0)
+    half = held.shape[0] // 2
+    near = [moved(held, x_then_y(bits)) for bits in (1, 3)]
     pieces = [held, moved(held, other_core)]
     block, scaled = transform_first(weights, decay, own, pieces)
     blocks = [block]
-    below, above, far = joined(others, blocks[0])
-    for chunk in (below, above):
+    near[0], near[1], blocks[0] = lax.optimization_barrier((near[0], near[1], blocks[0]))
+    far = [moved(near[1][:half], x_then_y(1)), moved(near[0][half:], x_then_y(3))]
+    for chunk in near:
         both = [chunk, moved(chunk, other_core)]
         blocks.append(transform(weights, scaled, both))
         pieces += both
-    last = [far, moved(far, other_core)]
+    far[0], far[1], blocks[1], blocks[2] = lax.optimization_barrier((*far, *blocks[1:]))
+    last = far + [moved(piece, other_core) for piece in far]
     return screen(weights, scaled, blocks, pieces, last).reshape(FREQS, rows, PANEL)
 
 

time: 66.3 us -> 64.1 us (0.967)
  waiting for transfers between devices: 26.1 us -> 21.8 us
  starting transfers between devices: 23.4 us -> 25.1 us
    ppermute x13 -> x15, waiting for transfers between devices: 26.1 us -> 21.8 us  [moved(): return lax.ppermute(value, TM + PTS, pairs)]
    ppermute x13 -> x15, starting transfers between devices: 23.4 us -> 25.1 us  [moved(): return lax.ppermute(value, TM + PTS, pairs)]
  transfers between devices with their start and end apart: 13 -> 15, of which waited for: 7 -> 11; matrix products, arithmetic and copies ran while one was open for 6% -> 6% of each run, Pallas kernels for 9% -> 9%
where the time goes in v4:
time: 64.1 us; the launch traced here: 63.8 us
  starting transfers between devices  25.1 us (39%)
  waiting for transfers between devices  21.8 us (34%)
  Pallas kernels  11.4 us (18%)
  other arithmetic  3.74 us (6%)
  local copies, waits for them, and re-layouts  1.34 us (2%)
    ppermute x15, starting transfers between devices, moved(): return lax.ppermute(value, TM + PTS, pairs)  25.1 us
    ppermute x15, waiting for transfers between devices, moved(): return lax.ppermute(value, TM + PTS, pairs)  21.8 us
    pallas_call x1, Pallas kernels, screen(): pl.pallas_call(functools.partial(screen_kernel, len(blocks), len(last)),...  5.63 us
    pallas_call x2, Pallas kernels, transform(): pl.pallas_call(transform_kernel, out_shape=jax.ShapeDtypeStruct((rows, wi...  3.68 us
    pallas_call x1, Pallas kernels, transform_first(): pl.pallas_call(first_kernel, out_shape=[jax.ShapeDtypeStruct((rows, width...  2.12 us
  transfers between devices with their start and end apart: 15, of which 11 were waited for; matrix products, arithmetic and copies ran while one was open for 6% of the time, Pallas kernels for 9%

profile of v4, /device:TPU:1, one launch (start us, length us, event | category | flops | bytes accessed | tf_op | source)
XLA Modules:
  0.0 63.8 jit_solution(5133273710454575270)
XLA Ops:
  0.0 0.7 %pad_add_fusion = bf16[4,3072]{1,0:T(4,128)(2,1)S(1)} fusion(bf16[4,1024]{1,0:T(4,128)(2,1)} %param.13, bf16[4,2048]{1,0:T(4,128)(2,1)} %param.8), kind=kLoop, calls=%fused_computation.4 | loop fusion | flops 49152 | bytes 49152 | tf_op jit(solution)/shard_map/add | solution.py:167
  0.8 7.8 %collective-permute-start = (bf16[4,3072]{1,0:T(4,128)(2,1)S(1)}, bf16[4,3072]{1,0:T(4,128)(2,1)S(1)}, u32[]{:S(2)}, u32[]{:S(2)}) collective-permute-start(bf16[4,3072]{1,0:T(4,128)(2,1)S(1)} %pad_add_fusion), channel_id=1, source_target_pairs={{0,8},{1,9},{2,10},{3,11},{4,12},{5,13},{6,14},{7,15},{8,0},{9,1},... | collective-permute-start | bytes 73736 | tf_op jit(solution)/shard_map/ppermute | solution.py:31
  8.6 0.7 %neg.9 = f32[2048]{0:T(1024)S(1)} negate(f32[2048]{0:T(1024)} %param.9) | non-fusion elementwise | flops 2048 | bytes 16384 | tf_op jit(solution)/shard_map/neg | solution.py:172
  9.3 0.7 %multiply_exponential_fusion.decay_ref = f32[8,2048]{1,0:T(8,128)S(1)} fusion(f32[8]{0:T(128)} %param.10, f32[2048]{0:T(1024)S(1)} %neg.9), kind=kLoop, calls=%fused_computation.2 | loop fusion | flops 16384 | bytes 73760 | tf_op jit(solution)/shard_map/exp | solution.py:172
  10.0 0.0 collective-permute-done
  10.1 1.3 %collective-permute-start.1 = (bf16[8,3072]{1,0:T(8,128)(2,1)S(1)}, bf16[8,3072]{1,0:T(8,128)(2,1)S(1)}, u32[]{:S(2)}, u32[]{:S(2)}) collective-permute-start(bf16[8,3072]{1,0:T(8,128)(2,1)S(1)} %pad_maximum_fusion.2), channel_id=1, source_target_pairs={{0,4},{1,5},{2,6},{3,7},{4,0},{5,1},{6,2},{7,3},{8,12},{9,13},{10,... | collective-permute-start | bytes 147464 | tf_op jit(solution)/shard_map/ppermute | solution.py:31
  11.4 1.1 %constant_dynamic-slice_fusion.rows_ref = bf16[128,2048]{1,0:T(8,128)(2,1)S(1)} fusion(bf16[1024,2048]{1,0:T(8,128)(2,1)} %param.7, s32[]{:T(128)S(6)} %select_n.3), kind=kLoop, calls=%fused_computation.10 | loop fusion | bytes 1048580 | tf_op jit(solution)/shard_map/dynamic_slice | solution.py:171
  12.5 0.7 %neg.8 = f32[8]{0:T(128)S(1)} negate(f32[8]{0:T(128)} %param.11) | non-fusion elementwise | flops 8 | bytes 64 | tf_op jit(solution)/shard_map/neg | solution.py:173
  13.1 0.9 %collective-permute-done.1 = bf16[8,3072]{1,0:T(8,128)(2,1)S(1)} collective-permute-done((bf16[8,3072]{1,0:T(8,128)(2,1)S(1)}, bf16[8,3072]{1,0:T(8,128)(2,1)S(1)}, u32[]{:S(2)}, u32[]{:S(2)}) %collective-permute-start.1) | collective-permute-done | bytes 49184 | tf_op jit(solution)/shard_map/ppermute | solution.py:31
  14.1 0.9 %collective-permute-start.2 = (bf16[16,3072]{1,0:T(8,128)(2,1)S(1)}, bf16[16,3072]{1,0:T(8,128)(2,1)S(1)}, u32[]{:S(2)}, u32[]{:S(2)}) collective-permute-start(bf16[16,3072]{1,0:T(8,128)(2,1)S(1)} %pad_maximum_fusion.1), channel_id=1, source_target_pairs={{0,2},{1,3},{2,0},{3,1},{4,6},{5,7},{6,4},{7,5},{8,10},{9,11},{10,... | collective-permute-start | bytes 294920 | tf_op jit(solution)/shard_map/ppermute | solution.py:31
  14.9 0.8 %cosine_multiply_fusion = f32[8,8]{1,0:T(8,128)S(1)} fusion(f32[8]{0:T(128)} %param.10, f32[8]{0:T(128)} %param.12, f32[8]{0:T(128)S(1)} %neg.8), kind=kLoop, calls=%fused_computation.9 | loop fusion | flops 128 | bytes 352 | tf_op jit(solution)/shard_map/mul | solution.py:173
  15.7 0.1 mul.57
  15.8 2.0 %collective-permute-done.2 = bf16[16,3072]{1,0:T(8,128)(2,1)S(1)} collective-permute-done((bf16[16,3072]{1,0:T(8,128)(2,1)S(1)}, bf16[16,3072]{1,0:T(8,128)(2,1)S(1)}, u32[]{:S(2)}, u32[]{:S(2)}) %collective-permute-start.2) | collective-permute-done | bytes 98336 | tf_op jit(solution)/shard_map/ppermute | solution.py:31
  17.8 0.1 broadcast_in_dim.2.weights_ref
  17.9 2.6 %collective-permute-start.5 = (bf16[32,3072]{1,0:T(8,128)(2,1)S(1)}, bf16[32,3072]{1,0:T(8,128)(2,1)S(1)}, u32[]{:S(2)}, u32[]{:S(2)}) collective-permute-start(bf16[32,3072]{1,0:T(8,128)(2,1)S(1)} %pad_maximum_fusion), channel_id=1, source_target_pairs={{0,16},{1,129},{2,18},{3,131},{4,20},{5,133},{6,22},{7,135},{8,24}... | collective-permute-start | bytes 589832 | tf_op jit(solution)/shard_map/ppermute | solution.py:31
  20.5 0.9 %collective-permute-start.4 = (bf16[32,3072]{1,0:T(8,128)(2,1)S(1)}, bf16[32,3072]{1,0:T(8,128)(2,1)S(1)}, u32[]{:S(2)}, u32[]{:S(2)}) collective-permute-start(bf16[32,3072]{1,0:T(8,128)(2,1)S(1)} %pad_maximum_fusion), channel_id=1, source_target_pairs={{0,48},{1,193},{2,50},{3,195},{4,52},{5,197},{6,54},{7,199},{8,56}... | collective-permute-start | bytes 589832 | tf_op jit(solution)/shard_map/ppermute | solution.py:31
  21.4 0.0 collective-permute-start.3
  21.4 4.6 %collective-permute-done.3 = bf16[32,3072]{1,0:T(8,128)(2,1)S(1)} collective-permute-done((bf16[32,3072]{1,0:T(8,128)(2,1)S(1)}, bf16[32,3072]{1,0:T(8,128)(2,1)S(1)}, u32[]{:S(2)}, u32[]{:S(2)}) %collective-permute-start.3) | collective-permute-done | bytes 196640 | tf_op jit(solution)/shard_map/ppermute | solution.py:31
  26.0 0.2 collective-permute-done.4
  26.3 0.0 collective-permute-done.5
  26.3 5.5 %collective-permute-start.6 = (bf16[128,3072]{1,0:T(8,128)(2,1)S(1)}, bf16[128,3072]{1,0:T(8,128)(2,1)S(1)}, u32[]{:S(2)}, u32[]{:S(2)}) collective-permute-start(bf16[128,3072]{1,0:T(8,128)(2,1)S(1)} %constant_dynamic-update-slice_fusion.refs_0_.refs_3_), channel_id=1, source_target_pairs={{0,1},{1,0},{2,3},{3,2},{4,5},{5,4},{6,7},{7,6},{8,9},{9,8},{10,11... | collective-permute-start | bytes 2359304 | tf_op jit(solution)/shard_map/ppermute | solution.py:31
  31.8 1.7 %collective-permute-start.8 = (bf16[128,3072]{1,0:T(8,128)(2,1)S(1)}, bf16[128,3072]{1,0:T(8,128)(2,1)S(1)}, u32[]{:S(2)}, u32[]{:S(2)}) collective-permute-start(bf16[128,3072]{1,0:T(8,128)(2,1)S(1)} %constant_dynamic-update-slice_fusion.refs_0_.refs_3_), channel_id=1, source_target_pairs={{0,192},{1,49},{2,194},{3,51},{4,196},{5,53},{6,198},{7,55},{8,200... | collective-permute-start | bytes 2359304 | tf_op jit(solution)/shard_map/ppermute | solution.py:31
  33.5 0.0 collective-permute-start.7
  33.5 0.2 collective-permute-done.6.refs_1_.refs_4_
  33.7 2.1 %shard_map.73 = (bf16[1024,256]{1,0:T(8,128)(2,1)S(1)}, bf16[1024,2048]{1,0:T(8,128)(2,1)S(1)}) custom-call(f32[64,256]{1,0:T(8,128)S(1)} %broadcast_in_dim.2.weights_ref, f32[8,2048]{1,0:T(8,128)S(1)} %multiply_exponential_fusion.decay_ref, bf16[128,2048]{1,0:T(8,128)(2,1)S(1)} %constant_dynamic-slice_fusion.rows_ref, ...), custom_call_target="tpu_custom_call" | custom-call | flops 1073741824 | bytes 1048576 | tf_op jit(solution)/shard_map/pallas_call | solution.py:132
  35.8 8.3 %collective-permute-done.8.refs_0_.refs_7_ = bf16[128,3072]{1,0:T(8,128)(2,1)S(1)} collective-permute-done((bf16[128,3072]{1,0:T(8,128)(2,1)S(1)}, bf16[128,3072]{1,0:T(8,128)(2,1)S(1)}, u32[]{:S(2)}, u32[]{:S(2)}) %collective-permute-start.8) | collective-permute-done | bytes 786464 | tf_op jit(solution)/shard_map/ppermute | solution.py:31
  44.1 0.5 collective-permute-done.7.refs_0_.refs_5_
  44.7 1.8 %collective-permute-start.12 = (bf16[128,3072]{1,0:T(8,128)(2,1)S(1)}, bf16[128,3072]{1,0:T(8,128)(2,1)S(1)}, u32[]{:S(2)}, u32[]{:S(2)}) collective-permute-start(bf16[128,3072]{1,0:T(8,128)(2,1)S(1)} %collective-permute-done.8.refs_0_.refs_7_), channel_id=1, source_target_pairs={{0,1},{1,0},{2,3},{3,2},{4,5},{5,4},{6,7},{7,6},{8,9},{9,8},{10,11... | collective-permute-start | bytes 2359304 | tf_op jit(solution)/shard_map/ppermute | solution.py:31
  46.4 0.0 collective-permute-start.11
  46.5 2.0 %collective-permute-start.10 = (bf16[64,3072]{1,0:T(8,128)(2,1)S(1)}, bf16[64,3072]{1,0:T(8,128)(2,1)S(1)}, u32[]{:S(2)}, u32[]{:S(2)}) collective-permute-start(bf16[64,3072]{1,0:T(8,128)(2,1)S(1)} %slice.7), channel_id=1, source_target_pairs={{0,192},{1,49},{2,194},{3,51},{4,196},{5,53},{6,198},{7,55},{8,200... | collective-permute-start | bytes 1179656 | tf_op jit(solution)/shard_map/ppermute | solution.py:31
  48.5 0.0 collective-permute-start.9
  48.5 0.0 collective-permute-done.12.refs_1_.refs_8_
  48.5 1.8 %shard_map.75.refs_2_ = bf16[1024,256]{1,0:T(8,128)(2,1)S(1)} custom-call(f32[64,256]{1,0:T(8,128)S(1)} %broadcast_in_dim.2.weights_ref, bf16[1024,2048]{1,0:T(8,128)(2,1)S(1)} %get-tuple-element.22.scaled_ref, bf16[128,3072]{1,0:T(8,128)(2,1)S(1)} %collective-permute-done.8.refs_0_.refs_7_, bf16[128,3072]{1,0:T(8,128)(2,1)S(1)} %collective-permute-done.12.refs_1_.refs_8_), custom_call_target="tpu_custom_call" | custom-call | flops 1073741824 | bytes 1048576 | tf_op jit(solution)/shard_map/pallas_call | solution.py:118
  50.4 0.0 collective-permute-done.11.refs_1_.refs_6_
  50.4 1.8 %shard_map.74.refs_1_ = bf16[1024,256]{1,0:T(8,128)(2,1)S(1)} custom-call(f32[64,256]{1,0:T(8,128)S(1)} %broadcast_in_dim.2.weights_ref, bf16[1024,2048]{1,0:T(8,128)(2,1)S(1)} %get-tuple-element.22.scaled_ref, bf16[128,3072]{1,0:T(8,128)(2,1)S(1)} %collective-permute-done.7.refs_0_.refs_5_, bf16[128,3072]{1,0:T(8,128)(2,1)S(1)} %collective-permute-done.11.refs_1_.refs_6_), custom_call_target="tpu_custom_call" | custom-call | flops 1073741824 | bytes 1048576 | tf_op jit(solution)/shard_map/pallas_call | solution.py:118
  52.2 2.5 %collective-permute-done.10.refs_10_ = bf16[64,3072]{1,0:T(8,128)(2,1)S(1)} collective-permute-done((bf16[64,3072]{1,0:T(8,128)(2,1)S(1)}, bf16[64,3072]{1,0:T(8,128)(2,1)S(1)}, u32[]{:S(2)}, u32[]{:S(2)}) %collective-permute-start.10) | collective-permute-done | bytes 393248 | tf_op jit(solution)/shard_map/ppermute | solution.py:31
  54.7 0.7 %collective-permute-done.9.refs_9_ = bf16[64,3072]{1,0:T(8,128)(2,1)S(1)} collective-permute-done((bf16[64,3072]{1,0:T(8,128)(2,1)S(1)}, bf16[64,3072]{1,0:T(8,128)(2,1)S(1)}, u32[]{:S(2)}, u32[]{:S(2)}) %collective-permute-start.9) | collective-permute-done | bytes 393248 | tf_op jit(solution)/shard_map/ppermute | solution.py:31
  55.4 0.6 collective-permute-start.13
  56.1 0.0 collective-permute-start.14
  56.1 1.3 %collective-permute-done.13.refs_11_ = bf16[64,3072]{1,0:T(8,128)(2,1)S(1)} collective-permute-done((bf16[64,3072]{1,0:T(8,128)(2,1)S(1)}, bf16[64,3072]{1,0:T(8,128)(2,1)S(1)}, u32[]{:S(2)}, u32[]{:S(2)}) %collective-permute-start.13) | collective-permute-done | bytes 393248 | tf_op jit(solution)/shard_map/ppermute | solution.py:31
  57.4 0.6 collective-permute-done.14.refs_12_
  58.0 5.6 %shard_map.76 = bf16[1024,1024]{1,0:T(8,128)(2,1)} custom-call(f32[64,256]{1,0:T(8,128)S(1)} %broadcast_in_dim.2.weights_ref, bf16[1024,2048]{1,0:T(8,128)(2,1)S(1)} %get-tuple-element.22.scaled_ref, bf16[1024,256]{1,0:T(8,128)(2,1)S(1)} %get-tuple-element.24.refs_0_, bf16[1024,256]{1,0:T(8,128)(2,1)S(1)} %shard_map.74.refs_1_, ...), custom_call_target="tpu_custom_call" | custom-call | flops 3221225472 | bytes 4194304 | tf_op jit(solution)/shard_map/pallas_call | solution.py:150
  (9 shorter events, 0.2 us)
Async XLA Ops:
  0.8 9.3 %collective-permute-start = (bf16[4,3072]{1,0:T(4,128)(2,1)S(1)}, bf16[4,3072]{1,0:T(4,128)(2,1)S(1)}, u32[]{:S(2)}, u32[]{:S(2)}) collective-permute-start(bf16[4,3072]{1,0:T(4,128)(2,1)S(1)} %pad_add_fusion), channel_id=1, source_target_pairs={{0,8},{1,9},{2,10},{3,11},{4,12},{5,13},{6,14},{7,15},{8,0},{9,1},... | collective-permute-start | bytes 73736 | tf_op jit(solution)/shard_map/ppermute | solution.py:31
  10.1 3.9 %collective-permute-start.1 = (bf16[8,3072]{1,0:T(8,128)(2,1)S(1)}, bf16[8,3072]{1,0:T(8,128)(2,1)S(1)}, u32[]{:S(2)}, u32[]{:S(2)}) collective-permute-start(bf16[8,3072]{1,0:T(8,128)(2,1)S(1)} %pad_maximum_fusion.2), channel_id=1, source_target_pairs={{0,4},{1,5},{2,6},{3,7},{4,0},{5,1},{6,2},{7,3},{8,12},{9,13},{10,... | collective-permute-start | bytes 147464 | tf_op jit(solution)/shard_map/ppermute | solution.py:31
  14.1 3.7 %collective-permute-start.2 = (bf16[16,3072]{1,0:T(8,128)(2,1)S(1)}, bf16[16,3072]{1,0:T(8,128)(2,1)S(1)}, u32[]{:S(2)}, u32[]{:S(2)}) collective-permute-start(bf16[16,3072]{1,0:T(8,128)(2,1)S(1)} %pad_maximum_fusion.1), channel_id=1, source_target_pairs={{0,2},{1,3},{2,0},{3,1},{4,6},{5,7},{6,4},{7,5},{8,10},{9,11},{10,... | collective-permute-start | bytes 294920 | tf_op jit(solution)/shard_map/ppermute | solution.py:31
  17.9 8.4 %collective-permute-start.5 = (bf16[32,3072]{1,0:T(8,128)(2,1)S(1)}, bf16[32,3072]{1,0:T(8,128)(2,1)S(1)}, u32[]{:S(2)}, u32[]{:S(2)}) collective-permute-start(bf16[32,3072]{1,0:T(8,128)(2,1)S(1)} %pad_maximum_fusion), channel_id=1, source_target_pairs={{0,16},{1,129},{2,18},{3,131},{4,20},{5,133},{6,22},{7,135},{8,24}... | collective-permute-start | bytes 589832 | tf_op jit(solution)/shard_map/ppermute | solution.py:31
  20.5 5.7 %collective-permute-start.4 = (bf16[32,3072]{1,0:T(8,128)(2,1)S(1)}, bf16[32,3072]{1,0:T(8,128)(2,1)S(1)}, u32[]{:S(2)}, u32[]{:S(2)}) collective-permute-start(bf16[32,3072]{1,0:T(8,128)(2,1)S(1)} %pad_maximum_fusion), channel_id=1, source_target_pairs={{0,48},{1,193},{2,50},{3,195},{4,52},{5,197},{6,54},{7,199},{8,56}... | collective-permute-start | bytes 589832 | tf_op jit(solution)/shard_map/ppermute | solution.py:31
  21.4 4.6 %collective-permute-start.3 = (bf16[32,3072]{1,0:T(8,128)(2,1)S(1)}, bf16[32,3072]{1,0:T(8,128)(2,1)S(1)}, u32[]{:S(2)}, u32[]{:S(2)}) collective-permute-start(bf16[32,3072]{1,0:T(8,128)(2,1)S(1)} %pad_maximum_fusion), channel_id=1, source_target_pairs={{0,32},{1,65},{2,34},{3,67},{4,36},{5,69},{6,38},{7,71},{8,40},{9,... | collective-permute-start | bytes 589832 | tf_op jit(solution)/shard_map/ppermute | solution.py:31
  26.3 7.4 %collective-permute-start.6 = (bf16[128,3072]{1,0:T(8,128)(2,1)S(1)}, bf16[128,3072]{1,0:T(8,128)(2,1)S(1)}, u32[]{:S(2)}, u32[]{:S(2)}) collective-permute-start(bf16[128,3072]{1,0:T(8,128)(2,1)S(1)} %constant_dynamic-update-slice_fusion.refs_0_.refs_3_), channel_id=1, source_target_pairs={{0,1},{1,0},{2,3},{3,2},{4,5},{5,4},{6,7},{7,6},{8,9},{9,8},{10,11... | collective-permute-start | bytes 2359304 | tf_op jit(solution)/shard_map/ppermute | solution.py:31
  31.8 12.3 %collective-permute-start.8 = (bf16[128,3072]{1,0:T(8,128)(2,1)S(1)}, bf16[128,3072]{1,0:T(8,128)(2,1)S(1)}, u32[]{:S(2)}, u32[]{:S(2)}) collective-permute-start(bf16[128,3072]{1,0:T(8,128)(2,1)S(1)} %constant_dynamic-update-slice_fusion.refs_0_.refs_3_), channel_id=1, source_target_pairs={{0,192},{1,49},{2,194},{3,51},{4,196},{5,53},{6,198},{7,55},{8,200... | collective-permute-start | bytes 2359304 | tf_op jit(solution)/shard_map/ppermute | solution.py:31
  33.5 11.1 %collective-permute-start.7 = (bf16[128,3072]{1,0:T(8,128)(2,1)S(1)}, bf16[128,3072]{1,0:T(8,128)(2,1)S(1)}, u32[]{:S(2)}, u32[]{:S(2)}) collective-permute-start(bf16[128,3072]{1,0:T(8,128)(2,1)S(1)} %constant_dynamic-update-slice_fusion.refs_0_.refs_3_), channel_id=1, source_target_pairs={{0,64},{1,33},{2,66},{3,35},{4,68},{5,37},{6,70},{7,39},{8,72},{9,... | collective-permute-start | bytes 2359304 | tf_op jit(solution)/shard_map/ppermute | solution.py:31
  44.7 3.9 %collective-permute-start.12 = (bf16[128,3072]{1,0:T(8,128)(2,1)S(1)}, bf16[128,3072]{1,0:T(8,128)(2,1)S(1)}, u32[]{:S(2)}, u32[]{:S(2)}) collective-permute-start(bf16[128,3072]{1,0:T(8,128)(2,1)S(1)} %collective-permute-done.8.refs_0_.refs_7_), channel_id=1, source_target_pairs={{0,1},{1,0},{2,3},{3,2},{4,5},{5,4},{6,7},{7,6},{8,9},{9,8},{10,11... | collective-permute-start | bytes 2359304 | tf_op jit(solution)/shard_map/ppermute | solution.py:31
  46.4 4.0 %collective-permute-start.11 = (bf16[128,3072]{1,0:T(8,128)(2,1)S(1)}, bf16[128,3072]{1,0:T(8,128)(2,1)S(1)}, u32[]{:S(2)}, u32[]{:S(2)}) collective-permute-start(bf16[128,3072]{1,0:T(8,128)(2,1)S(1)} %collective-permute-done.7.refs_0_.refs_5_), channel_id=1, source_target_pairs={{0,1},{1,0},{2,3},{3,2},{4,5},{5,4},{6,7},{7,6},{8,9},{9,8},{10,11... | collective-permute-start | bytes 2359304 | tf_op jit(solution)/shard_map/ppermute | solution.py:31
  46.5 8.2 %collective-permute-start.10 = (bf16[64,3072]{1,0:T(8,128)(2,1)S(1)}, bf16[64,3072]{1,0:T(8,128)(2,1)S(1)}, u32[]{:S(2)}, u32[]{:S(2)}) collective-permute-start(bf16[64,3072]{1,0:T(8,128)(2,1)S(1)} %slice.7), channel_id=1, source_target_pairs={{0,192},{1,49},{2,194},{3,51},{4,196},{5,53},{6,198},{7,55},{8,200... | collective-permute-start | bytes 1179656 | tf_op jit(solution)/shard_map/ppermute | solution.py:31
  48.5 6.9 %collective-permute-start.9 = (bf16[64,3072]{1,0:T(8,128)(2,1)S(1)}, bf16[64,3072]{1,0:T(8,128)(2,1)S(1)}, u32[]{:S(2)}, u32[]{:S(2)}) collective-permute-start(bf16[64,3072]{1,0:T(8,128)(2,1)S(1)} %slice.6), channel_id=1, source_target_pairs={{0,64},{1,33},{2,66},{3,35},{4,68},{5,37},{6,70},{7,39},{8,72},{9,... | collective-permute-start | bytes 1179656 | tf_op jit(solution)/shard_map/ppermute | solution.py:31
  55.4 2.0 %collective-permute-start.13 = (bf16[64,3072]{1,0:T(8,128)(2,1)S(1)}, bf16[64,3072]{1,0:T(8,128)(2,1)S(1)}, u32[]{:S(2)}, u32[]{:S(2)}) collective-permute-start(bf16[64,3072]{1,0:T(8,128)(2,1)S(1)} %collective-permute-done.9.refs_9_), channel_id=1, source_target_pairs={{0,1},{1,0},{2,3},{3,2},{4,5},{5,4},{6,7},{7,6},{8,9},{9,8},{10,11... | collective-permute-start | bytes 1179656 | tf_op jit(solution)/shard_map/ppermute | solution.py:31
  56.1 1.9 %collective-permute-start.14 = (bf16[64,3072]{1,0:T(8,128)(2,1)S(1)}, bf16[64,3072]{1,0:T(8,128)(2,1)S(1)}, u32[]{:S(2)}, u32[]{:S(2)}) collective-permute-start(bf16[64,3072]{1,0:T(8,128)(2,1)S(1)} %collective-permute-done.10.refs_10_), channel_id=1, source_target_pairs={{0,1},{1,0},{2,3},{3,2},{4,5},{5,4},{6,7},{7,6},{8,9},{9,8},{10,11... | collective-permute-start | bytes 1179656 | tf_op jit(solution)/shard_map/ppermute | solution.py:31

commit v5 on v4

--- a/solution.py
+++ b/solution.py
@@ -16,6 +16,7 @@
 FREQS = 8
 TAUS = 8
 COLS = 256
+STEPS = 4
 
 TM = ("x", "ylo")
 PTS = ("yhi", "z", "core")
@@ -86,22 +87,31 @@
     transform_kernel(weights_ref, scaled_ref, *pieces, out_ref)
 
 
-def screen_kernel(blocks_held, last_held, weights_ref, scaled_ref, *refs):
-    blocks, refs = refs[:blocks_held], refs[blocks_held:]
+def screen_kernel(*refs):
+    pieces, out_ref = refs[:-1], refs[-1]
+    held = len(pieces) // 3
+    blocks, pieces = pieces[:held], pieces[held:]
+    coulomb = jnp.concatenate([p[:, BANDS:] for p in pieces], axis=0)
+    step = out_ref.shape[0] // STEPS
+    for start in range(0, out_ref.shape[0], step):
+        here = slice(start, start + step)
+        transformed = jnp.concatenate([b[here, :] for b in blocks], axis=1)
+        out_ref[here, :] = jnp.dot(transformed, coulomb, preferred_element_type=jnp.float32)
+
+
+def last_kernel(weights_ref, scaled_ref, partial_ref, *refs):
     pieces, (out_ref, done_ref, sems) = refs[:-3], refs[-3:]
     rows = scaled_ref.shape[0] // TAUS
-    polar = polar_of(scaled_ref, pieces[-last_held:])
+    polar = polar_of(scaled_ref, pieces)
     coulomb = jnp.concatenate([p[:, BANDS:] for p in pieces], axis=0)
+    count = FREQS // STEPS
     copies = []
-    for step in range(FREQS // 2):
-        here = slice(2 * step * rows, 2 * (step + 1) * rows)
-        last = [at_frequency(weights_ref, polar, k) for k in (2 * step, 2 * step + 1)]
-        transformed = jnp.concatenate(
-            [b[here, :] for b in blocks] + [jnp.concatenate(last, axis=0)], axis=1
-        )
-        done_ref[here, :] = jnp.dot(
-            transformed, coulomb, preferred_element_type=jnp.float32
-        ).astype(jnp.bfloat16)
+    for step in range(STEPS):
+        here = slice(step * count * rows, (step + 1) * count * rows)
+        some = range(step * count, (step + 1) * count)
+        transformed = jnp.concatenate([at_frequency(weights_ref, polar, k) for k in some], axis=0)
+        product = jnp.dot(transformed, coulomb, preferred_element_type=jnp.float32)
+        done_ref[here, :] = (partial_ref[here, :] + product).astype(jnp.bfloat16)
         copies.append(
             pltpu.make_async_copy(done_ref.at[here, :], out_ref.at[here, :], sems.at[step])
         )
@@ -144,23 +154,36 @@
     )(weights, decay, own, *pieces)
 
 
-def screen(weights, scaled, blocks, pieces, last):
+def screen(blocks, pieces):
+    rows = blocks[0].shape[0]
+    return pl.pallas_call(
+        screen_kernel,
+        out_shape=jax.ShapeDtypeStruct((rows, PANEL), jnp.float32),
+        in_specs=[VMEM] * (len(blocks) + len(pieces)),
+        out_specs=VMEM,
+        compiler_params=pltpu.CompilerParams(vmem_limit_bytes=12 * 2**20),
+        cost_estimate=pl.CostEstimate(
+            flops=2 * rows * COLS * len(blocks) * PANEL, bytes_accessed=2**20, transcendentals=0
+        ),
+    )(*blocks, *pieces)
+
+
+def screen_last(weights, scaled, partial, pieces):
     rows = scaled.shape[0]
-    pieces = pieces + last
-    return pl.pallas_call(
-        functools.partial(screen_kernel, len(blocks), len(last)),
+    return pl.pallas_call(
+        last_kernel,
         out_shape=jax.ShapeDtypeStruct((rows, PANEL), jnp.bfloat16),
-        in_specs=[VMEM] * (2 + len(blocks) + len(pieces)),
+        in_specs=[VMEM] * (3 + len(pieces)),
         out_specs=pl.BlockSpec(memory_space=pl.ANY),
         scratch_shapes=[
             pltpu.VMEM((rows, PANEL), jnp.bfloat16),
-            pltpu.SemaphoreType.DMA((FREQS // 2,)),
+            pltpu.SemaphoreType.DMA((STEPS,)),
         ],
         compiler_params=pltpu.CompilerParams(vmem_limit_bytes=12 * 2**20),
         cost_estimate=pl.CostEstimate(
-            flops=2 * rows * PANEL * (PANEL + BANDS // 4), bytes_accessed=2**22, transcendentals=0
-        ),
-    )(weights, scaled, *blocks, *pieces)
+            flops=2 * rows * COLS * (PANEL + BANDS), bytes_accessed=2**22, transcendentals=0
+        ),
+    )(weights, scaled, partial, *pieces)
 
 
 def shards(orbitals, panel_orbitals, band_gap, tau_points, quad_weight, frequencies, coulomb):
@@ -174,7 +197,7 @@
     weights = jnp.broadcast_to(weights.reshape(FREQS * TAUS, 1), (FREQS * TAUS, COLS))
 
     held, weights, decay, own = lax.optimization_barrier((held, weights, decay, own))
-    held = jnp.concatenate([held] + [moved(held, y_then_x(bits)) for bits in (1, 3, 2)], axis=0)
+    held = jnp.concatenate([held] + [moved(held, y_then_x(bits)) for bits in (2, 1, 3)], axis=0)
     half = held.shape[0] // 2
     near = [moved(held, x_then_y(bits)) for bits in (1, 3)]
     pieces = [held, moved(held, other_core)]
@@ -186,9 +209,11 @@
         both = [chunk, moved(chunk, other_core)]
         blocks.append(transform(weights, scaled, both))
         pieces += both
-    far[0], far[1], blocks[1], blocks[2] = lax.optimization_barrier((*far, *blocks[1:]))
+    partial = screen(blocks, pieces)
+    far[0], partial = lax.optimization_barrier((far[0], partial))
+    far[1], partial = lax.optimization_barrier((far[1], partial))
     last = far + [moved(piece, other_core) for piece in far]
-    return screen(weights, scaled, blocks, pieces, last).reshape(FREQS, rows, PANEL)
+    return screen_last(weights, scaled, partial, last).reshape(FREQS, rows, PANEL)
 
 
 def solution(mesh):

time: 64.1 us -> 63.3 us (0.988)
  waiting for transfers between devices: 21.8 us -> 19.3 us
  starting transfers between devices: 25.1 us -> 26.7 us
    ppermute x15, waiting for transfers between devices: 21.8 us -> 19.3 us  [moved(): return lax.ppermute(value, TM + PTS, pairs)]
    ppermute x15, starting transfers between devices: 25.1 us -> 26.7 us  [moved(): return lax.ppermute(value, TM + PTS, pairs)]
    pallas_call x1 -> x2, Pallas kernels: 5.63 us -> 5.81 us  [the longest x1 4 us: screen_last(): pl.pallas_call(last_kernel, out_shape=jax.ShapeDtypeStruct((rows, PANEL),...]
  transfers between devices with their start and end apart: 15 -> 15, of which waited for: 11 -> 11; matrix products, arithmetic and copies ran while one was open for 6% -> 7% of each run, Pallas kernels for 9% -> 12%
where the time goes in v5:
time: 63.3 us; the launch traced here: 63 us
  starting transfers between devices  26.7 us (42%)
  waiting for transfers between devices  19.3 us (30%)
  Pallas kernels  11.6 us (18%)
  other arithmetic  3.74 us (6%)
  local copies, waits for them, and re-layouts  1.34 us (2%)
    ppermute x15, starting transfers between devices, moved(): return lax.ppermute(value, TM + PTS, pairs)  26.7 us
    ppermute x15, waiting for transfers between devices, moved(): return lax.ppermute(value, TM + PTS, pairs)  19.3 us
    pallas_call x1, Pallas kernels, screen_last(): pl.pallas_call(last_kernel, out_shape=jax.ShapeDtypeStruct((rows, PANEL),...  4 us
    pallas_call x2, Pallas kernels, transform(): pl.pallas_call(transform_kernel, out_shape=jax.ShapeDtypeStruct((rows, wi...  3.69 us
    pallas_call x1, Pallas kernels, transform_first(): pl.pallas_call(first_kernel, out_shape=[jax.ShapeDtypeStruct((rows, width...  2.12 us
    pallas_call x1, Pallas kernels, screen(): pl.pallas_call(screen_kernel, out_shape=jax.ShapeDtypeStruct((rows, PANEL...  1.81 us
  transfers between devices with their start and end apart: 15, of which 11 were waited for; matrix products, arithmetic and copies ran while one was open for 7% of the time, Pallas kernels for 12%

profile of v5, /device:TPU:1, one launch (start us, length us, event | category | flops | bytes accessed | tf_op | source)
XLA Modules:
  0.0 63.0 jit_solution(1964345061597075497)
XLA Ops:
  0.0 0.7 %pad_add_fusion = bf16[4,3072]{1,0:T(4,128)(2,1)S(1)} fusion(bf16[4,1024]{1,0:T(4,128)(2,1)} %param.13, bf16[4,2048]{1,0:T(4,128)(2,1)} %param.8), kind=kLoop, calls=%fused_computation.4 | loop fusion | flops 49152 | bytes 49152 | tf_op jit(solution)/shard_map/add | solution.py:190
  0.8 7.8 %collective-permute-start = (bf16[4,3072]{1,0:T(4,128)(2,1)S(1)}, bf16[4,3072]{1,0:T(4,128)(2,1)S(1)}, u32[]{:S(2)}, u32[]{:S(2)}) collective-permute-start(bf16[4,3072]{1,0:T(4,128)(2,1)S(1)} %pad_add_fusion), channel_id=1, source_target_pairs={{0,8},{1,9},{2,10},{3,11},{4,12},{5,13},{6,14},{7,15},{8,0},{9,1},... | collective-permute-start | bytes 73736 | tf_op jit(solution)/shard_map/ppermute | solution.py:32
  8.6 0.7 %neg.9 = f32[2048]{0:T(1024)S(1)} negate(f32[2048]{0:T(1024)} %param.9) | non-fusion elementwise | flops 2048 | bytes 16384 | tf_op jit(solution)/shard_map/neg | solution.py:195
  9.3 0.7 %multiply_exponential_fusion.decay_ref = f32[8,2048]{1,0:T(8,128)S(1)} fusion(f32[8]{0:T(128)} %param.10, f32[2048]{0:T(1024)S(1)} %neg.9), kind=kLoop, calls=%fused_computation.2 | loop fusion | flops 16384 | bytes 73760 | tf_op jit(solution)/shard_map/exp | solution.py:195
  10.0 0.0 collective-permute-done
  10.1 1.3 %collective-permute-start.1 = (bf16[8,3072]{1,0:T(8,128)(2,1)S(1)}, bf16[8,3072]{1,0:T(8,128)(2,1)S(1)}, u32[]{:S(2)}, u32[]{:S(2)}) collective-permute-start(bf16[8,3072]{1,0:T(8,128)(2,1)S(1)} %pad_maximum_fusion.2), channel_id=1, source_target_pairs={{0,4},{1,5},{2,6},{3,7},{4,0},{5,1},{6,2},{7,3},{8,12},{9,13},{10,... | collective-permute-start | bytes 147464 | tf_op jit(solution)/shard_map/ppermute | solution.py:32
  11.4 1.1 %constant_dynamic-slice_fusion.rows_ref = bf16[128,2048]{1,0:T(8,128)(2,1)S(1)} fusion(bf16[1024,2048]{1,0:T(8,128)(2,1)} %param.7, s32[]{:T(128)S(6)} %select_n.3), kind=kLoop, calls=%fused_computation.10 | loop fusion | bytes 1048580 | tf_op jit(solution)/shard_map/dynamic_slice | solution.py:194
  12.5 0.7 %neg.8 = f32[8]{0:T(128)S(1)} negate(f32[8]{0:T(128)} %param.11) | non-fusion elementwise | flops 8 | bytes 64 | tf_op jit(solution)/shard_map/neg | solution.py:196
  13.1 0.9 %collective-permute-done.1 = bf16[8,3072]{1,0:T(8,128)(2,1)S(1)} collective-permute-done((bf16[8,3072]{1,0:T(8,128)(2,1)S(1)}, bf16[8,3072]{1,0:T(8,128)(2,1)S(1)}, u32[]{:S(2)}, u32[]{:S(2)}) %collective-permute-start.1) | collective-permute-done | bytes 49184 | tf_op jit(solution)/shard_map/ppermute | solution.py:32
  14.1 0.9 %collective-permute-start.2 = (bf16[16,3072]{1,0:T(8,128)(2,1)S(1)}, bf16[16,3072]{1,0:T(8,128)(2,1)S(1)}, u32[]{:S(2)}, u32[]{:S(2)}) collective-permute-start(bf16[16,3072]{1,0:T(8,128)(2,1)S(1)} %pad_maximum_fusion.1), channel_id=1, source_target_pairs={{0,2},{1,3},{2,0},{3,1},{4,6},{5,7},{6,4},{7,5},{8,10},{9,11},{10,... | collective-permute-start | bytes 294920 | tf_op jit(solution)/shard_map/ppermute | solution.py:32
  14.9 0.8 %cosine_multiply_fusion = f32[8,8]{1,0:T(8,128)S(1)} fusion(f32[8]{0:T(128)} %param.10, f32[8]{0:T(128)} %param.12, f32[8]{0:T(128)S(1)} %neg.8), kind=kLoop, calls=%fused_computation.9 | loop fusion | flops 128 | bytes 352 | tf_op jit(solution)/shard_map/mul | solution.py:196
  15.7 0.1 mul.57
  15.8 2.0 %collective-permute-done.2 = bf16[16,3072]{1,0:T(8,128)(2,1)S(1)} collective-permute-done((bf16[16,3072]{1,0:T(8,128)(2,1)S(1)}, bf16[16,3072]{1,0:T(8,128)(2,1)S(1)}, u32[]{:S(2)}, u32[]{:S(2)}) %collective-permute-start.2) | collective-permute-done | bytes 98336 | tf_op jit(solution)/shard_map/ppermute | solution.py:32
  17.8 0.1 broadcast_in_dim.2.weights_ref
  17.9 2.6 %collective-permute-start.3 = (bf16[32,3072]{1,0:T(8,128)(2,1)S(1)}, bf16[32,3072]{1,0:T(8,128)(2,1)S(1)}, u32[]{:S(2)}, u32[]{:S(2)}) collective-permute-start(bf16[32,3072]{1,0:T(8,128)(2,1)S(1)} %pad_maximum_fusion), channel_id=1, source_target_pairs={{0,16},{1,129},{2,18},{3,131},{4,20},{5,133},{6,22},{7,135},{8,24}... | collective-permute-start | bytes 589832 | tf_op jit(solution)/shard_map/ppermute | solution.py:32
  20.5 0.3 collective-permute-start.4
  20.8 0.6 collective-permute-start.5
  21.4 2.6 %collective-permute-done.3 = bf16[32,3072]{1,0:T(8,128)(2,1)S(1)} collective-permute-done((bf16[32,3072]{1,0:T(8,128)(2,1)S(1)}, bf16[32,3072]{1,0:T(8,128)(2,1)S(1)}, u32[]{:S(2)}, u32[]{:S(2)}) %collective-permute-start.3) | collective-permute-done | bytes 196640 | tf_op jit(solution)/shard_map/ppermute | solution.py:32
  24.0 2.0 %collective-permute-done.4 = bf16[32,3072]{1,0:T(8,128)(2,1)S(1)} collective-permute-done((bf16[32,3072]{1,0:T(8,128)(2,1)S(1)}, bf16[32,3072]{1,0:T(8,128)(2,1)S(1)}, u32[]{:S(2)}, u32[]{:S(2)}) %collective-permute-start.4) | collective-permute-done | bytes 196640 | tf_op jit(solution)/shard_map/ppermute | solution.py:32
  26.0 0.6 collective-permute-done.5
  26.6 5.6 %collective-permute-start.6 = (bf16[128,3072]{1,0:T(8,128)(2,1)S(1)}, bf16[128,3072]{1,0:T(8,128)(2,1)S(1)}, u32[]{:S(2)}, u32[]{:S(2)}) collective-permute-start(bf16[128,3072]{1,0:T(8,128)(2,1)S(1)} %constant_dynamic-update-slice_fusion.refs_0_.refs_3_), channel_id=1, source_target_pairs={{0,1},{1,0},{2,3},{3,2},{4,5},{5,4},{6,7},{7,6},{8,9},{9,8},{10,11... | collective-permute-start | bytes 2359304 | tf_op jit(solution)/shard_map/ppermute | solution.py:32
  32.2 0.0 collective-permute-start.7
  32.2 1.7 %collective-permute-start.8 = (bf16[128,3072]{1,0:T(8,128)(2,1)S(1)}, bf16[128,3072]{1,0:T(8,128)(2,1)S(1)}, u32[]{:S(2)}, u32[]{:S(2)}) collective-permute-start(bf16[128,3072]{1,0:T(8,128)(2,1)S(1)} %constant_dynamic-update-slice_fusion.refs_0_.refs_3_), channel_id=1, source_target_pairs={{0,192},{1,49},{2,194},{3,51},{4,196},{5,53},{6,198},{7,55},{8,200... | collective-permute-start | bytes 2359304 | tf_op jit(solution)/shard_map/ppermute | solution.py:32
  33.9 0.2 collective-permute-done.6.refs_1_.refs_4_
  34.1 2.1 %shard_map.73 = (bf16[1024,256]{1,0:T(8,128)(2,1)S(1)}, bf16[1024,2048]{1,0:T(8,128)(2,1)S(1)}) custom-call(f32[64,256]{1,0:T(8,128)S(1)} %broadcast_in_dim.2.weights_ref, f32[8,2048]{1,0:T(8,128)S(1)} %multiply_exponential_fusion.decay_ref, bf16[128,2048]{1,0:T(8,128)(2,1)S(1)} %constant_dynamic-slice_fusion.rows_ref, ...), custom_call_target="tpu_custom_call" | custom-call | flops 1073741824 | bytes 1048576 | tf_op jit(solution)/shard_map/pallas_call | solution.py:142
  36.3 7.1 %collective-permute-done.7.refs_0_.refs_5_ = bf16[128,3072]{1,0:T(8,128)(2,1)S(1)} collective-permute-done((bf16[128,3072]{1,0:T(8,128)(2,1)S(1)}, bf16[128,3072]{1,0:T(8,128)(2,1)S(1)}, u32[]{:S(2)}, u32[]{:S(2)}) %collective-permute-start.7) | collective-permute-done | bytes 786464 | tf_op jit(solution)/shard_map/ppermute | solution.py:32
  43.4 1.2 %collective-permute-done.8.refs_0_.refs_7_ = bf16[128,3072]{1,0:T(8,128)(2,1)S(1)} collective-permute-done((bf16[128,3072]{1,0:T(8,128)(2,1)S(1)}, bf16[128,3072]{1,0:T(8,128)(2,1)S(1)}, u32[]{:S(2)}, u32[]{:S(2)}) %collective-permute-start.8) | collective-permute-done | bytes 786464 | tf_op jit(solution)/shard_map/ppermute | solution.py:32
  44.6 2.4 %collective-permute-start.12 = (bf16[128,3072]{1,0:T(8,128)(2,1)S(1)}, bf16[128,3072]{1,0:T(8,128)(2,1)S(1)}, u32[]{:S(2)}, u32[]{:S(2)}) collective-permute-start(bf16[128,3072]{1,0:T(8,128)(2,1)S(1)} %collective-permute-done.8.refs_0_.refs_7_), channel_id=1, source_target_pairs={{0,1},{1,0},{2,3},{3,2},{4,5},{5,4},{6,7},{7,6},{8,9},{9,8},{10,11... | collective-permute-start | bytes 2359304 | tf_op jit(solution)/shard_map/ppermute | solution.py:32
  47.0 0.0 collective-permute-start.11
  47.0 0.1 collective-permute-start.10
  47.2 2.0 %collective-permute-start.9 = (bf16[64,3072]{1,0:T(8,128)(2,1)S(1)}, bf16[64,3072]{1,0:T(8,128)(2,1)S(1)}, u32[]{:S(2)}, u32[]{:S(2)}) collective-permute-start(bf16[64,3072]{1,0:T(8,128)(2,1)S(1)} %slice.6), channel_id=1, source_target_pairs={{0,192},{1,49},{2,194},{3,51},{4,196},{5,53},{6,198},{7,55},{8,200... | collective-permute-start | bytes 1179656 | tf_op jit(solution)/shard_map/ppermute | solution.py:32
  49.2 0.0 collective-permute-done.12.refs_1_.refs_8_
  49.2 1.8 %shard_map.75.refs_2_ = bf16[1024,256]{1,0:T(8,128)(2,1)S(1)} custom-call(f32[64,256]{1,0:T(8,128)S(1)} %broadcast_in_dim.2.weights_ref, bf16[1024,2048]{1,0:T(8,128)(2,1)S(1)} %get-tuple-element.22.scaled_ref, bf16[128,3072]{1,0:T(8,128)(2,1)S(1)} %collective-permute-done.8.refs_0_.refs_7_, bf16[128,3072]{1,0:T(8,128)(2,1)S(1)} %collective-permute-done.12.refs_1_.refs_8_), custom_call_target="tpu_custom_call" | custom-call | flops 1073741824 | bytes 1048576 | tf_op jit(solution)/shard_map/pallas_call | solution.py:128
  51.0 0.0 collective-permute-done.11.refs_1_.refs_6_
  51.0 1.8 %shard_map.74.refs_1_ = bf16[1024,256]{1,0:T(8,128)(2,1)S(1)} custom-call(f32[64,256]{1,0:T(8,128)S(1)} %broadcast_in_dim.2.weights_ref, bf16[1024,2048]{1,0:T(8,128)(2,1)S(1)} %get-tuple-element.22.scaled_ref, bf16[128,3072]{1,0:T(8,128)(2,1)S(1)} %collective-permute-done.7.refs_0_.refs_5_, bf16[128,3072]{1,0:T(8,128)(2,1)S(1)} %collective-permute-done.11.refs_1_.refs_6_), custom_call_target="tpu_custom_call" | custom-call | flops 1073741824 | bytes 1048576 | tf_op jit(solution)/shard_map/pallas_call | solution.py:128
  52.9 1.8 %shard_map.76.partial_ref = f32[1024,1024]{1,0:T(8,128)S(1)} custom-call(bf16[1024,256]{1,0:T(8,128)(2,1)S(1)} %get-tuple-element.26.refs_0_, bf16[1024,256]{1,0:T(8,128)(2,1)S(1)} %shard_map.74.refs_1_, bf16[1024,256]{1,0:T(8,128)(2,1)S(1)} %shard_map.75.refs_2_, bf16[128,3072]{1,0:T(8,128)(2,1)S(1)} %constant_dynamic-update-slice_fusion.refs_0_.refs_3_, ...), custom_call_target="tpu_custom_call" | custom-call | flops 1610612736 | bytes 1048576 | tf_op jit(solution)/shard_map/pallas_call | solution.py:159
  54.7 0.0 collective-permute-done.10.refs_0_
  54.7 0.9 %collective-permute-done.9.refs_1_ = bf16[64,3072]{1,0:T(8,128)(2,1)S(1)} collective-permute-done((bf16[64,3072]{1,0:T(8,128)(2,1)S(1)}, bf16[64,3072]{1,0:T(8,128)(2,1)S(1)}, u32[]{:S(2)}, u32[]{:S(2)}) %collective-permute-start.9) | collective-permute-done | bytes 393248 | tf_op jit(solution)/shard_map/ppermute | solution.py:32
  55.6 1.4 %collective-permute-start.14 = (bf16[64,3072]{1,0:T(8,128)(2,1)S(1)}, bf16[64,3072]{1,0:T(8,128)(2,1)S(1)}, u32[]{:S(2)}, u32[]{:S(2)}) collective-permute-start(bf16[64,3072]{1,0:T(8,128)(2,1)S(1)} %collective-permute-done.9.refs_1_), channel_id=1, source_target_pairs={{0,1},{1,0},{2,3},{3,2},{4,5},{5,4},{6,7},{7,6},{8,9},{9,8},{10,11... | collective-permute-start | bytes 1179656 | tf_op jit(solution)/shard_map/ppermute | solution.py:32
  56.9 0.0 collective-permute-start.13
  57.0 1.3 %collective-permute-done.14.refs_3_ = bf16[64,3072]{1,0:T(8,128)(2,1)S(1)} collective-permute-done((bf16[64,3072]{1,0:T(8,128)(2,1)S(1)}, bf16[64,3072]{1,0:T(8,128)(2,1)S(1)}, u32[]{:S(2)}, u32[]{:S(2)}) %collective-permute-start.14) | collective-permute-done | bytes 393248 | tf_op jit(solution)/shard_map/ppermute | solution.py:32
  58.3 0.6 collective-permute-done.13.refs_2_
  58.9 4.0 %shard_map.77 = bf16[1024,1024]{1,0:T(8,128)(2,1)} custom-call(f32[64,256]{1,0:T(8,128)S(1)} %broadcast_in_dim.2.weights_ref, bf16[1024,2048]{1,0:T(8,128)(2,1)S(1)} %get-tuple-element.22.scaled_ref, f32[1024,1024]{1,0:T(8,128)S(1)} %shard_map.76.partial_ref, bf16[64,3072]{1,0:T(8,128)(2,1)S(1)} %collective-permute-done.10.refs_0_, ...), custom_call_target="tpu_custom_call" | custom-call | flops 1610612736 | bytes 4194304 | tf_op jit(solution)/shard_map/pallas_call | solution.py:173
  (9 shorter events, 0.2 us)
Async XLA Ops:
  0.8 9.3 %collective-permute-start = (bf16[4,3072]{1,0:T(4,128)(2,1)S(1)}, bf16[4,3072]{1,0:T(4,128)(2,1)S(1)}, u32[]{:S(2)}, u32[]{:S(2)}) collective-permute-start(bf16[4,3072]{1,0:T(4,128)(2,1)S(1)} %pad_add_fusion), channel_id=1, source_target_pairs={{0,8},{1,9},{2,10},{3,11},{4,12},{5,13},{6,14},{7,15},{8,0},{9,1},... | collective-permute-start | bytes 73736 | tf_op jit(solution)/shard_map/ppermute | solution.py:32
  10.1 3.9 %collective-permute-start.1 = (bf16[8,3072]{1,0:T(8,128)(2,1)S(1)}, bf16[8,3072]{1,0:T(8,128)(2,1)S(1)}, u32[]{:S(2)}, u32[]{:S(2)}) collective-permute-start(bf16[8,3072]{1,0:T(8,128)(2,1)S(1)} %pad_maximum_fusion.2), channel_id=1, source_target_pairs={{0,4},{1,5},{2,6},{3,7},{4,0},{5,1},{6,2},{7,3},{8,12},{9,13},{10,... | collective-permute-start | bytes 147464 | tf_op jit(solution)/shard_map/ppermute | solution.py:32
  14.1 3.7 %collective-permute-start.2 = (bf16[16,3072]{1,0:T(8,128)(2,1)S(1)}, bf16[16,3072]{1,0:T(8,128)(2,1)S(1)}, u32[]{:S(2)}, u32[]{:S(2)}) collective-permute-start(bf16[16,3072]{1,0:T(8,128)(2,1)S(1)} %pad_maximum_fusion.1), channel_id=1, source_target_pairs={{0,2},{1,3},{2,0},{3,1},{4,6},{5,7},{6,4},{7,5},{8,10},{9,11},{10,... | collective-permute-start | bytes 294920 | tf_op jit(solution)/shard_map/ppermute | solution.py:32
  17.9 6.1 %collective-permute-start.3 = (bf16[32,3072]{1,0:T(8,128)(2,1)S(1)}, bf16[32,3072]{1,0:T(8,128)(2,1)S(1)}, u32[]{:S(2)}, u32[]{:S(2)}) collective-permute-start(bf16[32,3072]{1,0:T(8,128)(2,1)S(1)} %pad_maximum_fusion), channel_id=1, source_target_pairs={{0,16},{1,129},{2,18},{3,131},{4,20},{5,133},{6,22},{7,135},{8,24}... | collective-permute-start | bytes 589832 | tf_op jit(solution)/shard_map/ppermute | solution.py:32
  20.5 5.5 %collective-permute-start.4 = (bf16[32,3072]{1,0:T(8,128)(2,1)S(1)}, bf16[32,3072]{1,0:T(8,128)(2,1)S(1)}, u32[]{:S(2)}, u32[]{:S(2)}) collective-permute-start(bf16[32,3072]{1,0:T(8,128)(2,1)S(1)} %pad_maximum_fusion), channel_id=1, source_target_pairs={{0,32},{1,65},{2,34},{3,67},{4,36},{5,69},{6,38},{7,71},{8,40},{9,... | collective-permute-start | bytes 589832 | tf_op jit(solution)/shard_map/ppermute | solution.py:32
  20.8 5.7 %collective-permute-start.5 = (bf16[32,3072]{1,0:T(8,128)(2,1)S(1)}, bf16[32,3072]{1,0:T(8,128)(2,1)S(1)}, u32[]{:S(2)}, u32[]{:S(2)}) collective-permute-start(bf16[32,3072]{1,0:T(8,128)(2,1)S(1)} %pad_maximum_fusion), channel_id=1, source_target_pairs={{0,48},{1,193},{2,50},{3,195},{4,52},{5,197},{6,54},{7,199},{8,56}... | collective-permute-start | bytes 589832 | tf_op jit(solution)/shard_map/ppermute | solution.py:32
  26.6 7.6 %collective-permute-start.6 = (bf16[128,3072]{1,0:T(8,128)(2,1)S(1)}, bf16[128,3072]{1,0:T(8,128)(2,1)S(1)}, u32[]{:S(2)}, u32[]{:S(2)}) collective-permute-start(bf16[128,3072]{1,0:T(8,128)(2,1)S(1)} %constant_dynamic-update-slice_fusion.refs_0_.refs_3_), channel_id=1, source_target_pairs={{0,1},{1,0},{2,3},{3,2},{4,5},{5,4},{6,7},{7,6},{8,9},{9,8},{10,11... | collective-permute-start | bytes 2359304 | tf_op jit(solution)/shard_map/ppermute | solution.py:32
  32.2 11.1 %collective-permute-start.7 = (bf16[128,3072]{1,0:T(8,128)(2,1)S(1)}, bf16[128,3072]{1,0:T(8,128)(2,1)S(1)}, u32[]{:S(2)}, u32[]{:S(2)}) collective-permute-start(bf16[128,3072]{1,0:T(8,128)(2,1)S(1)} %constant_dynamic-update-slice_fusion.refs_0_.refs_3_), channel_id=1, source_target_pairs={{0,64},{1,33},{2,66},{3,35},{4,68},{5,37},{6,70},{7,39},{8,72},{9,... | collective-permute-start | bytes 2359304 | tf_op jit(solution)/shard_map/ppermute | solution.py:32
  32.2 12.3 %collective-permute-start.8 = (bf16[128,3072]{1,0:T(8,128)(2,1)S(1)}, bf16[128,3072]{1,0:T(8,128)(2,1)S(1)}, u32[]{:S(2)}, u32[]{:S(2)}) collective-permute-start(bf16[128,3072]{1,0:T(8,128)(2,1)S(1)} %constant_dynamic-update-slice_fusion.refs_0_.refs_3_), channel_id=1, source_target_pairs={{0,192},{1,49},{2,194},{3,51},{4,196},{5,53},{6,198},{7,55},{8,200... | collective-permute-start | bytes 2359304 | tf_op jit(solution)/shard_map/ppermute | solution.py:32
  44.6 4.6 %collective-permute-start.12 = (bf16[128,3072]{1,0:T(8,128)(2,1)S(1)}, bf16[128,3072]{1,0:T(8,128)(2,1)S(1)}, u32[]{:S(2)}, u32[]{:S(2)}) collective-permute-start(bf16[128,3072]{1,0:T(8,128)(2,1)S(1)} %collective-permute-done.8.refs_0_.refs_7_), channel_id=1, source_target_pairs={{0,1},{1,0},{2,3},{3,2},{4,5},{5,4},{6,7},{7,6},{8,9},{9,8},{10,11... | collective-permute-start | bytes 2359304 | tf_op jit(solution)/shard_map/ppermute | solution.py:32
  47.0 4.0 %collective-permute-start.11 = (bf16[128,3072]{1,0:T(8,128)(2,1)S(1)}, bf16[128,3072]{1,0:T(8,128)(2,1)S(1)}, u32[]{:S(2)}, u32[]{:S(2)}) collective-permute-start(bf16[128,3072]{1,0:T(8,128)(2,1)S(1)} %collective-permute-done.7.refs_0_.refs_5_), channel_id=1, source_target_pairs={{0,1},{1,0},{2,3},{3,2},{4,5},{5,4},{6,7},{7,6},{8,9},{9,8},{10,11... | collective-permute-start | bytes 2359304 | tf_op jit(solution)/shard_map/ppermute | solution.py:32
  47.0 7.6 %collective-permute-start.10 = (bf16[64,3072]{1,0:T(8,128)(2,1)S(1)}, bf16[64,3072]{1,0:T(8,128)(2,1)S(1)}, u32[]{:S(2)}, u32[]{:S(2)}) collective-permute-start(bf16[64,3072]{1,0:T(8,128)(2,1)S(1)} %slice.7), channel_id=1, source_target_pairs={{0,64},{1,33},{2,66},{3,35},{4,68},{5,37},{6,70},{7,39},{8,72},{9,... | collective-permute-start | bytes 1179656 | tf_op jit(solution)/shard_map/ppermute | solution.py:32
  47.2 8.4 %collective-permute-start.9 = (bf16[64,3072]{1,0:T(8,128)(2,1)S(1)}, bf16[64,3072]{1,0:T(8,128)(2,1)S(1)}, u32[]{:S(2)}, u32[]{:S(2)}) collective-permute-start(bf16[64,3072]{1,0:T(8,128)(2,1)S(1)} %slice.6), channel_id=1, source_target_pairs={{0,192},{1,49},{2,194},{3,51},{4,196},{5,53},{6,198},{7,55},{8,200... | collective-permute-start | bytes 1179656 | tf_op jit(solution)/shard_map/ppermute | solution.py:32
  55.6 2.7 %collective-permute-start.14 = (bf16[64,3072]{1,0:T(8,128)(2,1)S(1)}, bf16[64,3072]{1,0:T(8,128)(2,1)S(1)}, u32[]{:S(2)}, u32[]{:S(2)}) collective-permute-start(bf16[64,3072]{1,0:T(8,128)(2,1)S(1)} %collective-permute-done.9.refs_1_), channel_id=1, source_target_pairs={{0,1},{1,0},{2,3},{3,2},{4,5},{5,4},{6,7},{7,6},{8,9},{9,8},{10,11... | collective-permute-start | bytes 1179656 | tf_op jit(solution)/shard_map/ppermute | solution.py:32
  56.9 1.9 %collective-permute-start.13 = (bf16[64,3072]{1,0:T(8,128)(2,1)S(1)}, bf16[64,3072]{1,0:T(8,128)(2,1)S(1)}, u32[]{:S(2)}, u32[]{:S(2)}) collective-permute-start(bf16[64,3072]{1,0:T(8,128)(2,1)S(1)} %collective-permute-done.10.refs_0_), channel_id=1, source_target_pairs={{0,1},{1,0},{2,3},{3,2},{4,5},{5,4},{6,7},{7,6},{8,9},{9,8},{10,11... | collective-permute-start | bytes 1179656 | tf_op jit(solution)/shard_map/ppermute | solution.py:32

commit v6 on v5

--- a/solution.py
+++ b/solution.py
@@ -188,8 +188,8 @@
 
 def shards(orbitals, panel_orbitals, band_gap, tau_points, quad_weight, frequencies, coulomb):
     held = jnp.pad(panel_orbitals, ((0, 0), (0, PANEL))) + jnp.pad(coulomb, ((0, 0), (BANDS, 0)))
-    for bit in (4, 2, 1):
-        held = jnp.concatenate([held, moved(held, z_flip(bit))], axis=0)
+    for group in ((1,), (4, 6, 2)):
+        held = jnp.concatenate([held] + [moved(held, z_flip(bits)) for bits in group], axis=0)
     rows = orbitals.shape[0] // lax.axis_size(TM)
     own = lax.dynamic_slice_in_dim(orbitals, lax.axis_index(TM) * rows, rows)
     decay = jnp.exp(-band_gap[None, :] * tau_points[:, None])

time: 63.3 us -> 62.7 us (level)
  starting transfers between devices: 26.7 us -> 25.3 us
  waiting for transfers between devices: 19.3 us -> 20 us
    ppermute x15 -> x16, starting transfers between devices: 26.7 us -> 25.3 us  [moved(): return lax.ppermute(value, TM + PTS, pairs)]
    ppermute x15 -> x16, waiting for transfers between devices: 19.3 us -> 20 us  [moved(): return lax.ppermute(value, TM + PTS, pairs)]
  transfers between devices with their start and end apart: 15 -> 16, of which waited for: 11 -> 11; matrix products, arithmetic and copies ran while one was open for 7% -> 7% of each run, Pallas kernels for 12% -> 12%
where the time goes in v6:
time: 62.7 us; the launch traced here: 62.3 us
  starting transfers between devices  25.3 us (40%)
  waiting for transfers between devices  20 us (32%)
  Pallas kernels  11.7 us (19%)
  other arithmetic  3.65 us (6%)
  local copies, waits for them, and re-layouts  1.39 us (2%)
    ppermute x16, starting transfers between devices, moved(): return lax.ppermute(value, TM + PTS, pairs)  25.3 us
    ppermute x16, waiting for transfers between devices, moved(): return lax.ppermute(value, TM + PTS, pairs)  20 us
    pallas_call x1, Pallas kernels, screen_last(): pl.pallas_call(last_kernel, out_shape=jax.ShapeDtypeStruct((rows, PANEL),...  4.01 us
    pallas_call x2, Pallas kernels, transform(): pl.pallas_call(transform_kernel, out_shape=jax.ShapeDtypeStruct((rows, wi...  3.68 us
    pallas_call x1, Pallas kernels, transform_first(): pl.pallas_call(first_kernel, out_shape=[jax.ShapeDtypeStruct((rows, width...  2.19 us
    pallas_call x1, Pallas kernels, screen(): pl.pallas_call(screen_kernel, out_shape=jax.ShapeDtypeStruct((rows, PANEL...  1.81 us
  transfers between devices with their start and end apart: 16, of which 11 were waited for; matrix products, arithmetic and copies ran while one was open for 7% of the time, Pallas kernels for 12%

profile of v6, /device:TPU:1, one launch (start us, length us, event | category | flops | bytes accessed | tf_op | source)
XLA Modules:
  0.0 62.3 jit_solution(12037750750614192585)
XLA Ops:
  0.0 0.7 %pad_add_fusion = bf16[4,3072]{1,0:T(4,128)(2,1)S(1)} fusion(bf16[4,1024]{1,0:T(4,128)(2,1)} %param.13, bf16[4,2048]{1,0:T(4,128)(2,1)} %param.8), kind=kLoop, calls=%fused_computation.2 | loop fusion | flops 49152 | bytes 49152 | tf_op jit(solution)/shard_map/add | solution.py:190
  0.8 2.6 %collective-permute-start = (bf16[4,3072]{1,0:T(4,128)(2,1)S(1)}, bf16[4,3072]{1,0:T(4,128)(2,1)S(1)}, u32[]{:S(2)}, u32[]{:S(2)}) collective-permute-start(bf16[4,3072]{1,0:T(4,128)(2,1)S(1)} %pad_add_fusion), channel_id=1, source_target_pairs={{0,2},{1,3},{2,0},{3,1},{4,6},{5,7},{6,4},{7,5},{8,10},{9,11},{10,... | collective-permute-start | bytes 73736 | tf_op jit(solution)/shard_map/ppermute | solution.py:32
  3.3 0.7 %neg.9 = f32[2048]{0:T(1024)S(1)} negate(f32[2048]{0:T(1024)} %param.9) | non-fusion elementwise | flops 2048 | bytes 16384 | tf_op jit(solution)/shard_map/neg | solution.py:195
  4.0 0.7 %multiply_exponential_fusion.decay_ref = f32[8,2048]{1,0:T(8,128)S(1)} fusion(f32[8]{0:T(128)} %param.10, f32[2048]{0:T(1024)S(1)} %neg.9), kind=kLoop, calls=%fused_computation | loop fusion | flops 16384 | bytes 73760 | tf_op jit(solution)/shard_map/exp | solution.py:195
  4.7 1.1 %constant_dynamic-slice_fusion.rows_ref = bf16[128,2048]{1,0:T(8,128)(2,1)S(1)} fusion(bf16[1024,2048]{1,0:T(8,128)(2,1)} %param.7, s32[]{:T(128)S(6)} %select_n.3), kind=kLoop, calls=%fused_computation.8 | loop fusion | bytes 1048580 | tf_op jit(solution)/shard_map/dynamic_slice | solution.py:194
  5.8 0.7 %neg.8 = f32[8]{0:T(128)S(1)} negate(f32[8]{0:T(128)} %param.11) | non-fusion elementwise | flops 8 | bytes 64 | tf_op jit(solution)/shard_map/neg | solution.py:196
  6.5 0.0 collective-permute-done
  6.5 6.1 %collective-permute-start.1 = (bf16[8,3072]{1,0:T(8,128)(2,1)S(1)}, bf16[8,3072]{1,0:T(8,128)(2,1)S(1)}, u32[]{:S(2)}, u32[]{:S(2)}) collective-permute-start(bf16[8,3072]{1,0:T(8,128)(2,1)S(1)} %pad_maximum_fusion), channel_id=1, source_target_pairs={{0,8},{1,9},{2,10},{3,11},{4,12},{5,13},{6,14},{7,15},{8,0},{9,1},... | collective-permute-start | bytes 147464 | tf_op jit(solution)/shard_map/ppermute | solution.py:32
  12.6 0.3 collective-permute-start.2
  12.9 0.9 %collective-permute-start.3 = (bf16[8,3072]{1,0:T(8,128)(2,1)S(1)}, bf16[8,3072]{1,0:T(8,128)(2,1)S(1)}, u32[]{:S(2)}, u32[]{:S(2)}) collective-permute-start(bf16[8,3072]{1,0:T(8,128)(2,1)S(1)} %pad_maximum_fusion), channel_id=1, source_target_pairs={{0,4},{1,5},{2,6},{3,7},{4,0},{5,1},{6,2},{7,3},{8,12},{9,13},{10,... | collective-permute-start | bytes 147464 | tf_op jit(solution)/shard_map/ppermute | solution.py:32
  13.8 0.8 %cosine_multiply_fusion = f32[8,8]{1,0:T(8,128)S(1)} fusion(f32[8]{0:T(128)} %param.10, f32[8]{0:T(128)} %param.12, f32[8]{0:T(128)S(1)} %neg.8), kind=kLoop, calls=%fused_computation.7 | loop fusion | flops 128 | bytes 352 | tf_op jit(solution)/shard_map/mul | solution.py:196
  14.6 0.1 mul.57
  14.7 0.0 collective-permute-done.1
  14.7 3.1 %collective-permute-done.2 = bf16[8,3072]{1,0:T(8,128)(2,1)S(1)} collective-permute-done((bf16[8,3072]{1,0:T(8,128)(2,1)S(1)}, bf16[8,3072]{1,0:T(8,128)(2,1)S(1)}, u32[]{:S(2)}, u32[]{:S(2)}) %collective-permute-start.2) | collective-permute-done | bytes 49184 | tf_op jit(solution)/shard_map/ppermute | solution.py:32
  17.8 0.3 collective-permute-done.3
  18.1 0.1 broadcast_in_dim.2.weights_ref
  18.1 2.5 %collective-permute-start.4 = (bf16[32,3072]{1,0:T(8,128)(2,1)S(1)}, bf16[32,3072]{1,0:T(8,128)(2,1)S(1)}, u32[]{:S(2)}, u32[]{:S(2)}) collective-permute-start(bf16[32,3072]{1,0:T(8,128)(2,1)S(1)} %concatenate.11), channel_id=1, source_target_pairs={{0,16},{1,129},{2,18},{3,131},{4,20},{5,133},{6,22},{7,135},{8,24}... | collective-permute-start | bytes 589832 | tf_op jit(solution)/shard_map/ppermute | solution.py:32
  20.7 0.3 collective-permute-start.5
  21.0 0.6 collective-permute-start.6
  21.6 2.6 %collective-permute-done.4 = bf16[32,3072]{1,0:T(8,128)(2,1)S(1)} collective-permute-done((bf16[32,3072]{1,0:T(8,128)(2,1)S(1)}, bf16[32,3072]{1,0:T(8,128)(2,1)S(1)}, u32[]{:S(2)}, u32[]{:S(2)}) %collective-permute-start.4) | collective-permute-done | bytes 196640 | tf_op jit(solution)/shard_map/ppermute | solution.py:32
  24.2 2.2 %collective-permute-done.5 = bf16[32,3072]{1,0:T(8,128)(2,1)S(1)} collective-permute-done((bf16[32,3072]{1,0:T(8,128)(2,1)S(1)}, bf16[32,3072]{1,0:T(8,128)(2,1)S(1)}, u32[]{:S(2)}, u32[]{:S(2)}) %collective-permute-start.5) | collective-permute-done | bytes 196640 | tf_op jit(solution)/shard_map/ppermute | solution.py:32
  26.5 0.6 collective-permute-done.6
  27.1 4.5 %collective-permute-start.7 = (bf16[128,3072]{1,0:T(8,128)(2,1)S(1)}, bf16[128,3072]{1,0:T(8,128)(2,1)S(1)}, u32[]{:S(2)}, u32[]{:S(2)}) collective-permute-start(bf16[128,3072]{1,0:T(8,128)(2,1)S(1)} %constant_dynamic-update-slice_fusion.refs_0_.refs_3_), channel_id=1, source_target_pairs={{0,1},{1,0},{2,3},{3,2},{4,5},{5,4},{6,7},{7,6},{8,9},{9,8},{10,11... | collective-permute-start | bytes 2359304 | tf_op jit(solution)/shard_map/ppermute | solution.py:32
  31.5 0.0 collective-permute-start.8
  31.5 1.7 %collective-permute-start.9 = (bf16[128,3072]{1,0:T(8,128)(2,1)S(1)}, bf16[128,3072]{1,0:T(8,128)(2,1)S(1)}, u32[]{:S(2)}, u32[]{:S(2)}) collective-permute-start(bf16[128,3072]{1,0:T(8,128)(2,1)S(1)} %constant_dynamic-update-slice_fusion.refs_0_.refs_3_), channel_id=1, source_target_pairs={{0,192},{1,49},{2,194},{3,51},{4,196},{5,53},{6,198},{7,55},{8,200... | collective-permute-start | bytes 2359304 | tf_op jit(solution)/shard_map/ppermute | solution.py:32
  33.3 0.2 collective-permute-done.7.refs_1_.refs_4_
  33.5 2.2 %shard_map.73 = (bf16[1024,256]{1,0:T(8,128)(2,1)S(1)}, bf16[1024,2048]{1,0:T(8,128)(2,1)S(1)}) custom-call(f32[64,256]{1,0:T(8,128)S(1)} %broadcast_in_dim.2.weights_ref, f32[8,2048]{1,0:T(8,128)S(1)} %multiply_exponential_fusion.decay_ref, bf16[128,2048]{1,0:T(8,128)(2,1)S(1)} %constant_dynamic-slice_fusion.rows_ref, ...), custom_call_target="tpu_custom_call" | custom-call | flops 1073741824 | bytes 1048576 | tf_op jit(solution)/shard_map/pallas_call | solution.py:142
  35.6 7.0 %collective-permute-done.8.refs_0_.refs_5_ = bf16[128,3072]{1,0:T(8,128)(2,1)S(1)} collective-permute-done((bf16[128,3072]{1,0:T(8,128)(2,1)S(1)}, bf16[128,3072]{1,0:T(8,128)(2,1)S(1)}, u32[]{:S(2)}, u32[]{:S(2)}) %collective-permute-start.8) | collective-permute-done | bytes 786464 | tf_op jit(solution)/shard_map/ppermute | solution.py:32
  42.7 1.2 %collective-permute-done.9.refs_0_.refs_7_ = bf16[128,3072]{1,0:T(8,128)(2,1)S(1)} collective-permute-done((bf16[128,3072]{1,0:T(8,128)(2,1)S(1)}, bf16[128,3072]{1,0:T(8,128)(2,1)S(1)}, u32[]{:S(2)}, u32[]{:S(2)}) %collective-permute-start.9) | collective-permute-done | bytes 786464 | tf_op jit(solution)/shard_map/ppermute | solution.py:32
  43.9 2.4 %collective-permute-start.13 = (bf16[128,3072]{1,0:T(8,128)(2,1)S(1)}, bf16[128,3072]{1,0:T(8,128)(2,1)S(1)}, u32[]{:S(2)}, u32[]{:S(2)}) collective-permute-start(bf16[128,3072]{1,0:T(8,128)(2,1)S(1)} %collective-permute-done.9.refs_0_.refs_7_), channel_id=1, source_target_pairs={{0,1},{1,0},{2,3},{3,2},{4,5},{5,4},{6,7},{7,6},{8,9},{9,8},{10,11... | collective-permute-start | bytes 2359304 | tf_op jit(solution)/shard_map/ppermute | solution.py:32
  46.3 0.0 collective-permute-start.12
  46.4 0.1 collective-permute-start.11
  46.5 2.0 %collective-permute-start.10 = (bf16[64,3072]{1,0:T(8,128)(2,1)S(1)}, bf16[64,3072]{1,0:T(8,128)(2,1)S(1)}, u32[]{:S(2)}, u32[]{:S(2)}) collective-permute-start(bf16[64,3072]{1,0:T(8,128)(2,1)S(1)} %slice.6), channel_id=1, source_target_pairs={{0,192},{1,49},{2,194},{3,51},{4,196},{5,53},{6,198},{7,55},{8,200... | collective-permute-start | bytes 1179656 | tf_op jit(solution)/shard_map/ppermute | solution.py:32
  48.5 0.0 collective-permute-done.13.refs_1_.refs_8_
  48.5 1.8 %shard_map.75.refs_2_ = bf16[1024,256]{1,0:T(8,128)(2,1)S(1)} custom-call(f32[64,256]{1,0:T(8,128)S(1)} %broadcast_in_dim.2.weights_ref, bf16[1024,2048]{1,0:T(8,128)(2,1)S(1)} %get-tuple-element.22.scaled_ref, bf16[128,3072]{1,0:T(8,128)(2,1)S(1)} %collective-permute-done.9.refs_0_.refs_7_, bf16[128,3072]{1,0:T(8,128)(2,1)S(1)} %collective-permute-done.13.refs_1_.refs_8_), custom_call_target="tpu_custom_call" | custom-call | flops 1073741824 | bytes 1048576 | tf_op jit(solution)/shard_map/pallas_call | solution.py:128
  50.3 0.0 collective-permute-done.12.refs_1_.refs_6_
  50.3 1.8 %shard_map.74.refs_1_ = bf16[1024,256]{1,0:T(8,128)(2,1)S(1)} custom-call(f32[64,256]{1,0:T(8,128)S(1)} %broadcast_in_dim.2.weights_ref, bf16[1024,2048]{1,0:T(8,128)(2,1)S(1)} %get-tuple-element.22.scaled_ref, bf16[128,3072]{1,0:T(8,128)(2,1)S(1)} %collective-permute-done.8.refs_0_.refs_5_, bf16[128,3072]{1,0:T(8,128)(2,1)S(1)} %collective-permute-done.12.refs_1_.refs_6_), custom_call_target="tpu_custom_call" | custom-call | flops 1073741824 | bytes 1048576 | tf_op jit(solution)/shard_map/pallas_call | solution.py:128
  52.2 1.8 %shard_map.76.partial_ref = f32[1024,1024]{1,0:T(8,128)S(1)} custom-call(bf16[1024,256]{1,0:T(8,128)(2,1)S(1)} %get-tuple-element.26.refs_0_, bf16[1024,256]{1,0:T(8,128)(2,1)S(1)} %shard_map.74.refs_1_, bf16[1024,256]{1,0:T(8,128)(2,1)S(1)} %shard_map.75.refs_2_, bf16[128,3072]{1,0:T(8,128)(2,1)S(1)} %constant_dynamic-update-slice_fusion.refs_0_.refs_3_, ...), custom_call_target="tpu_custom_call" | custom-call | flops 1610612736 | bytes 1048576 | tf_op jit(solution)/shard_map/pallas_call | solution.py:159
  54.0 0.0 collective-permute-done.11.refs_0_
  54.0 0.9 %collective-permute-done.10.refs_1_ = bf16[64,3072]{1,0:T(8,128)(2,1)S(1)} collective-permute-done((bf16[64,3072]{1,0:T(8,128)(2,1)S(1)}, bf16[64,3072]{1,0:T(8,128)(2,1)S(1)}, u32[]{:S(2)}, u32[]{:S(2)}) %collective-permute-start.10) | collective-permute-done | bytes 393248 | tf_op jit(solution)/shard_map/ppermute | solution.py:32
  54.9 1.4 %collective-permute-start.15 = (bf16[64,3072]{1,0:T(8,128)(2,1)S(1)}, bf16[64,3072]{1,0:T(8,128)(2,1)S(1)}, u32[]{:S(2)}, u32[]{:S(2)}) collective-permute-start(bf16[64,3072]{1,0:T(8,128)(2,1)S(1)} %collective-permute-done.10.refs_1_), channel_id=1, source_target_pairs={{0,1},{1,0},{2,3},{3,2},{4,5},{5,4},{6,7},{7,6},{8,9},{9,8},{10,11... | collective-permute-start | bytes 1179656 | tf_op jit(solution)/shard_map/ppermute | solution.py:32
  56.3 0.0 collective-permute-start.14
  56.3 1.3 %collective-permute-done.15.refs_3_ = bf16[64,3072]{1,0:T(8,128)(2,1)S(1)} collective-permute-done((bf16[64,3072]{1,0:T(8,128)(2,1)S(1)}, bf16[64,3072]{1,0:T(8,128)(2,1)S(1)}, u32[]{:S(2)}, u32[]{:S(2)}) %collective-permute-start.15) | collective-permute-done | bytes 393248 | tf_op jit(solution)/shard_map/ppermute | solution.py:32
  57.6 0.6 collective-permute-done.14.refs_2_
  58.2 4.0 %shard_map.77 = bf16[1024,1024]{1,0:T(8,128)(2,1)} custom-call(f32[64,256]{1,0:T(8,128)S(1)} %broadcast_in_dim.2.weights_ref, bf16[1024,2048]{1,0:T(8,128)(2,1)S(1)} %get-tuple-element.22.scaled_ref, f32[1024,1024]{1,0:T(8,128)S(1)} %shard_map.76.partial_ref, bf16[64,3072]{1,0:T(8,128)(2,1)S(1)} %collective-permute-done.11.refs_0_, ...), custom_call_target="tpu_custom_call" | custom-call | flops 1610612736 | bytes 4194304 | tf_op jit(solution)/shard_map/pallas_call | solution.py:173
  (8 shorter events, 0.2 us)
Async XLA Ops:
  0.8 5.7 %collective-permute-start = (bf16[4,3072]{1,0:T(4,128)(2,1)S(1)}, bf16[4,3072]{1,0:T(4,128)(2,1)S(1)}, u32[]{:S(2)}, u32[]{:S(2)}) collective-permute-start(bf16[4,3072]{1,0:T(4,128)(2,1)S(1)} %pad_add_fusion), channel_id=1, source_target_pairs={{0,2},{1,3},{2,0},{3,1},{4,6},{5,7},{6,4},{7,5},{8,10},{9,11},{10,... | collective-permute-start | bytes 73736 | tf_op jit(solution)/shard_map/ppermute | solution.py:32
  6.5 8.2 %collective-permute-start.1 = (bf16[8,3072]{1,0:T(8,128)(2,1)S(1)}, bf16[8,3072]{1,0:T(8,128)(2,1)S(1)}, u32[]{:S(2)}, u32[]{:S(2)}) collective-permute-start(bf16[8,3072]{1,0:T(8,128)(2,1)S(1)} %pad_maximum_fusion), channel_id=1, source_target_pairs={{0,8},{1,9},{2,10},{3,11},{4,12},{5,13},{6,14},{7,15},{8,0},{9,1},... | collective-permute-start | bytes 147464 | tf_op jit(solution)/shard_map/ppermute | solution.py:32
  12.6 5.1 %collective-permute-start.2 = (bf16[8,3072]{1,0:T(8,128)(2,1)S(1)}, bf16[8,3072]{1,0:T(8,128)(2,1)S(1)}, u32[]{:S(2)}, u32[]{:S(2)}) collective-permute-start(bf16[8,3072]{1,0:T(8,128)(2,1)S(1)} %pad_maximum_fusion), channel_id=1, source_target_pairs={{0,12},{1,13},{2,14},{3,15},{4,8},{5,9},{6,10},{7,11},{8,4},{9,5},... | collective-permute-start | bytes 147464 | tf_op jit(solution)/shard_map/ppermute | solution.py:32
  12.9 5.1 %collective-permute-start.3 = (bf16[8,3072]{1,0:T(8,128)(2,1)S(1)}, bf16[8,3072]{1,0:T(8,128)(2,1)S(1)}, u32[]{:S(2)}, u32[]{:S(2)}) collective-permute-start(bf16[8,3072]{1,0:T(8,128)(2,1)S(1)} %pad_maximum_fusion), channel_id=1, source_target_pairs={{0,4},{1,5},{2,6},{3,7},{4,0},{5,1},{6,2},{7,3},{8,12},{9,13},{10,... | collective-permute-start | bytes 147464 | tf_op jit(solution)/shard_map/ppermute | solution.py:32
  18.1 6.1 %collective-permute-start.4 = (bf16[32,3072]{1,0:T(8,128)(2,1)S(1)}, bf16[32,3072]{1,0:T(8,128)(2,1)S(1)}, u32[]{:S(2)}, u32[]{:S(2)}) collective-permute-start(bf16[32,3072]{1,0:T(8,128)(2,1)S(1)} %concatenate.11), channel_id=1, source_target_pairs={{0,16},{1,129},{2,18},{3,131},{4,20},{5,133},{6,22},{7,135},{8,24}... | collective-permute-start | bytes 589832 | tf_op jit(solution)/shard_map/ppermute | solution.py:32
  20.7 5.8 %collective-permute-start.5 = (bf16[32,3072]{1,0:T(8,128)(2,1)S(1)}, bf16[32,3072]{1,0:T(8,128)(2,1)S(1)}, u32[]{:S(2)}, u32[]{:S(2)}) collective-permute-start(bf16[32,3072]{1,0:T(8,128)(2,1)S(1)} %concatenate.11), channel_id=1, source_target_pairs={{0,32},{1,65},{2,34},{3,67},{4,36},{5,69},{6,38},{7,71},{8,40},{9,... | collective-permute-start | bytes 589832 | tf_op jit(solution)/shard_map/ppermute | solution.py:32
  21.0 6.0 %collective-permute-start.6 = (bf16[32,3072]{1,0:T(8,128)(2,1)S(1)}, bf16[32,3072]{1,0:T(8,128)(2,1)S(1)}, u32[]{:S(2)}, u32[]{:S(2)}) collective-permute-start(bf16[32,3072]{1,0:T(8,128)(2,1)S(1)} %concatenate.11), channel_id=1, source_target_pairs={{0,48},{1,193},{2,50},{3,195},{4,52},{5,197},{6,54},{7,199},{8,56}... | collective-permute-start | bytes 589832 | tf_op jit(solution)/shard_map/ppermute | solution.py:32
  27.1 6.4 %collective-permute-start.7 = (bf16[128,3072]{1,0:T(8,128)(2,1)S(1)}, bf16[128,3072]{1,0:T(8,128)(2,1)S(1)}, u32[]{:S(2)}, u32[]{:S(2)}) collective-permute-start(bf16[128,3072]{1,0:T(8,128)(2,1)S(1)} %constant_dynamic-update-slice_fusion.refs_0_.refs_3_), channel_id=1, source_target_pairs={{0,1},{1,0},{2,3},{3,2},{4,5},{5,4},{6,7},{7,6},{8,9},{9,8},{10,11... | collective-permute-start | bytes 2359304 | tf_op jit(solution)/shard_map/ppermute | solution.py:32
  31.5 11.1 %collective-permute-start.8 = (bf16[128,3072]{1,0:T(8,128)(2,1)S(1)}, bf16[128,3072]{1,0:T(8,128)(2,1)S(1)}, u32[]{:S(2)}, u32[]{:S(2)}) collective-permute-start(bf16[128,3072]{1,0:T(8,128)(2,1)S(1)} %constant_dynamic-update-slice_fusion.refs_0_.refs_3_), channel_id=1, source_target_pairs={{0,64},{1,33},{2,66},{3,35},{4,68},{5,37},{6,70},{7,39},{8,72},{9,... | collective-permute-start | bytes 2359304 | tf_op jit(solution)/shard_map/ppermute | solution.py:32
  31.5 12.3 %collective-permute-start.9 = (bf16[128,3072]{1,0:T(8,128)(2,1)S(1)}, bf16[128,3072]{1,0:T(8,128)(2,1)S(1)}, u32[]{:S(2)}, u32[]{:S(2)}) collective-permute-start(bf16[128,3072]{1,0:T(8,128)(2,1)S(1)} %constant_dynamic-update-slice_fusion.refs_0_.refs_3_), channel_id=1, source_target_pairs={{0,192},{1,49},{2,194},{3,51},{4,196},{5,53},{6,198},{7,55},{8,200... | collective-permute-start | bytes 2359304 | tf_op jit(solution)/shard_map/ppermute | solution.py:32
  43.9 4.6 %collective-permute-start.13 = (bf16[128,3072]{1,0:T(8,128)(2,1)S(1)}, bf16[128,3072]{1,0:T(8,128)(2,1)S(1)}, u32[]{:S(2)}, u32[]{:S(2)}) collective-permute-start(bf16[128,3072]{1,0:T(8,128)(2,1)S(1)} %collective-permute-done.9.refs_0_.refs_7_), channel_id=1, source_target_pairs={{0,1},{1,0},{2,3},{3,2},{4,5},{5,4},{6,7},{7,6},{8,9},{9,8},{10,11... | collective-permute-start | bytes 2359304 | tf_op jit(solution)/shard_map/ppermute | solution.py:32
  46.3 4.0 %collective-permute-start.12 = (bf16[128,3072]{1,0:T(8,128)(2,1)S(1)}, bf16[128,3072]{1,0:T(8,128)(2,1)S(1)}, u32[]{:S(2)}, u32[]{:S(2)}) collective-permute-start(bf16[128,3072]{1,0:T(8,128)(2,1)S(1)} %collective-permute-done.8.refs_0_.refs_5_), channel_id=1, source_target_pairs={{0,1},{1,0},{2,3},{3,2},{4,5},{5,4},{6,7},{7,6},{8,9},{9,8},{10,11... | collective-permute-start | bytes 2359304 | tf_op jit(solution)/shard_map/ppermute | solution.py:32
  46.4 7.6 %collective-permute-start.11 = (bf16[64,3072]{1,0:T(8,128)(2,1)S(1)}, bf16[64,3072]{1,0:T(8,128)(2,1)S(1)}, u32[]{:S(2)}, u32[]{:S(2)}) collective-permute-start(bf16[64,3072]{1,0:T(8,128)(2,1)S(1)} %slice.7), channel_id=1, source_target_pairs={{0,64},{1,33},{2,66},{3,35},{4,68},{5,37},{6,70},{7,39},{8,72},{9,... | collective-permute-start | bytes 1179656 | tf_op jit(solution)/shard_map/ppermute | solution.py:32
  46.5 8.4 %collective-permute-start.10 = (bf16[64,3072]{1,0:T(8,128)(2,1)S(1)}, bf16[64,3072]{1,0:T(8,128)(2,1)S(1)}, u32[]{:S(2)}, u32[]{:S(2)}) collective-permute-start(bf16[64,3072]{1,0:T(8,128)(2,1)S(1)} %slice.6), channel_id=1, source_target_pairs={{0,192},{1,49},{2,194},{3,51},{4,196},{5,53},{6,198},{7,55},{8,200... | collective-permute-start | bytes 1179656 | tf_op jit(solution)/shard_map/ppermute | solution.py:32
  54.9 2.7 %collective-permute-start.15 = (bf16[64,3072]{1,0:T(8,128)(2,1)S(1)}, bf16[64,3072]{1,0:T(8,128)(2,1)S(1)}, u32[]{:S(2)}, u32[]{:S(2)}) collective-permute-start(bf16[64,3072]{1,0:T(8,128)(2,1)S(1)} %collective-permute-done.10.refs_1_), channel_id=1, source_target_pairs={{0,1},{1,0},{2,3},{3,2},{4,5},{5,4},{6,7},{7,6},{8,9},{9,8},{10,11... | collective-permute-start | bytes 1179656 | tf_op jit(solution)/shard_map/ppermute | solution.py:32
  56.3 1.9 %collective-permute-start.14 = (bf16[64,3072]{1,0:T(8,128)(2,1)S(1)}, bf16[64,3072]{1,0:T(8,128)(2,1)S(1)}, u32[]{:S(2)}, u32[]{:S(2)}) collective-permute-start(bf16[64,3072]{1,0:T(8,128)(2,1)S(1)} %collective-permute-done.11.refs_0_), channel_id=1, source_target_pairs={{0,1},{1,0},{2,3},{3,2},{4,5},{5,4},{6,7},{7,6},{8,9},{9,8},{10,11... | collective-permute-start | bytes 1179656 | tf_op jit(solution)/shard_map/ppermute | solution.py:32

commit v7 on v6

--- a/solution.py
+++ b/solution.py
@@ -188,7 +188,7 @@
 
 def shards(orbitals, panel_orbitals, band_gap, tau_points, quad_weight, frequencies, coulomb):
     held = jnp.pad(panel_orbitals, ((0, 0), (0, PANEL))) + jnp.pad(coulomb, ((0, 0), (BANDS, 0)))
-    for group in ((1,), (4, 6, 2)):
+    for group in ((1,), (6, 4, 2)):
         held = jnp.concatenate([held] + [moved(held, z_flip(bits)) for bits in group], axis=0)
     rows = orbitals.shape[0] // lax.axis_size(TM)
     own = lax.dynamic_slice_in_dim(orbitals, lax.axis_index(TM) * rows, rows)

time: 62.7 us -> 64.1 us (1.022)
  waiting for transfers between devices: 20 us -> 20.8 us
  starting transfers between devices: 25.3 us -> 26 us
    ppermute x16, waiting for transfers between devices: 20 us -> 20.8 us  [moved(): return lax.ppermute(value, TM + PTS, pairs)]
  transfers between devices with their start and end apart: 16 -> 16, of which waited for: 11 -> 10; matrix products, arithmetic and copies ran while one was open for 7% -> 6% of each run, Pallas kernels for 12% -> 12%
where the time goes in v7:
time: 64.1 us; the launch traced here: 63.8 us
  starting transfers between devices  26 us (41%)
  waiting for transfers between devices  20.8 us (32%)
  Pallas kernels  11.7 us (18%)
  other arithmetic  3.65 us (6%)
  local copies, waits for them, and re-layouts  1.39 us (2%)
    ppermute x16, starting transfers between devices, moved(): return lax.ppermute(value, TM + PTS, pairs)  26 us
    ppermute x16, waiting for transfers between devices, moved(): return lax.ppermute(value, TM + PTS, pairs)  20.8 us
    pallas_call x1, Pallas kernels, screen_last(): pl.pallas_call(last_kernel, out_shape=jax.ShapeDtypeStruct((rows, PANEL),...  4 us
    pallas_call x2, Pallas kernels, transform(): pl.pallas_call(transform_kernel, out_shape=jax.ShapeDtypeStruct((rows, wi...  3.69 us
    pallas_call x1, Pallas kernels, transform_first(): pl.pallas_call(first_kernel, out_shape=[jax.ShapeDtypeStruct((rows, width...  2.18 us
    pallas_call x1, Pallas kernels, screen(): pl.pallas_call(screen_kernel, out_shape=jax.ShapeDtypeStruct((rows, PANEL...  1.81 us
  transfers between devices with their start and end apart: 16, of which 10 were waited for; matrix products, arithmetic and copies ran while one was open for 6% of the time, Pallas kernels for 12%

profile of v7, /device:TPU:1, one launch (start us, length us, event | category | flops | bytes accessed | tf_op | source)
XLA Modules:
  0.0 63.8 jit_solution(14937520977710380102)
XLA Ops:
  0.0 0.7 %pad_add_fusion = bf16[4,3072]{1,0:T(4,128)(2,1)S(1)} fusion(bf16[4,1024]{1,0:T(4,128)(2,1)} %param.13, bf16[4,2048]{1,0:T(4,128)(2,1)} %param.8), kind=kLoop, calls=%fused_computation.2 | loop fusion | flops 49152 | bytes 49152 | tf_op jit(solution)/shard_map/add | solution.py:190
  0.8 2.6 %collective-permute-start = (bf16[4,3072]{1,0:T(4,128)(2,1)S(1)}, bf16[4,3072]{1,0:T(4,128)(2,1)S(1)}, u32[]{:S(2)}, u32[]{:S(2)}) collective-permute-start(bf16[4,3072]{1,0:T(4,128)(2,1)S(1)} %pad_add_fusion), channel_id=1, source_target_pairs={{0,2},{1,3},{2,0},{3,1},{4,6},{5,7},{6,4},{7,5},{8,10},{9,11},{10,... | collective-permute-start | bytes 73736 | tf_op jit(solution)/shard_map/ppermute | solution.py:32
  3.3 0.7 %neg.9 = f32[2048]{0:T(1024)S(1)} negate(f32[2048]{0:T(1024)} %param.9) | non-fusion elementwise | flops 2048 | bytes 16384 | tf_op jit(solution)/shard_map/neg | solution.py:195
  4.0 0.7 %multiply_exponential_fusion.decay_ref = f32[8,2048]{1,0:T(8,128)S(1)} fusion(f32[8]{0:T(128)} %param.10, f32[2048]{0:T(1024)S(1)} %neg.9), kind=kLoop, calls=%fused_computation | loop fusion | flops 16384 | bytes 73760 | tf_op jit(solution)/shard_map/exp | solution.py:195
  4.7 1.1 %constant_dynamic-slice_fusion.rows_ref = bf16[128,2048]{1,0:T(8,128)(2,1)S(1)} fusion(bf16[1024,2048]{1,0:T(8,128)(2,1)} %param.7, s32[]{:T(128)S(6)} %select_n.3), kind=kLoop, calls=%fused_computation.8 | loop fusion | bytes 1048580 | tf_op jit(solution)/shard_map/dynamic_slice | solution.py:194
  5.8 0.7 %neg.8 = f32[8]{0:T(128)S(1)} negate(f32[8]{0:T(128)} %param.11) | non-fusion elementwise | flops 8 | bytes 64 | tf_op jit(solution)/shard_map/neg | solution.py:196
  6.5 0.0 collective-permute-done
  6.5 5.2 %collective-permute-start.1 = (bf16[8,3072]{1,0:T(8,128)(2,1)S(1)}, bf16[8,3072]{1,0:T(8,128)(2,1)S(1)}, u32[]{:S(2)}, u32[]{:S(2)}) collective-permute-start(bf16[8,3072]{1,0:T(8,128)(2,1)S(1)} %pad_maximum_fusion), channel_id=1, source_target_pairs={{0,12},{1,13},{2,14},{3,15},{4,8},{5,9},{6,10},{7,11},{8,4},{9,5},... | collective-permute-start | bytes 147464 | tf_op jit(solution)/shard_map/ppermute | solution.py:32
  11.7 1.2 %collective-permute-start.2 = (bf16[8,3072]{1,0:T(8,128)(2,1)S(1)}, bf16[8,3072]{1,0:T(8,128)(2,1)S(1)}, u32[]{:S(2)}, u32[]{:S(2)}) collective-permute-start(bf16[8,3072]{1,0:T(8,128)(2,1)S(1)} %pad_maximum_fusion), channel_id=1, source_target_pairs={{0,8},{1,9},{2,10},{3,11},{4,12},{5,13},{6,14},{7,15},{8,0},{9,1},... | collective-permute-start | bytes 147464 | tf_op jit(solution)/shard_map/ppermute | solution.py:32
  12.9 1.0 %collective-permute-start.3 = (bf16[8,3072]{1,0:T(8,128)(2,1)S(1)}, bf16[8,3072]{1,0:T(8,128)(2,1)S(1)}, u32[]{:S(2)}, u32[]{:S(2)}) collective-permute-start(bf16[8,3072]{1,0:T(8,128)(2,1)S(1)} %pad_maximum_fusion), channel_id=1, source_target_pairs={{0,4},{1,5},{2,6},{3,7},{4,0},{5,1},{6,2},{7,3},{8,12},{9,13},{10,... | collective-permute-start | bytes 147464 | tf_op jit(solution)/shard_map/ppermute | solution.py:32
  13.9 0.8 %cosine_multiply_fusion = f32[8,8]{1,0:T(8,128)S(1)} fusion(f32[8]{0:T(128)} %param.10, f32[8]{0:T(128)} %param.12, f32[8]{0:T(128)S(1)} %neg.8), kind=kLoop, calls=%fused_computation.7 | loop fusion | flops 128 | bytes 352 | tf_op jit(solution)/shard_map/mul | solution.py:196
  14.7 0.1 mul.57
  14.8 0.0 collective-permute-done.1
  14.8 4.2 %collective-permute-done.2 = bf16[8,3072]{1,0:T(8,128)(2,1)S(1)} collective-permute-done((bf16[8,3072]{1,0:T(8,128)(2,1)S(1)}, bf16[8,3072]{1,0:T(8,128)(2,1)S(1)}, u32[]{:S(2)}, u32[]{:S(2)}) %collective-permute-start.2) | collective-permute-done | bytes 49184 | tf_op jit(solution)/shard_map/ppermute | solution.py:32
  18.9 0.0 collective-permute-done.3
  19.0 0.1 broadcast_in_dim.2.weights_ref
  19.1 2.8 %collective-permute-start.4 = (bf16[32,3072]{1,0:T(8,128)(2,1)S(1)}, bf16[32,3072]{1,0:T(8,128)(2,1)S(1)}, u32[]{:S(2)}, u32[]{:S(2)}) collective-permute-start(bf16[32,3072]{1,0:T(8,128)(2,1)S(1)} %concatenate.11), channel_id=1, source_target_pairs={{0,16},{1,129},{2,18},{3,131},{4,20},{5,133},{6,22},{7,135},{8,24}... | collective-permute-start | bytes 589832 | tf_op jit(solution)/shard_map/ppermute | solution.py:32
  21.9 0.3 collective-permute-start.5
  22.2 0.6 collective-permute-start.6
  22.7 2.4 %collective-permute-done.4 = bf16[32,3072]{1,0:T(8,128)(2,1)S(1)} collective-permute-done((bf16[32,3072]{1,0:T(8,128)(2,1)S(1)}, bf16[32,3072]{1,0:T(8,128)(2,1)S(1)}, u32[]{:S(2)}, u32[]{:S(2)}) %collective-permute-start.4) | collective-permute-done | bytes 196640 | tf_op jit(solution)/shard_map/ppermute | solution.py:32
  25.2 2.5 %collective-permute-done.5 = bf16[32,3072]{1,0:T(8,128)(2,1)S(1)} collective-permute-done((bf16[32,3072]{1,0:T(8,128)(2,1)S(1)}, bf16[32,3072]{1,0:T(8,128)(2,1)S(1)}, u32[]{:S(2)}, u32[]{:S(2)}) %collective-permute-start.5) | collective-permute-done | bytes 196640 | tf_op jit(solution)/shard_map/ppermute | solution.py:32
  27.6 0.6 collective-permute-done.6
  28.2 4.8 %collective-permute-start.7 = (bf16[128,3072]{1,0:T(8,128)(2,1)S(1)}, bf16[128,3072]{1,0:T(8,128)(2,1)S(1)}, u32[]{:S(2)}, u32[]{:S(2)}) collective-permute-start(bf16[128,3072]{1,0:T(8,128)(2,1)S(1)} %constant_dynamic-update-slice_fusion.refs_0_.refs_3_), channel_id=1, source_target_pairs={{0,1},{1,0},{2,3},{3,2},{4,5},{5,4},{6,7},{7,6},{8,9},{9,8},{10,11... | collective-permute-start | bytes 2359304 | tf_op jit(solution)/shard_map/ppermute | solution.py:32
  33.0 0.0 collective-permute-start.8
  33.0 1.7 %collective-permute-start.9 = (bf16[128,3072]{1,0:T(8,128)(2,1)S(1)}, bf16[128,3072]{1,0:T(8,128)(2,1)S(1)}, u32[]{:S(2)}, u32[]{:S(2)}) collective-permute-start(bf16[128,3072]{1,0:T(8,128)(2,1)S(1)} %constant_dynamic-update-slice_fusion.refs_0_.refs_3_), channel_id=1, source_target_pairs={{0,192},{1,49},{2,194},{3,51},{4,196},{5,53},{6,198},{7,55},{8,200... | collective-permute-start | bytes 2359304 | tf_op jit(solution)/shard_map/ppermute | solution.py:32
  34.7 0.2 collective-permute-done.7.refs_1_.refs_4_
  34.9 2.2 %shard_map.73 = (bf16[1024,256]{1,0:T(8,128)(2,1)S(1)}, bf16[1024,2048]{1,0:T(8,128)(2,1)S(1)}) custom-call(f32[64,256]{1,0:T(8,128)S(1)} %broadcast_in_dim.2.weights_ref, f32[8,2048]{1,0:T(8,128)S(1)} %multiply_exponential_fusion.decay_ref, bf16[128,2048]{1,0:T(8,128)(2,1)S(1)} %constant_dynamic-slice_fusion.rows_ref, ...), custom_call_target="tpu_custom_call" | custom-call | flops 1073741824 | bytes 1048576 | tf_op jit(solution)/shard_map/pallas_call | solution.py:142
  37.1 7.0 %collective-permute-done.8.refs_0_.refs_5_ = bf16[128,3072]{1,0:T(8,128)(2,1)S(1)} collective-permute-done((bf16[128,3072]{1,0:T(8,128)(2,1)S(1)}, bf16[128,3072]{1,0:T(8,128)(2,1)S(1)}, u32[]{:S(2)}, u32[]{:S(2)}) %collective-permute-start.8) | collective-permute-done | bytes 786464 | tf_op jit(solution)/shard_map/ppermute | solution.py:32
  44.1 1.2 %collective-permute-done.9.refs_0_.refs_7_ = bf16[128,3072]{1,0:T(8,128)(2,1)S(1)} collective-permute-done((bf16[128,3072]{1,0:T(8,128)(2,1)S(1)}, bf16[128,3072]{1,0:T(8,128)(2,1)S(1)}, u32[]{:S(2)}, u32[]{:S(2)}) %collective-permute-start.9) | collective-permute-done | bytes 786464 | tf_op jit(solution)/shard_map/ppermute | solution.py:32
  45.3 2.4 %collective-permute-start.13 = (bf16[128,3072]{1,0:T(8,128)(2,1)S(1)}, bf16[128,3072]{1,0:T(8,128)(2,1)S(1)}, u32[]{:S(2)}, u32[]{:S(2)}) collective-permute-start(bf16[128,3072]{1,0:T(8,128)(2,1)S(1)} %collective-permute-done.9.refs_0_.refs_7_), channel_id=1, source_target_pairs={{0,1},{1,0},{2,3},{3,2},{4,5},{5,4},{6,7},{7,6},{8,9},{9,8},{10,11... | collective-permute-start | bytes 2359304 | tf_op jit(solution)/shard_map/ppermute | solution.py:32
  47.8 0.0 collective-permute-start.12
  47.8 0.1 collective-permute-start.11
  47.9 2.0 %collective-permute-start.10 = (bf16[64,3072]{1,0:T(8,128)(2,1)S(1)}, bf16[64,3072]{1,0:T(8,128)(2,1)S(1)}, u32[]{:S(2)}, u32[]{:S(2)}) collective-permute-start(bf16[64,3072]{1,0:T(8,128)(2,1)S(1)} %slice.6), channel_id=1, source_target_pairs={{0,192},{1,49},{2,194},{3,51},{4,196},{5,53},{6,198},{7,55},{8,200... | collective-permute-start | bytes 1179656 | tf_op jit(solution)/shard_map/ppermute | solution.py:32
  49.9 0.0 collective-permute-done.13.refs_1_.refs_8_
  49.9 1.8 %shard_map.75.refs_2_ = bf16[1024,256]{1,0:T(8,128)(2,1)S(1)} custom-call(f32[64,256]{1,0:T(8,128)S(1)} %broadcast_in_dim.2.weights_ref, bf16[1024,2048]{1,0:T(8,128)(2,1)S(1)} %get-tuple-element.22.scaled_ref, bf16[128,3072]{1,0:T(8,128)(2,1)S(1)} %collective-permute-done.9.refs_0_.refs_7_, bf16[128,3072]{1,0:T(8,128)(2,1)S(1)} %collective-permute-done.13.refs_1_.refs_8_), custom_call_target="tpu_custom_call" | custom-call | flops 1073741824 | bytes 1048576 | tf_op jit(solution)/shard_map/pallas_call | solution.py:128
  51.8 0.0 collective-permute-done.12.refs_1_.refs_6_
  51.8 1.8 %shard_map.74.refs_1_ = bf16[1024,256]{1,0:T(8,128)(2,1)S(1)} custom-call(f32[64,256]{1,0:T(8,128)S(1)} %broadcast_in_dim.2.weights_ref, bf16[1024,2048]{1,0:T(8,128)(2,1)S(1)} %get-tuple-element.22.scaled_ref, bf16[128,3072]{1,0:T(8,128)(2,1)S(1)} %collective-permute-done.8.refs_0_.refs_5_, bf16[128,3072]{1,0:T(8,128)(2,1)S(1)} %collective-permute-done.12.refs_1_.refs_6_), custom_call_target="tpu_custom_call" | custom-call | flops 1073741824 | bytes 1048576 | tf_op jit(solution)/shard_map/pallas_call | solution.py:128
  53.6 1.8 %shard_map.76.partial_ref = f32[1024,1024]{1,0:T(8,128)S(1)} custom-call(bf16[1024,256]{1,0:T(8,128)(2,1)S(1)} %get-tuple-element.26.refs_0_, bf16[1024,256]{1,0:T(8,128)(2,1)S(1)} %shard_map.74.refs_1_, bf16[1024,256]{1,0:T(8,128)(2,1)S(1)} %shard_map.75.refs_2_, bf16[128,3072]{1,0:T(8,128)(2,1)S(1)} %constant_dynamic-update-slice_fusion.refs_0_.refs_3_, ...), custom_call_target="tpu_custom_call" | custom-call | flops 1610612736 | bytes 1048576 | tf_op jit(solution)/shard_map/pallas_call | solution.py:159
  55.4 0.0 collective-permute-done.11.refs_0_
  55.5 0.9 %collective-permute-done.10.refs_1_ = bf16[64,3072]{1,0:T(8,128)(2,1)S(1)} collective-permute-done((bf16[64,3072]{1,0:T(8,128)(2,1)S(1)}, bf16[64,3072]{1,0:T(8,128)(2,1)S(1)}, u32[]{:S(2)}, u32[]{:S(2)}) %collective-permute-start.10) | collective-permute-done | bytes 393248 | tf_op jit(solution)/shard_map/ppermute | solution.py:32
  56.3 1.4 %collective-permute-start.15 = (bf16[64,3072]{1,0:T(8,128)(2,1)S(1)}, bf16[64,3072]{1,0:T(8,128)(2,1)S(1)}, u32[]{:S(2)}, u32[]{:S(2)}) collective-permute-start(bf16[64,3072]{1,0:T(8,128)(2,1)S(1)} %collective-permute-done.10.refs_1_), channel_id=1, source_target_pairs={{0,1},{1,0},{2,3},{3,2},{4,5},{5,4},{6,7},{7,6},{8,9},{9,8},{10,11... | collective-permute-start | bytes 1179656 | tf_op jit(solution)/shard_map/ppermute | solution.py:32
  57.7 0.0 collective-permute-start.14
  57.7 1.3 %collective-permute-done.15.refs_3_ = bf16[64,3072]{1,0:T(8,128)(2,1)S(1)} collective-permute-done((bf16[64,3072]{1,0:T(8,128)(2,1)S(1)}, bf16[64,3072]{1,0:T(8,128)(2,1)S(1)}, u32[]{:S(2)}, u32[]{:S(2)}) %collective-permute-start.15) | collective-permute-done | bytes 393248 | tf_op jit(solution)/shard_map/ppermute | solution.py:32
  59.1 0.6 collective-permute-done.14.refs_2_
  59.6 4.0 %shard_map.77 = bf16[1024,1024]{1,0:T(8,128)(2,1)} custom-call(f32[64,256]{1,0:T(8,128)S(1)} %broadcast_in_dim.2.weights_ref, bf16[1024,2048]{1,0:T(8,128)(2,1)S(1)} %get-tuple-element.22.scaled_ref, f32[1024,1024]{1,0:T(8,128)S(1)} %shard_map.76.partial_ref, bf16[64,3072]{1,0:T(8,128)(2,1)S(1)} %collective-permute-done.11.refs_0_, ...), custom_call_target="tpu_custom_call" | custom-call | flops 1610612736 | bytes 4194304 | tf_op jit(solution)/shard_map/pallas_call | solution.py:173
  (8 shorter events, 0.2 us)
Async XLA Ops:
  0.8 5.7 %collective-permute-start = (bf16[4,3072]{1,0:T(4,128)(2,1)S(1)}, bf16[4,3072]{1,0:T(4,128)(2,1)S(1)}, u32[]{:S(2)}, u32[]{:S(2)}) collective-permute-start(bf16[4,3072]{1,0:T(4,128)(2,1)S(1)} %pad_add_fusion), channel_id=1, source_target_pairs={{0,2},{1,3},{2,0},{3,1},{4,6},{5,7},{6,4},{7,5},{8,10},{9,11},{10,... | collective-permute-start | bytes 73736 | tf_op jit(solution)/shard_map/ppermute | solution.py:32
  6.5 8.3 %collective-permute-start.1 = (bf16[8,3072]{1,0:T(8,128)(2,1)S(1)}, bf16[8,3072]{1,0:T(8,128)(2,1)S(1)}, u32[]{:S(2)}, u32[]{:S(2)}) collective-permute-start(bf16[8,3072]{1,0:T(8,128)(2,1)S(1)} %pad_maximum_fusion), channel_id=1, source_target_pairs={{0,12},{1,13},{2,14},{3,15},{4,8},{5,9},{6,10},{7,11},{8,4},{9,5},... | collective-permute-start | bytes 147464 | tf_op jit(solution)/shard_map/ppermute | solution.py:32
  11.7 7.2 %collective-permute-start.2 = (bf16[8,3072]{1,0:T(8,128)(2,1)S(1)}, bf16[8,3072]{1,0:T(8,128)(2,1)S(1)}, u32[]{:S(2)}, u32[]{:S(2)}) collective-permute-start(bf16[8,3072]{1,0:T(8,128)(2,1)S(1)} %pad_maximum_fusion), channel_id=1, source_target_pairs={{0,8},{1,9},{2,10},{3,11},{4,12},{5,13},{6,14},{7,15},{8,0},{9,1},... | collective-permute-start | bytes 147464 | tf_op jit(solution)/shard_map/ppermute | solution.py:32
  12.9 6.0 %collective-permute-start.3 = (bf16[8,3072]{1,0:T(8,128)(2,1)S(1)}, bf16[8,3072]{1,0:T(8,128)(2,1)S(1)}, u32[]{:S(2)}, u32[]{:S(2)}) collective-permute-start(bf16[8,3072]{1,0:T(8,128)(2,1)S(1)} %pad_maximum_fusion), channel_id=1, source_target_pairs={{0,4},{1,5},{2,6},{3,7},{4,0},{5,1},{6,2},{7,3},{8,12},{9,13},{10,... | collective-permute-start | bytes 147464 | tf_op jit(solution)/shard_map/ppermute | solution.py:32
  19.1 6.1 %collective-permute-start.4 = (bf16[32,3072]{1,0:T(8,128)(2,1)S(1)}, bf16[32,3072]{1,0:T(8,128)(2,1)S(1)}, u32[]{:S(2)}, u32[]{:S(2)}) collective-permute-start(bf16[32,3072]{1,0:T(8,128)(2,1)S(1)} %concatenate.11), channel_id=1, source_target_pairs={{0,16},{1,129},{2,18},{3,131},{4,20},{5,133},{6,22},{7,135},{8,24}... | collective-permute-start | bytes 589832 | tf_op jit(solution)/shard_map/ppermute | solution.py:32
  21.9 5.8 %collective-permute-start.5 = (bf16[32,3072]{1,0:T(8,128)(2,1)S(1)}, bf16[32,3072]{1,0:T(8,128)(2,1)S(1)}, u32[]{:S(2)}, u32[]{:S(2)}) collective-permute-start(bf16[32,3072]{1,0:T(8,128)(2,1)S(1)} %concatenate.11), channel_id=1, source_target_pairs={{0,32},{1,65},{2,34},{3,67},{4,36},{5,69},{6,38},{7,71},{8,40},{9,... | collective-permute-start | bytes 589832 | tf_op jit(solution)/shard_map/ppermute | solution.py:32
  22.2 6.0 %collective-permute-start.6 = (bf16[32,3072]{1,0:T(8,128)(2,1)S(1)}, bf16[32,3072]{1,0:T(8,128)(2,1)S(1)}, u32[]{:S(2)}, u32[]{:S(2)}) collective-permute-start(bf16[32,3072]{1,0:T(8,128)(2,1)S(1)} %concatenate.11), channel_id=1, source_target_pairs={{0,48},{1,193},{2,50},{3,195},{4,52},{5,197},{6,54},{7,199},{8,56}... | collective-permute-start | bytes 589832 | tf_op jit(solution)/shard_map/ppermute | solution.py:32
  28.2 6.7 %collective-permute-start.7 = (bf16[128,3072]{1,0:T(8,128)(2,1)S(1)}, bf16[128,3072]{1,0:T(8,128)(2,1)S(1)}, u32[]{:S(2)}, u32[]{:S(2)}) collective-permute-start(bf16[128,3072]{1,0:T(8,128)(2,1)S(1)} %constant_dynamic-update-slice_fusion.refs_0_.refs_3_), channel_id=1, source_target_pairs={{0,1},{1,0},{2,3},{3,2},{4,5},{5,4},{6,7},{7,6},{8,9},{9,8},{10,11... | collective-permute-start | bytes 2359304 | tf_op jit(solution)/shard_map/ppermute | solution.py:32
  33.0 11.1 %collective-permute-start.8 = (bf16[128,3072]{1,0:T(8,128)(2,1)S(1)}, bf16[128,3072]{1,0:T(8,128)(2,1)S(1)}, u32[]{:S(2)}, u32[]{:S(2)}) collective-permute-start(bf16[128,3072]{1,0:T(8,128)(2,1)S(1)} %constant_dynamic-update-slice_fusion.refs_0_.refs_3_), channel_id=1, source_target_pairs={{0,64},{1,33},{2,66},{3,35},{4,68},{5,37},{6,70},{7,39},{8,72},{9,... | collective-permute-start | bytes 2359304 | tf_op jit(solution)/shard_map/ppermute | solution.py:32
  33.0 12.3 %collective-permute-start.9 = (bf16[128,3072]{1,0:T(8,128)(2,1)S(1)}, bf16[128,3072]{1,0:T(8,128)(2,1)S(1)}, u32[]{:S(2)}, u32[]{:S(2)}) collective-permute-start(bf16[128,3072]{1,0:T(8,128)(2,1)S(1)} %constant_dynamic-update-slice_fusion.refs_0_.refs_3_), channel_id=1, source_target_pairs={{0,192},{1,49},{2,194},{3,51},{4,196},{5,53},{6,198},{7,55},{8,200... | collective-permute-start | bytes 2359304 | tf_op jit(solution)/shard_map/ppermute | solution.py:32
  45.3 4.6 %collective-permute-start.13 = (bf16[128,3072]{1,0:T(8,128)(2,1)S(1)}, bf16[128,3072]{1,0:T(8,128)(2,1)S(1)}, u32[]{:S(2)}, u32[]{:S(2)}) collective-permute-start(bf16[128,3072]{1,0:T(8,128)(2,1)S(1)} %collective-permute-done.9.refs_0_.refs_7_), channel_id=1, source_target_pairs={{0,1},{1,0},{2,3},{3,2},{4,5},{5,4},{6,7},{7,6},{8,9},{9,8},{10,11... | collective-permute-start | bytes 2359304 | tf_op jit(solution)/shard_map/ppermute | solution.py:32
  47.8 4.0 %collective-permute-start.12 = (bf16[128,3072]{1,0:T(8,128)(2,1)S(1)}, bf16[128,3072]{1,0:T(8,128)(2,1)S(1)}, u32[]{:S(2)}, u32[]{:S(2)}) collective-permute-start(bf16[128,3072]{1,0:T(8,128)(2,1)S(1)} %collective-permute-done.8.refs_0_.refs_5_), channel_id=1, source_target_pairs={{0,1},{1,0},{2,3},{3,2},{4,5},{5,4},{6,7},{7,6},{8,9},{9,8},{10,11... | collective-permute-start | bytes 2359304 | tf_op jit(solution)/shard_map/ppermute | solution.py:32
  47.8 7.6 %collective-permute-start.11 = (bf16[64,3072]{1,0:T(8,128)(2,1)S(1)}, bf16[64,3072]{1,0:T(8,128)(2,1)S(1)}, u32[]{:S(2)}, u32[]{:S(2)}) collective-permute-start(bf16[64,3072]{1,0:T(8,128)(2,1)S(1)} %slice.7), channel_id=1, source_target_pairs={{0,64},{1,33},{2,66},{3,35},{4,68},{5,37},{6,70},{7,39},{8,72},{9,... | collective-permute-start | bytes 1179656 | tf_op jit(solution)/shard_map/ppermute | solution.py:32
  47.9 8.4 %collective-permute-start.10 = (bf16[64,3072]{1,0:T(8,128)(2,1)S(1)}, bf16[64,3072]{1,0:T(8,128)(2,1)S(1)}, u32[]{:S(2)}, u32[]{:S(2)}) collective-permute-start(bf16[64,3072]{1,0:T(8,128)(2,1)S(1)} %slice.6), channel_id=1, source_target_pairs={{0,192},{1,49},{2,194},{3,51},{4,196},{5,53},{6,198},{7,55},{8,200... | collective-permute-start | bytes 1179656 | tf_op jit(solution)/shard_map/ppermute | solution.py:32
  56.3 2.7 %collective-permute-start.15 = (bf16[64,3072]{1,0:T(8,128)(2,1)S(1)}, bf16[64,3072]{1,0:T(8,128)(2,1)S(1)}, u32[]{:S(2)}, u32[]{:S(2)}) collective-permute-start(bf16[64,3072]{1,0:T(8,128)(2,1)S(1)} %collective-permute-done.10.refs_1_), channel_id=1, source_target_pairs={{0,1},{1,0},{2,3},{3,2},{4,5},{5,4},{6,7},{7,6},{8,9},{9,8},{10,11... | collective-permute-start | bytes 1179656 | tf_op jit(solution)/shard_map/ppermute | solution.py:32
  57.7 1.9 %collective-permute-start.14 = (bf16[64,3072]{1,0:T(8,128)(2,1)S(1)}, bf16[64,3072]{1,0:T(8,128)(2,1)S(1)}, u32[]{:S(2)}, u32[]{:S(2)}) collective-permute-start(bf16[64,3072]{1,0:T(8,128)(2,1)S(1)} %collective-permute-done.11.refs_0_), channel_id=1, source_target_pairs={{0,1},{1,0},{2,3},{3,2},{4,5},{5,4},{6,7},{7,6},{8,9},{9,8},{10,11... | collective-permute-start | bytes 1179656 | tf_op jit(solution)/shard_map/ppermute | solution.py:32
